TPU v7x, 256 devices: a whole 4x4x8 slice. The times are simulated.
256 devices in a mesh: arc: 8 (over z), tile: 32 (over x, y, core).
Axes of the slice: x: 4, y: 4, z: 8, core: 2. Of those that a mesh axis runs over, the one named last changes fastest.
Arguments:
- design: bfloat16 [2048, 128, 512], P(('arc', 'tile')), may hold values from -0.059814453 to 0.059814453
- observed: float32 [2048, 128], P(('arc', 'tile')), may hold values from -6 to 6
- obs_type: int32 [2048, 128], P(('arc', 'tile')), may hold values from 0 to 7
- owner_of: int32 [2048, 4], P(('arc', 'tile')), may hold values from 0 to 31, all different within a row; in each aligned block of 8 rows (0 to 7, 8 to 15, ...) at most 2 rows name the same one
- sub_of: int32 [2048, 4], P(('arc', 'tile')), may hold values from 0 to 2
- sigma_table: float32 [8], replicated, may hold values from 0.3 to 3
- solution: float32 [12288], P('tile'), may hold values from -6 to 6
- prior: float32 [12288, 12288], P('arc', 'tile'), may hold values from -0.6 to 0.6
Outputs:
- normal_matrix: float32 [12288, 12288], P('arc', 'tile')
- gradient: float32 [12288], P('tile')
Inputs may be any that keep to these rules, and one draw needn't show every extreme that they name: `owner_of`: each block names 4 different owners. Among the 8 blocks of one device no owner is named more than 2 times, a bound that some block reaches in every draw.
All inputs are finite; a program needn't handle non-finite values.
Results may differ from a plain program's by a relative error of at most 0.006.
Values may be sent and summed in bfloat16 or wider, within the bound.
No kernel may reach another device: no remote copies, remote signals or barrier semaphores. Data moves between devices by JAX's collectives and lax.ppermute only.
A program may use at most 128 MiB of HBM per device.

v0:
```python
import jax
import jax.numpy as jnp
from jax import lax
from jax.sharding import PartitionSpec as P

huber_limit = 1.345


def route_table(owner_ids, target_ids, capacity):
    matched = (owner_ids == target_ids[:, None, None]).astype(jnp.int32)
    hit_count = jnp.sum(matched, axis=2)
    slot_pos = jnp.sum(matched * jnp.arange(owner_ids.shape[2], dtype=jnp.int32), axis=2)
    slot_rank = jnp.cumsum(hit_count, axis=1) - 1
    slot_ids = jnp.arange(capacity, dtype=jnp.int32)
    chosen = hit_count[:, None, :] * (slot_rank[:, None, :] == slot_ids[None, :, None]).astype(
        jnp.int32
    )
    live_slot = jnp.sum(chosen, axis=2)
    block_of = jnp.sum(chosen * jnp.arange(owner_ids.shape[1], dtype=jnp.int32), axis=2)
    slot_k = jnp.take_along_axis(slot_pos, block_of, axis=1)
    return (live_slot, block_of, slot_k)


def on_device(design, observed, obs_type, owner_of, sub_of, sigma_table, solution, prior):
    n_owner = lax.axis_size("tile")
    blocks, block_rows, row_width = design.shape
    tile_width = row_width // 4
    params = solution.shape[0] * n_owner
    tile_count = params // tile_width
    per_owner = tile_count // n_owner
    capacity = 2 * ((4 * blocks + n_owner - 1) // n_owner)
    item_count = n_owner * capacity
    own_index = lax.axis_index("tile")
    whole_solution = lax.all_gather(solution, "tile", axis=0, tiled=True)
    tile_ids = owner_of * per_owner + sub_of
    touched = whole_solution.reshape(tile_count, tile_width)[tile_ids]
    design_tiles = design.reshape(blocks, block_rows, 4, tile_width)
    predicted = jnp.einsum(
        "bqlc,blc->bq", design_tiles.astype(jnp.float32), touched, precision=lax.Precision.HIGHEST
    )
    residual = observed - predicted
    type_ids = jnp.arange(sigma_table.shape[0], dtype=jnp.int32)
    spread = jnp.sum(jnp.where(obs_type[:, :, None] == type_ids, sigma_table, 0.0), axis=2)
    scaled = jnp.abs(residual) / spread
    root_weight = jnp.sqrt(huber_limit / jnp.maximum(scaled, huber_limit)) / spread
    weighted = (root_weight[:, :, None, None] * design_tiles).astype(jnp.bfloat16)
    target = (root_weight * residual).astype(jnp.bfloat16)
    owner_copies = jnp.broadcast_to(owner_of[None], (n_owner, blocks, 4))
    send_live, send_block, send_k = route_table(
        owner_copies, jnp.arange(n_owner, dtype=jnp.int32), capacity
    )
    all_owner, all_sub = (
        lax.all_gather(owner_of, "tile", axis=0, tiled=True),
        lax.all_gather(sub_of, "tile", axis=0, tiled=True),
    )
    all_owner = all_owner.reshape(n_owner, blocks, 4)
    all_sub = all_sub.reshape(n_owner, blocks, 4)
    recv_live, recv_block, recv_k = route_table(
        all_owner, jnp.full((n_owner,), own_index, jnp.int32), capacity
    )
    block_pick = jnp.broadcast_to(recv_block[:, :, None], (n_owner, capacity, 4))
    col_tiles = jnp.take_along_axis(all_owner * per_owner + all_sub, block_pick, axis=1)
    sub_rows = jnp.take_along_axis(all_sub, block_pick, axis=1)
    row_sub = jnp.take_along_axis(sub_rows, recv_k[:, :, None], axis=2)[:, :, 0]
    products = jnp.einsum(
        "bqlc,bqmr->bmlcr", weighted, weighted, preferred_element_type=jnp.float32
    )
    pull_terms = jnp.einsum("bqmr,bq->bmr", weighted, target, preferred_element_type=jnp.float32)
    flat_index = send_block * 4 + send_k
    live_mask = send_live.astype(jnp.float32)
    send_prod = (
        products.reshape(blocks * 4, 4, tile_width, tile_width)[flat_index]
        * live_mask[:, :, None, None, None]
    )
    send_pull = pull_terms.reshape(blocks * 4, tile_width)[flat_index] * live_mask[:, :, None]
    got_prod, got_pull = (
        lax.all_to_all(send_prod, "tile", split_axis=0, concat_axis=0, tiled=True),
        lax.all_to_all(send_pull, "tile", split_axis=0, concat_axis=0, tiled=True),
    )
    item_prod = got_prod.reshape(item_count, 4, tile_width, tile_width)
    item_pull = got_pull.reshape(item_count, tile_width)
    col_flat = col_tiles.reshape(item_count, 4)
    sub_flat = row_sub.reshape(item_count)
    gram_panel = jnp.zeros((tile_count, tile_width, per_owner, tile_width), jnp.float32)
    gram_panel = gram_panel.at[col_flat, :, sub_flat[:, None], :].add(item_prod)
    grad_part = jnp.zeros((per_owner, tile_width), jnp.float32).at[sub_flat].add(item_pull)
    summed = lax.psum_scatter(
        gram_panel.reshape(params, per_owner * tile_width).astype(jnp.bfloat16),
        "arc",
        scatter_dimension=0,
        tiled=True,
    ).astype(jnp.float32)
    gradient = lax.psum(grad_part.reshape(per_owner * tile_width), "arc")
    return (prior + summed, gradient)


def solution(mesh):
    in_specs = (
        P(("arc", "tile"), None, None),
        P(("arc", "tile"), None),
        P(("arc", "tile"), None),
        P(("arc", "tile"), None),
        P(("arc", "tile"), None),
        P(),
        P("tile"),
        P("arc", "tile"),
    )
    out_specs = (P("arc", "tile"), P("tile"))
    return jax.shard_map(
        on_device, mesh=mesh, in_specs=in_specs, out_specs=out_specs, check_vma=False
    )
```

profile of v0, /device:TPU:1, one launch (start us, length us, event | category | flops | bytes accessed | tf_op | source)
XLA Modules:
  0.0 622.8 jit_solution(12829713550981996982)
XLA Ops:
  7.2 0.8 convert_reduce_fusion
  8.0 0.1 copy.106
  8.1 0.1 reshape.349
  8.3 0.7 gather_fusion.7
  9.0 0.1 reshape.352
  9.1 0.1 copy.107
  9.2 0.1 copy.108
  9.3 0.1 reshape.254
  9.4 0.7 copy.122
  10.2 25.9 %all-gather.2 = f32[32,1,384]{2,1,0:T(1,128)S(1)} all-gather(f32[1,1,384]{2,1,0:T(1,128)S(1)} %reshape.324), channel_id=1, replica_groups=mesh['arc'=8,'tile'=32] {'tile'}, dimensions={0}, use_global_device_ids=true | all-gather | bytes 50688 | tf_op jit(solution)/shard_map/all_gather | solution.py:34
  36.1 0.1 copy.103
  36.1 0.1 reshape.246
  36.2 0.6 gather_fusion
  36.8 0.5 fusion.22
  37.4 0.1 select_reduce_fusion
  37.5 4.5 fusion
  42.0 12.0 %gather_fusion.1 = f32[64,4,128,128]{2,3,1,0:T(8,128)} fusion(f32[32,4,128,128]{2,3,1,0:T(8,128)} %bitcast.76, s32[1024]{0:T(1024)S(1)} %pad_clamp_fusion), kind=kCustom, calls=%fused_computation.5 | custom fusion | bytes 33554688 | tf_op jit(solution)/shard_map/gather | solution.py:72
  54.0 17.5 %copy.110 = f32[32,2,4,128,128]{4,3,2,1,0:T(8,128)} copy(f32[32,2,4,128,128]{3,4,2,1,0:T(8,128)} %bitcast.77) | data formatting | bytes 33554432 | tf_op jit(solution)/shard_map/gather | solution.py:72
  71.5 0.1 copy.109
  71.6 12.0 %broadcast_multiply_fusion = f32[32,2,4,128,128]{4,3,2,1,0:T(8,128)} fusion(f32[32,2,4,128,128]{4,3,2,1,0:T(8,128)} %copy.110, f32[32,2]{1,0:T(8,128)S(1)} %copy.109), kind=kLoop, calls=%fused_computation.11 | loop fusion | flops 4194304 | bytes 33554688 | tf_op jit(solution)/shard_map/mul | solution.py:72
  83.5 5.0 all-to-all-start
  88.6 283.4 %all-gather = s32[32,8,4]{1,2,0:T(4,128)S(1)} all-gather(s32[1,8,4]{1,2,0:T(4,128)S(1)} %bitcast.89), channel_id=1, replica_groups=mesh['arc'=8,'tile'=32] {'tile'}, dimensions={0}, use_global_device_ids=true | all-gather | bytes 4224 | tf_op jit(solution)/shard_map/all_gather | solution.py:53
  372.1 0.1 copy.95
  372.2 0.1 reshape.329
  372.3 0.1 reduce_window_sum.19
  372.5 0.1 copy.98
  372.7 0.2 fusion.6
  372.8 0.1 reshape.334
  373.0 25.3 %all-gather.1 = s32[32,8,4]{1,2,0:T(4,128)S(1)} all-gather(s32[1,8,4]{1,2,0:T(4,128)S(1)} %bitcast.91), channel_id=1, replica_groups=mesh['arc'=8,'tile'=32] {'tile'}, dimensions={0}, use_global_device_ids=true | all-gather | bytes 4224 | tf_op jit(solution)/shard_map/all_gather | solution.py:54
  398.3 2.7 gather_fusion.6
  401.0 2.7 gather_fusion.4
  403.8 0.1 reshape.337
  403.9 0.1 reshape.347
  404.1 0.1 copy.99
  404.1 0.1 reshape.339
  404.2 0.1 reduce_sum.77
  404.3 0.8 gather_fusion.5
  405.1 0.1 reshape.342
  405.3 0.1 copy.100
  405.4 0.1 copy.102
  405.5 0.1 reshape.270
  405.6 0.1 copy.101
  405.7 0.1 and.39
  405.8 0.2 broadcast_select_fusion
  406.0 1.0 gather_fusion.3
  407.0 0.1 fusion.8
  407.1 0.1 reshape.276
  407.2 8.9 %broadcast_in_dim.33 = f32[96,128,3,128]{3,1,2,0:T(8,128)} broadcast(f32[]{:T(128)} %constant.26.clone.1), dimensions={} | broadcast | bytes 18874372 | tf_op jit(solution)/shard_map/broadcast_in_dim | solution.py:84
  416.1 53.9 %scatter_fusion = f32[96,128,3,128]{3,1,2,0:T(8,128)} fusion(f32[96,128,3,128]{3,1,2,0:T(8,128)} %broadcast_in_dim.33, s32[256]{0:T(256)S(1)} %reshape.276, f32[256,128,128]{2,1,0:T(8,128)} %bitcast.22), kind=kCustom, calls=%fused_computation.8 | custom fusion | flops 4194304 | bytes 50333696 | tf_op jit(solution)/shard_map/scatter-add | solution.py:85
  470.0 10.1 %convert_element_type.44 = bf16[96,128,3,128]{3,1,2,0:T(8,128)(2,1)} convert(f32[96,128,3,128]{3,1,2,0:T(8,128)} %scatter_fusion) | non-fusion elementwise | flops 4718592 | bytes 28311552 | tf_op jit(solution)/shard_map/convert_element_type | solution.py:88
  480.0 13.2 %copy.111 = bf16[96,128,3,128]{1,0,3,2:T(8,128)(2,1)} copy(bf16[96,128,3,128]{3,1,2,0:T(8,128)(2,1)} %convert_element_type.44) | data formatting | bytes 18874368 | tf_op jit(solution)/shard_map/convert_element_type | solution.py:88
  493.3 11.9 %copy.129 = bf16[48,8,96,128]{3,1,2,0:T(8,128)(2,1)} copy(bf16[48,8,96,128]{3,2,1,0:T(8,128)(2,1)} %bitcast.79) | data formatting | bytes 18874368
  505.2 0.4 fusion.3
  505.6 0.6 gather_fusion.2
  506.2 0.7 broadcast_multiply_fusion.1
  506.9 4.1 all-to-all-start.1
  510.9 0.1 and.40
  511.1 2.0 copy.112
  513.1 5.1 all-to-all-done.1
  518.2 0.9 scatter_custom_fusion.1
  519.1 19.3 %psum.7 = f32[384]{0:T(512)} all-reduce(f32[384]{0:T(512)S(1)} %bitcast.92), channel_id=1, replica_groups=mesh['arc'=8,'tile'=32] {'arc'}, use_global_device_ids=true, to_apply=%region_13.16 | all-reduce | flops 384 | bytes 3072 | tf_op jit(solution)/shard_map/psum | solution.py:93
  538.4 71.5 %reduce-scatter.2.cloned.1.call-done = bf16[1536,384]{0,1:T(8,128)(2,1)} async-done(((bf16[12288,384]{0,1:T(8,128)(2,1)}), bf16[1536,384]{0,1:T(8,128)(2,1)}) %reduce-scatter.2.cloned.1.call-update) | async-done | bytes 1179664 | tf_op jit(solution)/shard_map/reduce_scatter | solution.py:87
  610.0 3.0 convert_add_fusion
  612.9 3.0 copy.115
  (47 shorter events, 0.6 us)
Async XLA Ops:
  8.2 1.2 copy-start
  8.2 1.9 copy-start.5
  8.2 27.8 %copy-start.1 = (s32[8,4]{0,1:T(4,128)S(1)}, s32[8,4]{0,1:T(4,128)}, u32[]{:S(2)}) copy-start(s32[8,4]{0,1:T(4,128)} %param.15) | copy-start | bytes 388
  8.2 27.8 %copy-start.2 = (s32[8,4]{0,1:T(4,128)S(1)}, s32[8,4]{0,1:T(4,128)}, u32[]{:S(2)}) copy-start(s32[8,4]{0,1:T(4,128)} %param.16) | copy-start | bytes 388
  8.2 29.1 %copy-start.3 = (s32[8,128]{1,0:T(8,128)S(1)}, s32[8,128]{1,0:T(8,128)}, u32[]{:S(2)}) copy-start(s32[8,128]{1,0:T(8,128)} %param.14) | copy-start | bytes 12292
  8.2 29.1 %copy-start.6 = (f32[8]{0:T(128)S(1)}, f32[8]{0:T(128)}, u32[]{:S(2)}) copy-start(f32[8]{0:T(128)} %param.17) | copy-start | bytes 100
  8.3 29.2 %copy-start.4 = (f32[8,128]{1,0:T(8,128)S(1)}, f32[8,128]{1,0:T(8,128)}, u32[]{:S(2)}) copy-start(f32[8,128]{1,0:T(8,128)} %param.13) | copy-start | bytes 12292
  83.5 323.6 %all-to-all-start = ((f32[32,2,4,128,128]{4,3,2,1,0:T(8,128)}), f32[32,2,4,128,128]{4,3,2,1,0:T(8,128)}, u32[]{:S(2)}, u32[]{:S(2)}) async-start(f32[32,2,4,128,128]{4,3,2,1,0:T(8,128)} %broadcast_multiply_fusion), calls=%async_computation | async-start | bytes 33554432 | tf_op jit(solution)/shard_map/all_to_all | solution.py:77
  88.5 521.4 %reduce-scatter.2.cloned.1.call-start = ((), (), s32[]{:S(2)}) async-start(), calls=%async_computation.3 | async-start | bytes 10616832 | tf_op jit(solution)/shard_map/reduce_scatter | solution.py:87
  506.9 11.3 %all-to-all-start.1 = ((f32[32,2,128]{2,1,0:T(2,128)}), f32[32,2,128]{2,1,0:T(2,128)S(1)}, u32[]{:S(2)}, u32[]{:S(2)}) async-start(f32[32,2,128]{2,1,0:T(2,128)} %broadcast_multiply_fusion.1), calls=%async_computation.2 | async-start | bytes 65536 | tf_op jit(solution)/shard_map/all_to_all | solution.py:78
Sparse Core Ops, SparseCore 0:
  505.3 104.6 reduce-scatter.1
where the time goes:
time: 625 us; the launch traced here: 623 us
  blocking collectives  354 us (57%)
  other arithmetic  82.1 us (13%)
  local copies, waits for them, and re-layouts  81.2 us (13%)
  waiting for transfers between devices  76.6 us (12%)
  between operations  14.4 us (2%)
  starting transfers between devices  9.08 us (1%)
    all_gather x1, blocking collectives, on_device(): lax.all_gather(owner_of, 'tile', axis=0, tiled=True)  283 us
    reduce_scatter x1, waiting for transfers between devices, on_device(): lax.psum_scatter(gram_panel.reshape(params, per_owner * tile_width).astyp...  71.5 us
    scatter-add x1, other arithmetic, on_device(): gram_panel = gram_panel.at[col_flat, :, sub_flat[:, None], :].add(item_prod)  53.9 us
    gather x2, local copies, waits for them, and re-layouts, on_device(): products.reshape(blocks * 4, 4, tile_width, tile_width)[flat_index]  29.5 us
    all_gather x1, blocking collectives, on_device(): whole_solution = lax.all_gather(solution, 'tile', axis=0, tiled=True)  25.9 us
    all_gather x1, blocking collectives, on_device(): lax.all_gather(sub_of, 'tile', axis=0, tiled=True)  25.3 us
    psum x1, blocking collectives, on_device(): gradient = lax.psum(grad_part.reshape(per_owner * tile_width), 'arc')  19.3 us
    unnamed x20, local copies, waits for them, and re-layouts  17 us
  transfers between devices with their start and end apart: 3, of which 2 were waited for; matrix products, arithmetic and copies ran while one was open for 2% of the time, Pallas kernels for 0%

commit v1 on v0

v1 whole, which is shorter than its diff:
```python
import functools

import jax
import jax.numpy as jnp
from jax import lax
from jax.experimental import pallas as pl
from jax.experimental.pallas import tpu as pltpu
from jax.sharding import PartitionSpec as P

HUBER = 1.345
TW = 128
SLOTS = 2
HEAD = 16
CHUNKS = 2
F32 = jnp.float32
BF16 = jnp.bfloat16
NT = (((1,), (1,)), ((), ()))


def pack_kernel(
    owner_ref, ids_ref, sigma_ref, design_ref, observed_ref, type_ref, sol_ref, *refs
):
    outs, (dt_ref, head_ref, table_ref) = refs[:-3], refs[-3:]
    blocks = observed_ref.shape[0]
    step = pl.program_id(0)
    group = outs[0].shape[0]
    part = TW // len(outs)

    @pl.when(step == 0)
    def _():
        n_slot = table_ref.shape[0]

        @pl.loop(0, n_slot)
        def _(i):
            table_ref[i] = -1

        @pl.loop(0, blocks * 4)
        def _(i):
            first = owner_ref[i] * SLOTS
            table_ref[jnp.where(table_ref[first] < 0, first, first + 1)] = i

        head_ref[...] = jnp.zeros_like(head_ref)
        spread = jnp.zeros(observed_ref.shape, F32)
        for k in range(sigma_ref.shape[0]):
            spread = jnp.where(type_ref[...] == k, sigma_ref[k], spread)
        for b in range(blocks):
            predicted = jnp.zeros((1, TW), F32)
            for l in range(4):
                tile = design_ref[b, :, l * TW : (l + 1) * TW].astype(F32).T
                s = sol_ref[pl.ds(ids_ref[b * 4 + l], 1), :]
                s = jnp.broadcast_to(s, (8, TW))
                predicted += jnp.dot(
                    s, tile, precision=lax.Precision.HIGHEST, preferred_element_type=F32
                )[0:1]
                dt_ref[b * 4 + l] = tile.astype(BF16)
            residual = observed_ref[b : b + 1] - predicted
            spr = spread[b : b + 1]
            scaled = jnp.abs(residual) / spr
            root = jnp.sqrt(HUBER / jnp.maximum(scaled, HUBER)) / spr
            head_ref[b, 0:1, :] = (root * residual).astype(BF16)
            for l in range(4):
                dt_ref[b * 4 + l] = (root * dt_ref[b * 4 + l].astype(F32)).astype(BF16)

    @pl.loop(0, group)
    def _(g):
        item = table_ref[step * group + g]

        @pl.when(item >= 0)
        def _():
            b = item // 4
            m = item - b * 4
            outs[0][g, 0:TW, :] = dt_ref[item]
            outs[0][g, TW : TW + HEAD, :] = head_ref[b]
            for r in range(3):
                other = b * 4 + lax.rem(m + r + 1, 4)
                for j, out in enumerate(outs):
                    base = (TW + HEAD if j == 0 else 0) + r * part
                    out[g, base : base + part, :] = dt_ref[
                        other, j * part : (j + 1) * part, :
                    ]


def pack(owner, ids, sigma, design, observed, obs_type, sol, n_owner):
    n_slot = n_owner * SLOTS
    part = TW // CHUNKS
    group = 8
    rows = [TW + HEAD + 3 * part] + [3 * part] * (CHUNKS - 1)
    blocks = observed.shape[0]
    whole = lambda *shape: pl.BlockSpec(shape, lambda i, *_: (0,) * len(shape))
    return pl.pallas_call(
        pack_kernel,
        grid_spec=pltpu.PrefetchScalarGridSpec(
            num_scalar_prefetch=3,
            grid=(n_slot // group,),
            in_specs=[
                whole(*design.shape),
                whole(*observed.shape),
                whole(*obs_type.shape),
                whole(*sol.shape),
            ],
            out_specs=[pl.BlockSpec((group, r, TW), lambda i, *_: (i, 0, 0)) for r in rows],
            scratch_shapes=[
                pltpu.VMEM((blocks * 4, TW, TW), BF16),
                pltpu.VMEM((blocks, HEAD, TW), BF16),
                pltpu.SMEM((n_slot,), jnp.int32),
            ],
        ),
        out_shape=[jax.ShapeDtypeStruct((n_slot, r, TW), BF16) for r in rows],
        name="pack",
    )(owner, ids, sigma, design, observed, obs_type, sol)


def gather_kernel(chunk, table_ref, *refs):
    first = chunk == 0
    if first:
        main_ref, panel_ref, grad_ref, acc_ref = refs
        side_ref = main_ref
    else:
        main_ref, side_ref, panel_ref, acc_ref = refs
    group = main_ref.shape[0]
    part = panel_ref.shape[1]
    base = TW + HEAD if first else 0
    step = pl.program_id(0)

    @pl.when(step == 0)
    def _():
        acc_ref[...] = jnp.zeros_like(acc_ref)
        if first:
            grad_ref[...] = jnp.zeros_like(grad_ref)

    @pl.loop(0, group)
    def _(g):
        item = (step * group + g) * 6

        @pl.when(table_ref[item] > 0)
        def _():
            own = main_ref[g, 0:TW, :]
            if first:
                side = side_ref[g, TW : base + 3 * part, :]
            else:
                side = side_ref[g]
            prod = lax.dot_general(side, own, NT, preferred_element_type=F32)
            diag = lax.dot_general(
                main_ref[g, chunk * part : (chunk + 1) * part, :],
                own,
                NT,
                preferred_element_type=F32,
            )
            acc_ref[table_ref[item + 2]] += diag
            skip = HEAD if first else 0
            for r in range(3):
                acc_ref[table_ref[item + 3 + r]] += prod[
                    skip + r * part : skip + (r + 1) * part
                ]
            if first:
                sub = table_ref[item + 1]
                grad_ref[pl.ds(sub, 1), :] += prod[0:1]

    @pl.when(step == pl.num_programs(0) - 1)
    def _():
        @pl.loop(0, acc_ref.shape[0])
        def _(i):
            panel_ref[i] = acc_ref[i].astype(BF16)


def gather(chunk, table, got, n_tile_slots):
    part = TW // CHUNKS
    group = 8
    n_slot = got[0].shape[0]
    main_rows = got[0].shape[1] if chunk == 0 else TW
    in_specs = [pl.BlockSpec((group, main_rows, TW), lambda i, *_: (i, 0, 0))]
    args = [got[0]]
    out_specs = [pl.BlockSpec((n_tile_slots, part, TW), lambda i, *_: (0, 0, 0))]
    out_shape = [jax.ShapeDtypeStruct((n_tile_slots, part, TW), BF16)]
    if chunk == 0:
        out_specs.append(pl.BlockSpec((8, TW), lambda i, *_: (0, 0)))
        out_shape.append(jax.ShapeDtypeStruct((8, TW), F32))
    else:
        in_specs.append(pl.BlockSpec((group, 3 * part, TW), lambda i, *_: (i, 0, 0)))
        args.append(got[chunk])
    return pl.pallas_call(
        functools.partial(gather_kernel, chunk),
        grid_spec=pltpu.PrefetchScalarGridSpec(
            num_scalar_prefetch=1,
            grid=(n_slot // group,),
            in_specs=in_specs,
            out_specs=out_specs,
            scratch_shapes=[pltpu.VMEM((n_tile_slots, part, TW), F32)],
        ),
        out_shape=out_shape,
        name=f"gather{chunk}",
    )(table, *args)


def final_kernel(prior_ref, *refs):
    reds, out_ref = refs[:-1], refs[-1]
    part = TW // len(reds)
    per = reds[0].shape[0]
    for j, red in enumerate(reds):
        rows = slice(j * part, (j + 1) * part)
        for s in range(per):
            cols = slice(s * TW, (s + 1) * TW)
            out_ref[rows, cols] = prior_ref[rows, cols] + red[s, 0].astype(F32)


def final(prior, reds):
    n_row = prior.shape[0] // TW
    per, _, part, _ = reds[0].shape
    spec = pl.BlockSpec((TW, prior.shape[1]), lambda i: (i, 0))
    return pl.pallas_call(
        final_kernel,
        grid=(n_row,),
        in_specs=[spec]
        + [pl.BlockSpec((per, 1, part, TW), lambda i: (0, i, 0, 0))] * len(reds),
        out_specs=spec,
        out_shape=jax.ShapeDtypeStruct(prior.shape, F32),
        name="final",
    )(prior, *reds)


def on_device(design, observed, obs_type, owner_of, sub_of, sigma_table, solution, prior):
    n_owner = lax.axis_size("tile")
    n_arc = lax.axis_size("arc")
    blocks = design.shape[0]
    per_owner = solution.shape[0] // TW
    tile_count = per_owner * n_owner
    row_tiles = tile_count // n_arc
    own_index = lax.axis_index("tile")

    tile_ids = (owner_of * per_owner + sub_of).reshape(blocks * 4)
    small = jnp.concatenate([solution, tile_ids.astype(F32)])
    small = jnp.pad(small, (0, 8 * TW - small.shape[0])).reshape(8, TW)
    everyone = lax.all_gather(small, "tile", axis=0, tiled=True).reshape(n_owner, 8, TW)
    sol = everyone[:, :per_owner].reshape(tile_count, TW)
    all_ids = everyone[:, per_owner, : blocks * 4].astype(jnp.int32)

    payload = pack(
        owner_of.reshape(-1), tile_ids, sigma_table, design, observed, obs_type, sol, n_owner
    )
    got = []
    for p in payload:
        p = p.reshape(n_owner, SLOTS, *p.shape[1:])
        g = lax.all_to_all(p, "tile", split_axis=0, concat_axis=0, tiled=True)
        got.append(g.reshape(n_owner * SLOTS, *p.shape[2:]))

    hit = (all_ids // per_owner == own_index).astype(jnp.int32)
    items = blocks * 4
    lower = (jnp.arange(items)[:, None] < jnp.arange(items)[None, :]).astype(jnp.int32)
    rank = jnp.sum(hit[:, :, None] * lower[None], axis=1)
    pick = hit[:, None, :] * (rank[:, None, :] == jnp.arange(SLOTS)[None, :, None]).astype(
        jnp.int32
    )
    sub = all_ids % per_owner
    grid = all_ids.reshape(n_owner, blocks, 4)
    columns = [jnp.ones_like(sub), sub]
    for r in range(4):
        ids = jnp.roll(grid, -r, axis=2).reshape(n_owner, items)
        columns.append(
            (ids // row_tiles) * (per_owner * row_tiles) + sub * row_tiles + ids % row_tiles
        )
    table = jnp.stack([jnp.sum(pick * c[:, None, :], axis=2) for c in columns], axis=2)
    table = table.reshape(-1)

    reds = []
    for j in range(CHUNKS):
        out = gather(j, table, got, tile_count * per_owner)
        if j == 0:
            grad = out[1][:per_owner].reshape(-1)
        panel = out[0].reshape(n_arc, per_owner, row_tiles, TW // CHUNKS, TW)
        red = lax.psum_scatter(panel, "arc", scatter_dimension=0, tiled=True)
        reds.append(red.reshape(panel.shape[1:]))
    gradient = lax.psum(grad, "arc")
    return final(prior, reds), gradient


def solution(mesh):
    both = ("arc", "tile")
    in_specs = (
        P(both, None, None),
        P(both, None),
        P(both, None),
        P(both, None),
        P(both, None),
        P(),
        P("tile"),
        P("arc", "tile"),
    )
    return jax.shard_map(
        on_device,
        mesh=mesh,
        in_specs=in_specs,
        out_specs=(P("arc", "tile"), P("tile")),
        check_vma=False,
    )
```

time: 625 us -> 321 us (0.51)
  blocking collectives: 354 us -> 89.7 us
  waiting for transfers between devices: 76.6 us -> 160 us
  other arithmetic: 82.1 us -> 2.65 us
  local copies, waits for them, and re-layouts: 81.2 us -> 4.54 us
  Pallas kernels: 0 us -> 45.2 us
    all_gather x3 -> x1, blocking collectives: 335 us -> 26.3 us  [on_device(): lax.all_gather(small, 'tile', axis=0, tiled=True).reshape(n_owner, 8, TW)]
    all_to_all x2 -> x1, waiting for transfers between devices: 5.11 us -> 64.6 us  [on_device(): g = lax.all_to_all(p, 'tile', split_axis=0, concat_axis=0, tiled=True)]
    scatter-add x2 -> x0, other arithmetic: 54.8 us -> none  [the longest x1 53.9 us: on_device(): gram_panel = gram_panel.at[col_flat, :, sub_flat[:, None], :].add(item_prod)]
    pallas_call x0 -> x4, Pallas kernels: none -> 45.2 us  [the longest x2 28.3 us: gather(): pl.pallas_call(functools.partial(gather_kernel, chunk), grid_spec=pltpu.P...]
    all_to_all x0 -> x1, blocking collectives: none -> 44.4 us  [on_device(): g = lax.all_to_all(p, 'tile', split_axis=0, concat_axis=0, tiled=True)]
    gather x22 -> x0, local copies, waits for them, and re-layouts: 39.9 us -> none  [the longest x2 29.5 us: on_device(): products.reshape(blocks * 4, 4, tile_width, tile_width)[flat_index]]
    reduce_scatter x1 -> x2, waiting for transfers between devices: 71.5 us -> 95 us  [on_device(): red = lax.psum_scatter(panel, 'arc', scatter_dimension=0, tiled=True)]
    unnamed x20 -> x10, local copies, waits for them, and re-layouts: 17 us -> 1.47 us
  transfers between devices with their start and end apart: 3 -> 3, of which waited for: 2 -> 3; matrix products, arithmetic and copies ran while one was open for 2% -> 1% of each run, Pallas kernels for 0% -> 5%
where the time goes in v1:
time: 321 us
  waiting for transfers between devices  160 us (50%)
  blocking collectives  89.7 us (28%)
  Pallas kernels  45.2 us (14%)
  between operations  14.2 us (4%)
  starting transfers between devices  4.75 us (1%)
  local copies, waits for them, and re-layouts  4.54 us (1%)
    reduce_scatter x2, waiting for transfers between devices, on_device(): red = lax.psum_scatter(panel, 'arc', scatter_dimension=0, tiled=True)  95 us
    all_to_all x1, waiting for transfers between devices, on_device(): g = lax.all_to_all(p, 'tile', split_axis=0, concat_axis=0, tiled=True)  64.6 us
    all_to_all x1, blocking collectives, on_device(): g = lax.all_to_all(p, 'tile', split_axis=0, concat_axis=0, tiled=True)  44.4 us
    pallas_call x2, Pallas kernels, gather(): pl.pallas_call(functools.partial(gather_kernel, chunk), grid_spec=pltpu.P...  28.3 us
    all_gather x1, blocking collectives, on_device(): lax.all_gather(small, 'tile', axis=0, tiled=True).reshape(n_owner, 8, TW)  26.3 us
    psum x1, blocking collectives, on_device(): gradient = lax.psum(grad, 'arc')  19 us
    pallas_call x1, Pallas kernels, pack(): pl.pallas_call(pack_kernel, grid_spec=pltpu.PrefetchScalarGridSpec(num_sc...  9.16 us
    pallas_call x1, Pallas kernels, final(): pl.pallas_call(final_kernel, grid=(n_row,), in_specs=[spec] + [pl.BlockSp...  7.7 us
  transfers between devices with their start and end apart: 3, of which 3 were waited for; matrix products, arithmetic and copies ran while one was open for 1% of the time, Pallas kernels for 5%

profile of v1, /device:TPU:1, one launch (start us, length us, event | category | flops | bytes accessed | tf_op | source)
XLA Modules:
  0.0 320.8 jit_solution(11321448577880953713)
XLA Ops:
  7.2 0.8 copy.87
  7.9 0.7 multiply_add_fusion
  8.6 0.1 copy.63
  8.7 0.1 reshape.300.ids_ref
  8.8 0.0 copy-start
  8.8 0.7 fusion.12
  9.5 26.3 %all_gather.3 = f32[256,128]{1,0:T(8,128)S(1)} all-gather(f32[8,128]{1,0:T(8,128)S(1)} %fusion.12), channel_id=1, replica_groups=mesh['arc'=8,'tile'=32] {'tile'}, dimensions={0}, use_global_device_ids=true | all-gather | bytes 135168 | tf_op jit(solution)/shard_map/all_gather | solution.py:233
  35.8 0.6 reshape.305.sol_ref
  36.5 0.6 reshape.304.owner_ref
  37.0 0.0 copy-done
  37.0 9.2 %pack.1 = (bf16[64,336,128]{2,1,0:T(8,128)(2,1)}, bf16[64,192,128]{2,1,0:T(8,128)(2,1)}) custom-call(s32[32]{0:T(128)} %reshape.304.owner_ref, s32[32]{0:T(128)} %copy-done, f32[8]{0:T(128)} %sigma_ref.1, bf16[8,128,512]{2,1,0:T(8,128)(2,1)} %design_ref.1, f32[8,128]{1,0:T(8,128)} %observed_ref.1, s32[8,128]{1,0:T(8,128)} %type_ref.1, ...), custom_call_target="tpu_custom_call" | custom-call | tf_op jit(solution)/shard_map/pack/pallas_call | solution.py:90
  46.2 44.4 %all_to_all.10 = bf16[32,2,192,128]{3,2,1,0:T(8,128)(2,1)} all-to-all(bf16[32,2,192,128]{3,2,1,0:T(8,128)(2,1)} %bitcast.48), channel_id=1, replica_groups=mesh['arc'=8,'tile'=32] {'tile'}, dimensions={0} | all-to-all | bytes 6291456 | tf_op jit(solution)/shard_map/all_to_all | solution.py:243
  90.6 4.7 %all-to-all-start = ((bf16[32,2,336,128]{3,2,1,0:T(8,128)(2,1)}), bf16[32,2,336,128]{3,2,1,0:T(8,128)(2,1)}, u32[]{:S(2)}, u32[]{:S(2)}) async-start(bf16[32,2,336,128]{3,2,1,0:T(8,128)(2,1)} %bitcast.46), calls=%async_computation | async-start | bytes 11010048 | tf_op jit(solution)/shard_map/all_to_all | solution.py:243
  95.3 0.0 reduce-scatter.5.cloned.1.call-start
  95.4 0.1 copy.64
  95.5 0.1 copy.65
  95.6 0.1 copy.67
  95.7 0.1 copy.79
  95.7 0.1 copy.81
  95.8 0.1 sign_compare_fusion
  95.9 0.1 copy.66
  96.0 0.1 copy.80
  96.1 0.1 copy.72
  96.2 0.1 copy.74
  96.3 0.1 copy.73
  96.4 0.1 compare_convert_fusion
  96.6 0.2 multiply_reduce_fusion
  96.8 0.2 fusion.5
  97.0 0.2 fusion.6
  97.2 0.3 fusion.4
  97.6 0.1 copy.86
  97.7 0.7 reshape.303.table_ref
  98.4 64.6 %all-to-all-done = bf16[32,2,336,128]{3,2,1,0:T(8,128)(2,1)} async-done(((bf16[32,2,336,128]{3,2,1,0:T(8,128)(2,1)}), bf16[32,2,336,128]{3,2,1,0:T(8,128)(2,1)}, u32[]{:S(2)}, u32[]{:S(2)}) %all-to-all-start) | async-done | bytes 5505056 | tf_op jit(solution)/shard_map/all_to_all | solution.py:243
  163.0 13.9 %gather1.1 = bf16[288,64,128]{2,1,0:T(8,128)(2,1)} custom-call(s32[384]{0:T(512)} %reshape.303.table_ref, bf16[64,336,128]{2,1,0:T(8,128)(2,1)} %bitcast.26.refs_0_, bf16[64,192,128]{2,1,0:T(8,128)(2,1)} %bitcast.45), custom_call_target="tpu_custom_call" | custom-call | tf_op jit(solution)/shard_map/gather1/pallas_call | solution.py:181
  176.9 0.0 reduce-scatter.5.cloned.1.call-update
  176.9 0.0 reduce-scatter.3.cloned.1.call-start
  177.0 14.5 %gather0.1 = (bf16[288,64,128]{2,1,0:T(8,128)(2,1)}, f32[8,128]{1,0:T(8,128)}) custom-call(s32[384]{0:T(512)} %reshape.303.table_ref, bf16[64,336,128]{2,1,0:T(8,128)(2,1)} %bitcast.26.refs_0_), custom_call_target="tpu_custom_call" | custom-call | tf_op jit(solution)/shard_map/gather0/pallas_call | solution.py:181
  191.5 0.0 copy-start.1
  191.5 0.0 reduce-scatter.3.cloned.1.call-update
  191.5 0.7 copy-done.1
  192.2 19.0 %psum.7 = f32[384]{0:T(512)} all-reduce(f32[384]{0:T(512)S(1)} %slice_bitcast_fusion), channel_id=1, replica_groups=mesh['arc'=8,'tile'=32] {'arc'}, use_global_device_ids=true, to_apply=%region_9.10 | all-reduce | flops 384 | bytes 3072 | tf_op jit(solution)/shard_map/psum | solution.py:272
  211.2 33.7 %reduce-scatter.5.cloned.1.call-done = bf16[1,3,12,64,128]{4,3,2,1,0:T(8,128)(2,1)} async-done(((bf16[8,3,12,64,128]{4,3,2,1,0:T(8,128)(2,1)}), bf16[1,3,12,64,128]{4,3,2,1,0:T(8,128)(2,1)}) %reduce-scatter.5.cloned.1.call-update) | async-done | bytes 589840 | tf_op jit(solution)/shard_map/reduce_scatter | solution.py:270
  244.9 61.3 %reduce-scatter.3.cloned.1.call-done = bf16[1,3,12,64,128]{4,3,2,1,0:T(8,128)(2,1)} async-done(((bf16[8,3,12,64,128]{4,3,2,1,0:T(8,128)(2,1)}), bf16[1,3,12,64,128]{4,3,2,1,0:T(8,128)(2,1)}) %reduce-scatter.3.cloned.1.call-update) | async-done | bytes 589840 | tf_op jit(solution)/shard_map/reduce_scatter | solution.py:270
  306.2 7.7 %final.1 = f32[1536,384]{1,0:T(8,128)} custom-call(f32[1536,384]{1,0:T(8,128)} %prior_ref.1, bf16[3,12,64,128]{3,2,1,0:T(8,128)(2,1)} %bitcast.50, bf16[3,12,64,128]{3,2,1,0:T(8,128)(2,1)} %bitcast.49), custom_call_target="tpu_custom_call" | custom-call | tf_op jit(solution)/shard_map/final/pallas_call | solution.py:210
  (17 shorter events, 0.2 us)
Async XLA Ops:
  8.8 28.3 %copy-start = (s32[32]{0:T(128)}, s32[32]{0:T(128)S(1)}, u32[]{:S(2)}) copy-start(s32[32]{0:T(128)S(1)} %reshape.300.ids_ref) | copy-start | bytes 388
  90.6 72.4 %all-to-all-start = ((bf16[32,2,336,128]{3,2,1,0:T(8,128)(2,1)}), bf16[32,2,336,128]{3,2,1,0:T(8,128)(2,1)}, u32[]{:S(2)}, u32[]{:S(2)}) async-start(bf16[32,2,336,128]{3,2,1,0:T(8,128)(2,1)} %bitcast.46), calls=%async_computation | async-start | bytes 11010048 | tf_op jit(solution)/shard_map/all_to_all | solution.py:243
  95.3 149.6 %reduce-scatter.5.cloned.1.call-start = ((), (), s32[]{:S(2)}) async-start(), calls=%async_computation.5 | async-start | bytes 5308416 | tf_op jit(solution)/shard_map/reduce_scatter | solution.py:270
  176.9 129.3 %reduce-scatter.3.cloned.1.call-start = ((), (), s32[]{:S(2)}) async-start(), calls=%async_computation.4 | async-start | bytes 5308416 | tf_op jit(solution)/shard_map/reduce_scatter | solution.py:270
  191.5 0.7 copy-start.1
Sparse Core Ops, SparseCore 0:
  177.1 67.7 reduce-scatter.4
  247.4 58.7 reduce-scatter.2

commit v2 on v1

v2 whole, which is shorter than its diff:
```python
import functools

import jax
import jax.numpy as jnp
from jax import lax
from jax.experimental import pallas as pl
from jax.experimental.pallas import tpu as pltpu
from jax.sharding import PartitionSpec as P

HUBER = 1.345
TW = 128
SLOTS = 2
HEAD = 16
PARTS = (48, 80)
UNROLL = 4
F32 = jnp.float32
BF16 = jnp.bfloat16
NT = (((1,), (1,)), ((), ()))


def weigh_kernel(
    ids_ref, sigma_ref, design_ref, observed_ref, type_ref, sol_ref, wt_ref, head_ref
):
    blocks = observed_ref.shape[0]
    head_ref[...] = jnp.zeros_like(head_ref)
    spread = jnp.zeros(observed_ref.shape, F32)
    for k in range(sigma_ref.shape[0]):
        spread = jnp.where(type_ref[...] == k, sigma_ref[k], spread)
    row = lax.broadcasted_iota(jnp.int32, (8, TW), 0)
    for b in range(blocks):
        predicted = jnp.zeros((8, TW), F32)
        for l in range(4):
            s = jnp.broadcast_to(sol_ref[pl.ds(ids_ref[b * 4 + l], 1), :], (8, TW))
            hi = s.astype(BF16).astype(F32)
            mid = (s - hi).astype(BF16).astype(F32)
            low = s - hi - mid
            terms = jnp.where(row == 0, hi, jnp.where(row == 1, mid, low))
            terms = jnp.where(row < 3, terms, 0.0).astype(BF16)
            predicted += lax.dot_general(
                terms,
                design_ref[b, :, l * TW : (l + 1) * TW],
                NT,
                preferred_element_type=F32,
            )
        predicted = jnp.sum(predicted, axis=0, keepdims=True)
        residual = observed_ref[b : b + 1] - predicted
        spr = spread[b : b + 1]
        scaled = jnp.abs(residual) / spr
        root = jnp.sqrt(HUBER / jnp.maximum(scaled, HUBER)) / spr
        head_ref[b, 0:1, :] = (root * residual).astype(BF16)
        for l in range(4):
            tile = design_ref[b, :, l * TW : (l + 1) * TW].T
            wt_ref[b * 4 + l] = (root * tile.astype(F32)).astype(BF16)


def weigh(ids, sigma, design, observed, obs_type, sol):
    blocks = observed.shape[0]
    vmem = pl.BlockSpec(memory_space=pltpu.VMEM)
    smem = pl.BlockSpec(memory_space=pltpu.SMEM)
    return pl.pallas_call(
        weigh_kernel,
        in_specs=[smem, smem, vmem, vmem, vmem, vmem],
        out_specs=[vmem, vmem],
        out_shape=[
            jax.ShapeDtypeStruct((blocks * 4, TW, TW), BF16),
            jax.ShapeDtypeStruct((blocks, HEAD, TW), BF16),
        ],
        name="weigh",
    )(ids, sigma, design, observed, obs_type, sol)


def pack_kernel(chunk, owner_ref, wt_ref, head_ref, out_ref, table_ref):
    step = pl.program_id(0)
    group = out_ref.shape[0]
    begin, part = sum(PARTS[:chunk]), PARTS[chunk]

    @pl.when(step == 0)
    def _():
        @pl.loop(0, table_ref.shape[0])
        def _(i):
            table_ref[i] = -1

        @pl.loop(0, wt_ref.shape[0])
        def _(i):
            first = owner_ref[i] * SLOTS
            table_ref[jnp.where(table_ref[first] < 0, first, first + 1)] = i

    @pl.loop(0, group)
    def _(g):
        item = table_ref[step * group + g]

        @pl.when(item >= 0)
        def _():
            b = item // 4
            m = item - b * 4
            base = 0
            if chunk == 0:
                out_ref[g, 0:TW, :] = wt_ref[item]
                base = TW
            if chunk == len(PARTS) - 1:
                out_ref[g, base : base + HEAD, :] = head_ref[b]
                base += HEAD
            for r in range(3):
                other = b * 4 + lax.rem(m + r + 1, 4)
                out_ref[g, base : base + part, :] = wt_ref[other, begin : begin + part, :]
                base += part


def payload_rows(chunk):
    rows = 3 * PARTS[chunk]
    return rows + TW * (chunk == 0) + HEAD * (chunk == len(PARTS) - 1)


def pack(chunk, owner, wt, head, n_owner):
    n_slot = n_owner * SLOTS
    group = 8
    rows = payload_rows(chunk)
    whole = lambda x: pl.BlockSpec(x.shape, lambda i, *_: (0, 0, 0))
    return pl.pallas_call(
        functools.partial(pack_kernel, chunk),
        grid_spec=pltpu.PrefetchScalarGridSpec(
            num_scalar_prefetch=1,
            grid=(n_slot // group,),
            in_specs=[whole(wt), whole(head)],
            out_specs=pl.BlockSpec((group, rows, TW), lambda i, *_: (i, 0, 0)),
            scratch_shapes=[pltpu.SMEM((n_slot,), jnp.int32)],
        ),
        out_shape=jax.ShapeDtypeStruct((n_slot, rows, TW), BF16),
        name=f"pack{chunk}",
    )(owner, wt, head)


def gather_kernel(chunk, table_ref, *refs):
    last = chunk == len(PARTS) - 1
    main_ref = refs[0]
    side_ref = refs[0] if chunk == 0 else refs[1]
    panel_ref = refs[1 if chunk == 0 else 2]
    grad_ref = refs[-2] if last else None
    acc_ref = refs[-1]
    group = main_ref.shape[0]
    begin, part = sum(PARTS[:chunk]), PARTS[chunk]
    skip = HEAD if last else 0
    top = TW if chunk == 0 else 0
    step = pl.program_id(0)

    @pl.when(step == 0)
    def _():
        if last:
            grad_ref[...] = jnp.zeros_like(grad_ref)

        @pl.loop(0, acc_ref.shape[0])
        def _(i):
            acc_ref[i] = jnp.zeros(acc_ref.shape[1:], F32)

    for g0 in range(0, group, UNROLL):
        prods = []
        for g in range(g0, g0 + UNROLL):
            own = main_ref[g, 0:TW, :]
            side = side_ref[g, top : top + skip + 3 * part, :]
            diag = main_ref[g, begin : begin + part, :]
            prods.append(
                [
                    lax.dot_general(x, own, NT, preferred_element_type=F32)
                    for x in (side, diag)
                ]
            )
        for u, (side, diag) in enumerate(prods):
            item = (step * group + g0 + u) * 5
            acc_ref[table_ref[item + 1]] += diag
            for r in range(3):
                acc_ref[table_ref[item + 2 + r]] += side[
                    skip + r * part : skip + (r + 1) * part
                ]
            if last:
                grad_ref[pl.ds(table_ref[item], 1), :] += side[0:1]

    @pl.when(step == pl.num_programs(0) - 1)
    def _():
        @pl.loop(0, panel_ref.shape[0])
        def _(i):
            panel_ref[i] = acc_ref[i].astype(BF16)


def gather(chunk, table, got, n_tile_slots):
    part = PARTS[chunk]
    group = 8
    n_slot = got[0].shape[0]
    main_rows = got[0].shape[1] if chunk == 0 else TW
    in_specs = [pl.BlockSpec((group, main_rows, TW), lambda i, *_: (i, 0, 0))]
    args = [got[0]]
    out_specs = [pl.BlockSpec((n_tile_slots, part, TW), lambda i, *_: (0, 0, 0))]
    out_shape = [jax.ShapeDtypeStruct((n_tile_slots, part, TW), BF16)]
    if chunk > 0:
        in_specs.append(
            pl.BlockSpec((group, payload_rows(chunk), TW), lambda i, *_: (i, 0, 0))
        )
        args.append(got[chunk])
    if chunk == len(PARTS) - 1:
        out_specs.append(pl.BlockSpec((8, TW), lambda i, *_: (0, 0)))
        out_shape.append(jax.ShapeDtypeStruct((8, TW), F32))
    return pl.pallas_call(
        functools.partial(gather_kernel, chunk),
        grid_spec=pltpu.PrefetchScalarGridSpec(
            num_scalar_prefetch=1,
            grid=(n_slot // group,),
            in_specs=in_specs,
            out_specs=out_specs,
            scratch_shapes=[pltpu.VMEM((n_tile_slots + 1, part, TW), F32)],
        ),
        out_shape=out_shape,
        name=f"gather{chunk}",
    )(table, *args)


def final_kernel(prior_ref, red_ref, *refs):
    out_ref = refs[-1]
    for s in range(red_ref.shape[0]):
        cols = slice(s * TW, (s + 1) * TW)
        out_ref[:, :, cols] = prior_ref[:, :, cols] + red_ref[s].astype(F32)


def final(chunk, prior, red, out):
    begin, part = sum(PARTS[:chunk]), PARTS[chunk]
    step = 16
    n_row, _, width = prior.shape
    per = red.shape[0]
    spec = pl.BlockSpec((n_row, step, width), lambda i: (0, begin // step + i, 0))
    args, in_specs, alias = [prior, red], [spec], {}
    in_specs.append(pl.BlockSpec((per, n_row, step, TW), lambda i: (0, 0, i, 0)))
    if out is not None:
        args.append(out)
        in_specs.append(pl.BlockSpec(memory_space=pl.ANY))
        alias = {2: 0}
    return pl.pallas_call(
        final_kernel,
        grid=(part // step,),
        in_specs=in_specs,
        out_specs=spec,
        out_shape=jax.ShapeDtypeStruct(prior.shape, F32),
        input_output_aliases=alias,
        name=f"final{chunk}",
    )(*args)


def on_device(design, observed, obs_type, owner_of, sub_of, sigma_table, solution, prior):
    n_owner = lax.axis_size("tile")
    n_arc = lax.axis_size("arc")
    blocks = design.shape[0]
    per_owner = solution.shape[0] // TW
    tile_count = per_owner * n_owner
    row_tiles = tile_count // n_arc
    own_index = lax.axis_index("tile")

    tile_ids = (owner_of * per_owner + sub_of).reshape(blocks * 4)
    small = jnp.concatenate([solution, tile_ids.astype(F32)])
    small = jnp.pad(small, (0, 4 * TW - small.shape[0])).reshape(1, 4, TW)
    small = jnp.broadcast_to(small, (n_owner, 4, TW))
    everyone = lax.all_to_all(small, "tile", split_axis=0, concat_axis=0, tiled=True)
    sol = everyone[:, :per_owner].reshape(tile_count, TW)
    all_ids = everyone[:, per_owner, : blocks * 4].astype(jnp.int32)

    wt, head = weigh(tile_ids, sigma_table, design, observed, obs_type, sol)
    owners = owner_of.reshape(-1)

    def exchange(chunk):
        p = pack(chunk, owners, wt, head, n_owner)
        p = p.reshape(n_owner, SLOTS, *p.shape[1:])
        return p

    def send(p):
        g = lax.all_to_all(p, "tile", split_axis=0, concat_axis=0, tiled=True)
        return g.reshape(n_owner * SLOTS, *p.shape[2:])

    spare = tile_count * per_owner
    hit = (all_ids // per_owner == own_index).astype(jnp.int32)
    items = blocks * 4
    lower = (jnp.arange(items)[:, None] < jnp.arange(items)[None, :]).astype(jnp.int32)
    rank = jnp.sum(hit[:, :, None] * lower[None], axis=1)
    pick = hit[:, None, :] * (rank[:, None, :] == jnp.arange(SLOTS)[None, :, None]).astype(
        jnp.int32
    )
    dead = 1 - jnp.sum(pick, axis=2)
    sub = all_ids % per_owner
    grid = all_ids.reshape(n_owner, blocks, 4)
    columns = [jnp.sum(pick * sub[:, None, :], axis=2) + dead * per_owner]
    for r in range(4):
        ids = jnp.roll(grid, -r, axis=2).reshape(n_owner, items)
        place = (
            (ids // row_tiles) * (per_owner * row_tiles) + sub * row_tiles + ids % row_tiles
        )
        columns.append(jnp.sum(pick * place[:, None, :], axis=2) + dead * spare)
    table = jnp.stack(columns, axis=2).reshape(-1)

    got, reds = [], []
    payload = exchange(0)
    got.append(send(payload))
    payload = exchange(1)
    panel, = gather(0, table, got, spare)
    panel, payload = lax.optimization_barrier((panel, payload))
    panel = panel.reshape(n_arc, per_owner, row_tiles, PARTS[0], TW)
    reds.append(lax.psum_scatter(panel, "arc", scatter_dimension=0, tiled=True)[0])
    got.append(send(payload))
    panel, grad = gather(1, table, got, spare)
    panel = panel.reshape(n_arc, per_owner, row_tiles, PARTS[1], TW)
    reds.append(lax.psum_scatter(panel, "arc", scatter_dimension=0, tiled=True)[0])
    gradient = lax.psum(grad[:per_owner].reshape(-1), "arc")

    prior = prior.reshape(row_tiles, TW, per_owner * TW)
    out = final(0, prior, reds[0], None)
    out = final(1, prior, reds[1], out)
    return out.reshape(row_tiles * TW, per_owner * TW), gradient


def solution(mesh):
    both = ("arc", "tile")
    in_specs = (
        P(both, None, None),
        P(both, None),
        P(both, None),
        P(both, None),
        P(both, None),
        P(),
        P("tile"),
        P("arc", "tile"),
    )
    return jax.shard_map(
        on_device,
        mesh=mesh,
        in_specs=in_specs,
        out_specs=(P("arc", "tile"), P("tile")),
        check_vma=False,
    )
```

time: 321 us -> 262 us (0.82)
  waiting for transfers between devices: 160 us -> 102 us
  blocking collectives: 89.7 us -> 75.9 us
  starting transfers between devices: 4.75 us -> 13.5 us
    reduce_scatter x2, waiting for transfers between devices: 95 us -> 49.1 us  [on_device(): lax.psum_scatter(panel, 'arc', scatter_dimension=0, tiled=True)[0]]
    all_gather x1 -> x0, blocking collectives: 26.3 us -> none  [on_device(): lax.all_gather(small, 'tile', axis=0, tiled=True).reshape(n_owner, 8, TW)]
    all_to_all x1, blocking collectives: 44.4 us -> 57.9 us  [send(): g = lax.all_to_all(p, 'tile', split_axis=0, concat_axis=0, tiled=True)]
    all_to_all x1 -> x2, waiting for transfers between devices: 64.6 us -> 52.9 us  [the longest x1 46.8 us: send(): g = lax.all_to_all(p, 'tile', split_axis=0, concat_axis=0, tiled=True)]
    all_to_all x1 -> x2, starting transfers between devices: 4.66 us -> 13.4 us  [the longest x1 8.58 us: on_device(): lax.all_to_all(small, 'tile', split_axis=0, concat_axis=0, tiled=True)]
    pallas_call x2 -> x5, Pallas kernels: 16.9 us -> 22.1 us  [the longest x2 11.8 us: pack(): pl.pallas_call(functools.partial(pack_kernel, chunk), grid_spec=pltpu.Pre...]
  transfers between devices with their start and end apart: 3 -> 4, of which waited for: 3 -> 3; matrix products, arithmetic and copies ran while one was open for 1% -> 1% of each run, Pallas kernels for 5% -> 9%
where the time goes in v2:
time: 262 us; the launch traced here: 261 us
  waiting for transfers between devices  102 us (39%)
  blocking collectives  75.9 us (29%)
  Pallas kernels  47.9 us (18%)
  between operations  14.2 us (5%)
  starting transfers between devices  13.5 us (5%)
  local copies, waits for them, and re-layouts  5.11 us (2%)
    all_to_all x1, blocking collectives, send(): g = lax.all_to_all(p, 'tile', split_axis=0, concat_axis=0, tiled=True)  57.9 us
    reduce_scatter x2, waiting for transfers between devices, on_device(): lax.psum_scatter(panel, 'arc', scatter_dimension=0, tiled=True)[0]  49.1 us
    all_to_all x1, waiting for transfers between devices, send(): g = lax.all_to_all(p, 'tile', split_axis=0, concat_axis=0, tiled=True)  46.8 us
    pallas_call x2, Pallas kernels, gather(): pl.pallas_call(functools.partial(gather_kernel, chunk), grid_spec=pltpu.P...  25.8 us
    psum x1, blocking collectives, on_device(): gradient = lax.psum(grad[:per_owner].reshape(-1), 'arc')  18 us
    pallas_call x2, Pallas kernels, pack(): pl.pallas_call(functools.partial(pack_kernel, chunk), grid_spec=pltpu.Pre...  11.8 us
    all_to_all x1, starting transfers between devices, on_device(): lax.all_to_all(small, 'tile', split_axis=0, concat_axis=0, tiled=True)  8.58 us
    pallas_call x2, Pallas kernels, final(): pl.pallas_call(final_kernel, grid=(part // step,), in_specs=in_specs, out...  7.28 us
  transfers between devices with their start and end apart: 4, of which 3 were waited for; matrix products, arithmetic and copies ran while one was open for 1% of the time, Pallas kernels for 9%

profile of v2, /device:TPU:1, one launch (start us, length us, event | category | flops | bytes accessed | tf_op | source)
XLA Modules:
  0.0 260.8 jit_solution(825847571761271883)
XLA Ops:
  7.2 0.7 multiply_add_fusion
  7.9 0.1 copy.65
  8.0 0.1 reshape.372.ids_ref
  8.0 0.0 copy-start
  8.0 0.7 fusion.27
  8.7 0.6 broadcast_in_dim.5
  9.4 8.6 %all-to-all-start = ((f32[32,4,128]{2,1,0:T(4,128)}), f32[32,4,128]{2,1,0:T(4,128)S(1)}, u32[]{:S(2)}, u32[]{:S(2)}) async-start(f32[32,4,128]{2,1,0:T(4,128)} %broadcast_in_dim.5), calls=%async_computation | async-start | bytes 131072 | tf_op jit(solution)/shard_map/all_to_all | solution.py:258
  18.0 0.8 copy.90
  18.7 0.6 reshape.374.owner_ref
  19.3 6.0 %all-to-all-done = f32[32,4,128]{2,1,0:T(4,128)S(1)} async-done(((f32[32,4,128]{2,1,0:T(4,128)}), f32[32,4,128]{2,1,0:T(4,128)S(1)}, u32[]{:S(2)}, u32[]{:S(2)}) %all-to-all-start) | async-done | bytes 65568 | tf_op jit(solution)/shard_map/all_to_all | solution.py:258
  25.3 0.6 reshape.375.sol_ref
  26.0 0.0 copy-done
  26.0 3.0 %weigh.1 = (bf16[32,128,128]{2,1,0:T(8,128)(2,1)}, bf16[8,16,128]{2,1,0:T(8,128)(2,1)}) custom-call(s32[32]{0:T(128)} %copy-done, f32[8]{0:T(128)} %sigma_ref.1, bf16[8,128,512]{2,1,0:T(8,128)(2,1)} %design_ref.1, f32[8,128]{1,0:T(8,128)} %observed_ref.1, s32[8,128]{1,0:T(8,128)} %type_ref.1, f32[96,128]{1,0:T(8,128)} %reshape.375.sol_ref), custom_call_target="tpu_custom_call" | custom-call | tf_op jit(solution)/shard_map/weigh/pallas_call | solution.py:60
  29.0 6.0 %pack0.1 = bf16[64,272,128]{2,1,0:T(8,128)(2,1)} custom-call(s32[32]{0:T(128)} %reshape.374.owner_ref, bf16[32,128,128]{2,1,0:T(8,128)(2,1)} %get-tuple-element.8.wt_ref, bf16[8,16,128]{2,1,0:T(8,128)(2,1)} %get-tuple-element.9.head_ref), custom_call_target="tpu_custom_call" | custom-call | tf_op jit(solution)/shard_map/pack0/pallas_call | solution.py:119
  34.9 4.8 %all-to-all-start.1 = ((bf16[32,2,272,128]{3,2,1,0:T(8,128)(2,1)}), bf16[32,2,272,128]{3,2,1,0:T(8,128)(2,1)}, u32[]{:S(2)}, u32[]{:S(2)}) async-start(bf16[32,2,272,128]{3,2,1,0:T(8,128)(2,1)} %bitcast.54), calls=%async_computation.1 | async-start | bytes 8912896 | tf_op jit(solution)/shard_map/all_to_all | solution.py:271
  39.7 0.0 reduce-scatter.5.cloned.1.call-start
  39.8 5.9 %pack1.1 = bf16[64,256,128]{2,1,0:T(8,128)(2,1)} custom-call(s32[32]{0:T(128)} %reshape.374.owner_ref, bf16[32,128,128]{2,1,0:T(8,128)(2,1)} %get-tuple-element.8.wt_ref, bf16[8,16,128]{2,1,0:T(8,128)(2,1)} %get-tuple-element.9.head_ref), custom_call_target="tpu_custom_call" | custom-call | tf_op jit(solution)/shard_map/pack1/pallas_call | solution.py:119
  45.7 0.1 copy.67
  45.8 0.1 copy.76
  46.0 0.1 copy.75
  46.0 0.1 copy.77
  46.2 0.1 copy.83
  46.3 0.1 copy.69
  46.4 0.1 broadcast_remainder_fusion
  46.4 0.1 copy.82
  46.5 0.1 copy.84
  46.6 0.1 copy.70
  46.6 0.1 copy.68
  46.7 0.2 multiply_reduce_fusion
  47.0 0.1 fusion.28
  47.1 0.3 fusion.4
  47.4 0.1 copy.89
  47.5 0.7 reshape.373.table_ref
  48.2 46.8 %all-to-all-done.1 = bf16[32,2,272,128]{3,2,1,0:T(8,128)(2,1)} async-done(((bf16[32,2,272,128]{3,2,1,0:T(8,128)(2,1)}), bf16[32,2,272,128]{3,2,1,0:T(8,128)(2,1)}, u32[]{:S(2)}, u32[]{:S(2)}) %all-to-all-start.1) | async-done | bytes 4456480 | tf_op jit(solution)/shard_map/all_to_all | solution.py:271
  95.1 12.4 %gather0.1 = bf16[288,48,128]{2,1,0:T(8,128)(2,1)} custom-call(s32[320]{0:T(512)} %reshape.373.table_ref, bf16[64,272,128]{2,1,0:T(8,128)(2,1)} %bitcast.26.refs_0_), custom_call_target="tpu_custom_call" | custom-call | tf_op jit(solution)/shard_map/gather0/pallas_call | solution.py:201
  107.5 0.0 reduce-scatter.5.cloned.1.call-update
  107.5 0.0 reduce-scatter.3.cloned.1.call-start
  107.5 57.9 %all_to_all.15 = bf16[32,2,256,128]{3,2,1,0:T(8,128)(2,1)} all-to-all(bf16[32,2,256,128]{3,2,1,0:T(8,128)(2,1)} %bitcast.56), channel_id=1, replica_groups=mesh['arc'=8,'tile'=32] {'tile'}, dimensions={0} | all-to-all | bytes 8388608 | tf_op jit(solution)/shard_map/all_to_all | solution.py:271
  165.5 13.4 %gather1.1 = (bf16[288,80,128]{2,1,0:T(8,128)(2,1)}, f32[8,128]{1,0:T(8,128)}) custom-call(s32[320]{0:T(512)} %reshape.373.table_ref, bf16[64,272,128]{2,1,0:T(8,128)(2,1)} %bitcast.26.refs_0_, bf16[64,256,128]{2,1,0:T(8,128)(2,1)} %bitcast.55), custom_call_target="tpu_custom_call" | custom-call | tf_op jit(solution)/shard_map/gather1/pallas_call | solution.py:201
  178.9 0.0 copy-start.1
  178.9 0.0 reduce-scatter.3.cloned.1.call-update
  179.0 0.7 copy-done.1
  179.6 18.0 %psum.7 = f32[384]{0:T(512)} all-reduce(f32[384]{0:T(512)S(1)} %slice_bitcast_fusion), channel_id=1, replica_groups=mesh['arc'=8,'tile'=32] {'arc'}, use_global_device_ids=true, to_apply=%region_9.10 | all-reduce | flops 384 | bytes 3072 | tf_op jit(solution)/shard_map/psum | solution.py:306
  197.6 0.0 reduce-scatter.5.cloned.1.call-done
  197.6 3.1 %final0.1.refs_0_ = f32[12,128,384]{2,1,0:T(8,128)} custom-call(f32[12,128,384]{2,1,0:T(8,128)} %bitcast.58, bf16[3,12,48,128]{3,2,1,0:T(8,128)(2,1)} %bitcast.63), custom_call_target="tpu_custom_call" | custom-call | tf_op jit(solution)/shard_map/final0/pallas_call | solution.py:234
  200.7 49.1 %reduce-scatter.3.cloned.1.call-done = bf16[1,3,12,80,128]{4,3,2,1,0:T(8,128)(2,1)} async-done(((bf16[8,3,12,80,128]{4,3,2,1,0:T(8,128)(2,1)}), bf16[1,3,12,80,128]{4,3,2,1,0:T(8,128)(2,1)}) %reduce-scatter.3.cloned.1.call-update) | async-done | bytes 737296 | tf_op jit(solution)/shard_map/reduce_scatter | solution.py:305
  249.7 4.2 %final1.1 = f32[12,128,384]{2,1,0:T(8,128)} custom-call(f32[12,128,384]{2,1,0:T(8,128)} %bitcast.59, bf16[3,12,80,128]{3,2,1,0:T(8,128)(2,1)} %bitcast.62, f32[12,128,384]{2,1,0:T(8,128)} %final0.1.refs_0_), custom_call_target="tpu_custom_call", output_to_operand_aliasing={{}: (2, {})} | custom-call | tf_op jit(solution)/shard_map/final1/pallas_call | solution.py:234
  (18 shorter events, 0.3 us)
Async XLA Ops:
  8.0 17.9 %copy-start = (s32[32]{0:T(128)}, s32[32]{0:T(128)S(1)}, u32[]{:S(2)}) copy-start(s32[32]{0:T(128)S(1)} %reshape.372.ids_ref) | copy-start | bytes 388
  9.4 16.0 %all-to-all-start = ((f32[32,4,128]{2,1,0:T(4,128)}), f32[32,4,128]{2,1,0:T(4,128)S(1)}, u32[]{:S(2)}, u32[]{:S(2)}) async-start(f32[32,4,128]{2,1,0:T(4,128)} %broadcast_in_dim.5), calls=%async_computation | async-start | bytes 131072 | tf_op jit(solution)/shard_map/all_to_all | solution.py:258
  34.9 60.1 %all-to-all-start.1 = ((bf16[32,2,272,128]{3,2,1,0:T(8,128)(2,1)}), bf16[32,2,272,128]{3,2,1,0:T(8,128)(2,1)}, u32[]{:S(2)}, u32[]{:S(2)}) async-start(bf16[32,2,272,128]{3,2,1,0:T(8,128)(2,1)} %bitcast.54), calls=%async_computation.1 | async-start | bytes 8912896 | tf_op jit(solution)/shard_map/all_to_all | solution.py:271
  39.7 157.9 %reduce-scatter.5.cloned.1.call-start = ((), (), s32[]{:S(2)}) async-start(), calls=%async_computation.6 | async-start | bytes 3981312 | tf_op jit(solution)/shard_map/reduce_scatter | solution.py:301
  107.5 142.2 %reduce-scatter.3.cloned.1.call-start = ((), (), s32[]{:S(2)}) async-start(), calls=%async_computation.5 | async-start | bytes 6635520 | tf_op jit(solution)/shard_map/reduce_scatter | solution.py:305
  178.9 0.7 copy-start.1
Sparse Core Ops, SparseCore 0:
  107.6 51.4 reduce-scatter.4
  179.1 70.6 reduce-scatter.2

commit v3 on v2

--- a/solution.py
+++ b/solution.py
@@ -7,20 +7,53 @@
 from jax.experimental.pallas import tpu as pltpu
 from jax.sharding import PartitionSpec as P
 
+
 HUBER = 1.345
 TW = 128
 SLOTS = 2
 HEAD = 16
 PARTS = (48, 80)
-UNROLL = 4
+UNROLL = 8
+BATCH = 6
 F32 = jnp.float32
 BF16 = jnp.bfloat16
 NT = (((1,), (1,)), ((), ()))
 
 
-def weigh_kernel(
-    ids_ref, sigma_ref, design_ref, observed_ref, type_ref, sol_ref, wt_ref, head_ref
-):
+def prepare_kernel(owner_ref, design_ref, dt_ref, table_ref):
+    blocks = design_ref.shape[0]
+
+    @pl.loop(0, table_ref.shape[0])
+    def _(i):
+        table_ref[i] = -1
+
+    @pl.loop(0, blocks * 4)
+    def _(i):
+        first = owner_ref[i] * SLOTS
+        table_ref[jnp.where(table_ref[first] < 0, first, first + 1)] = i
+
+    for b in range(blocks):
+        for l in range(4):
+            dt_ref[b * 4 + l] = design_ref[b, :, l * TW : (l + 1) * TW].T
+
+
+def prepare(owner, design, n_owner):
+    blocks = design.shape[0]
+    vmem = pl.BlockSpec(memory_space=pltpu.VMEM)
+    smem = pl.BlockSpec(memory_space=pltpu.SMEM)
+    return pl.pallas_call(
+        prepare_kernel,
+        in_specs=[smem, vmem],
+        out_specs=[vmem, smem],
+        out_shape=[
+            jax.ShapeDtypeStruct((blocks * 4, TW, TW), BF16),
+            jax.ShapeDtypeStruct((n_owner * SLOTS,), jnp.int32),
+        ],
+        name="prepare",
+    )(owner, design)
+
+
+def weigh(ids_ref, sigma_ref, dt_ref, observed_ref, type_ref, sol_ref, wt_ref, head_ref):
     blocks = observed_ref.shape[0]
     head_ref[...] = jnp.zeros_like(head_ref)
     spread = jnp.zeros(observed_ref.shape, F32)
@@ -36,12 +69,7 @@
             low = s - hi - mid
             terms = jnp.where(row == 0, hi, jnp.where(row == 1, mid, low))
             terms = jnp.where(row < 3, terms, 0.0).astype(BF16)
-            predicted += lax.dot_general(
-                terms,
-                design_ref[b, :, l * TW : (l + 1) * TW],
-                NT,
-                preferred_element_type=F32,
-            )
+            predicted += jnp.dot(terms, dt_ref[b * 4 + l], preferred_element_type=F32)
         predicted = jnp.sum(predicted, axis=0, keepdims=True)
         residual = observed_ref[b : b + 1] - predicted
         spr = spread[b : b + 1]
@@ -49,44 +77,24 @@
         root = jnp.sqrt(HUBER / jnp.maximum(scaled, HUBER)) / spr
         head_ref[b, 0:1, :] = (root * residual).astype(BF16)
         for l in range(4):
-            tile = design_ref[b, :, l * TW : (l + 1) * TW].T
-            wt_ref[b * 4 + l] = (root * tile.astype(F32)).astype(BF16)
-
-
-def weigh(ids, sigma, design, observed, obs_type, sol):
-    blocks = observed.shape[0]
-    vmem = pl.BlockSpec(memory_space=pltpu.VMEM)
-    smem = pl.BlockSpec(memory_space=pltpu.SMEM)
-    return pl.pallas_call(
-        weigh_kernel,
-        in_specs=[smem, smem, vmem, vmem, vmem, vmem],
-        out_specs=[vmem, vmem],
-        out_shape=[
-            jax.ShapeDtypeStruct((blocks * 4, TW, TW), BF16),
-            jax.ShapeDtypeStruct((blocks, HEAD, TW), BF16),
-        ],
-        name="weigh",
-    )(ids, sigma, design, observed, obs_type, sol)
-
-
-def pack_kernel(chunk, owner_ref, wt_ref, head_ref, out_ref, table_ref):
+            wt_ref[b * 4 + l] = (root * dt_ref[b * 4 + l].astype(F32)).astype(BF16)
+
+
+def pack_kernel(chunk, table_ref, *refs):
+    if chunk == 0:
+        wt_ref, head_ref, out_ref = refs[-3:]
+
+        @pl.when(pl.program_id(0) == 0)
+        def _():
+            weigh(*refs[:-1])
+
+    else:
+        wt_ref, head_ref, out_ref = refs
     step = pl.program_id(0)
     group = out_ref.shape[0]
     begin, part = sum(PARTS[:chunk]), PARTS[chunk]
 
-    @pl.when(step == 0)
-    def _():
-        @pl.loop(0, table_ref.shape[0])
-        def _(i):
-            table_ref[i] = -1
-
-        @pl.loop(0, wt_ref.shape[0])
-        def _(i):
-            first = owner_ref[i] * SLOTS
-            table_ref[jnp.where(table_ref[first] < 0, first, first + 1)] = i
-
-    @pl.loop(0, group)
-    def _(g):
+    for g in range(group):
         item = table_ref[step * group + g]
 
         @pl.when(item >= 0)
@@ -111,23 +119,35 @@
     return rows + TW * (chunk == 0) + HEAD * (chunk == len(PARTS) - 1)
 
 
-def pack(chunk, owner, wt, head, n_owner):
-    n_slot = n_owner * SLOTS
+def pack(chunk, table, *args):
+    n_slot = table.shape[0]
     group = 8
     rows = payload_rows(chunk)
-    whole = lambda x: pl.BlockSpec(x.shape, lambda i, *_: (0, 0, 0))
+    whole = lambda x: pl.BlockSpec(x.shape, lambda i, *_: (0,) * len(x.shape))
+    out_specs = [pl.BlockSpec((group, rows, TW), lambda i, *_: (i, 0, 0))]
+    out_shape = [jax.ShapeDtypeStruct((n_slot, rows, TW), BF16)]
+    if chunk == 0:
+        dt, observed = args[2], args[3]
+        kept = [
+            jax.ShapeDtypeStruct(dt.shape, BF16),
+            jax.ShapeDtypeStruct((observed.shape[0], HEAD, TW), BF16),
+        ]
+        smem = pl.BlockSpec(memory_space=pltpu.SMEM)
+        in_specs = [smem, smem] + [whole(x) for x in args[2:]]
+        out_specs = [whole(x) for x in kept] + out_specs
+        out_shape = kept + out_shape
+    else:
+        in_specs = [whole(x) for x in args]
     return pl.pallas_call(
         functools.partial(pack_kernel, chunk),
         grid_spec=pltpu.PrefetchScalarGridSpec(
             num_scalar_prefetch=1,
             grid=(n_slot // group,),
-            in_specs=[whole(wt), whole(head)],
-            out_specs=pl.BlockSpec((group, rows, TW), lambda i, *_: (i, 0, 0)),
-            scratch_shapes=[pltpu.SMEM((n_slot,), jnp.int32)],
+            in_specs=in_specs,
+            out_specs=out_specs,
         ),
-        out_shape=jax.ShapeDtypeStruct((n_slot, rows, TW), BF16),
-        name=f"pack{chunk}",
-    )(owner, wt, head)
+        out_shape=out_shape,
+    )(table, *args)
 
 
 def gather_kernel(chunk, table_ref, *refs):
@@ -135,8 +155,8 @@
     main_ref = refs[0]
     side_ref = refs[0] if chunk == 0 else refs[1]
     panel_ref = refs[1 if chunk == 0 else 2]
-    grad_ref = refs[-2] if last else None
-    acc_ref = refs[-1]
+    grad_ref = refs[-4] if last else None
+    acc_ref, cast_ref, sems = refs[-3:]
     group = main_ref.shape[0]
     begin, part = sum(PARTS[:chunk]), PARTS[chunk]
     skip = HEAD if last else 0
@@ -148,9 +168,10 @@
         if last:
             grad_ref[...] = jnp.zeros_like(grad_ref)
 
-        @pl.loop(0, acc_ref.shape[0])
+        @pl.loop(0, cast_ref.shape[0] // BATCH)
         def _(i):
-            acc_ref[i] = jnp.zeros(acc_ref.shape[1:], F32)
+            for k in range(BATCH):
+                acc_ref[i * BATCH + k] = jnp.zeros(acc_ref.shape[1:], F32)
 
     for g0 in range(0, group, UNROLL):
         prods = []
@@ -176,9 +197,24 @@
 
     @pl.when(step == pl.num_programs(0) - 1)
     def _():
-        @pl.loop(0, panel_ref.shape[0])
-        def _(i):
-            panel_ref[i] = acc_ref[i].astype(BF16)
+        pieces = sems.shape[0]
+        piece = cast_ref.shape[0] // pieces
+        copies = []
+        for p in range(pieces):
+
+            @pl.loop(0, piece // BATCH)
+            def _(i):
+                for k in range(BATCH):
+                    at = p * piece + i * BATCH + k
+                    cast_ref[at] = acc_ref[at].astype(BF16)
+
+            rows = pl.ds(p * piece, piece)
+            copies.append(
+                pltpu.make_async_copy(cast_ref.at[rows], panel_ref.at[rows], sems.at[p])
+            )
+            copies[-1].start()
+        for copy in copies:
+            copy.wait()
 
 
 def gather(chunk, table, got, n_tile_slots):
@@ -188,7 +224,7 @@
     main_rows = got[0].shape[1] if chunk == 0 else TW
     in_specs = [pl.BlockSpec((group, main_rows, TW), lambda i, *_: (i, 0, 0))]
     args = [got[0]]
-    out_specs = [pl.BlockSpec((n_tile_slots, part, TW), lambda i, *_: (0, 0, 0))]
+    out_specs = [pl.BlockSpec(memory_space=pltpu.HBM)]
     out_shape = [jax.ShapeDtypeStruct((n_tile_slots, part, TW), BF16)]
     if chunk > 0:
         in_specs.append(
@@ -205,10 +241,13 @@
             grid=(n_slot // group,),
             in_specs=in_specs,
             out_specs=out_specs,
-            scratch_shapes=[pltpu.VMEM((n_tile_slots + 1, part, TW), F32)],
+            scratch_shapes=[
+                pltpu.VMEM((n_tile_slots + 1, part, TW), F32),
+                pltpu.VMEM((n_tile_slots, part, TW), BF16),
+                pltpu.SemaphoreType.DMA((4,)),
+            ],
         ),
         out_shape=out_shape,
-        name=f"gather{chunk}",
     )(table, *args)
 
 
@@ -238,7 +277,6 @@
         out_specs=spec,
         out_shape=jax.ShapeDtypeStruct(prior.shape, F32),
         input_output_aliases=alias,
-        name=f"final{chunk}",
     )(*args)
 
 
@@ -259,15 +297,13 @@
     sol = everyone[:, :per_owner].reshape(tile_count, TW)
     all_ids = everyone[:, per_owner, : blocks * 4].astype(jnp.int32)
 
-    wt, head = weigh(tile_ids, sigma_table, design, observed, obs_type, sol)
-    owners = owner_of.reshape(-1)
-
-    def exchange(chunk):
-        p = pack(chunk, owners, wt, head, n_owner)
+    dt, slots = prepare(owner_of.reshape(-1), design, n_owner)
+    wt, head, payload = pack(
+        0, slots, tile_ids, sigma_table, dt, observed, obs_type, sol
+    )
+
+    def send(p):
         p = p.reshape(n_owner, SLOTS, *p.shape[1:])
-        return p
-
-    def send(p):
         g = lax.all_to_all(p, "tile", split_axis=0, concat_axis=0, tiled=True)
         return g.reshape(n_owner * SLOTS, *p.shape[2:])
 
@@ -292,11 +328,11 @@
     table = jnp.stack(columns, axis=2).reshape(-1)
 
     got, reds = [], []
-    payload = exchange(0)
-    got.append(send(payload))
-    payload = exchange(1)
-    panel, = gather(0, table, got, spare)
-    panel, payload = lax.optimization_barrier((panel, payload))
+    first = send(payload)
+    (payload,) = pack(1, slots, wt, head)
+    first, payload = lax.optimization_barrier((first, payload))
+    got.append(first)
+    (panel,) = gather(0, table, got, spare)
     panel = panel.reshape(n_arc, per_owner, row_tiles, PARTS[0], TW)
     reds.append(lax.psum_scatter(panel, "arc", scatter_dimension=0, tiled=True)[0])
     got.append(send(payload))

time: 262 us -> 256 us (0.977)
  waiting for transfers between devices: 102 us -> 98.8 us
  Pallas kernels: 47.9 us -> 45 us
    pallas_call x2, Pallas kernels: 25.8 us -> 21.8 us  [gather(): pl.pallas_call(functools.partial(gather_kernel, chunk), grid_spec=pltpu.P...]
    all_to_all x1, waiting for transfers between devices: 6.01 us -> 2.62 us  [on_device(): lax.all_to_all(small, 'tile', split_axis=0, concat_axis=0, tiled=True)]
  transfers between devices with their start and end apart: 4 -> 4, of which waited for: 3 -> 3; matrix products, arithmetic and copies ran while one was open for 1% -> 2% of each run, Pallas kernels for 9% -> 9%
where the time goes in v3:
time: 256 us; the launch traced here: 255 us
  waiting for transfers between devices  98.8 us (39%)
  blocking collectives  75.8 us (30%)
  Pallas kernels  45 us (18%)
  between operations  14.2 us (6%)
  starting transfers between devices  13.5 us (5%)
  local copies, waits for them, and re-layouts  5.09 us (2%)
    all_to_all x1, blocking collectives, send(): g = lax.all_to_all(p, 'tile', split_axis=0, concat_axis=0, tiled=True)  57.9 us
    reduce_scatter x2, waiting for transfers between devices, on_device(): lax.psum_scatter(panel, 'arc', scatter_dimension=0, tiled=True)[0]  49.1 us
    all_to_all x1, waiting for transfers between devices, send(): g = lax.all_to_all(p, 'tile', split_axis=0, concat_axis=0, tiled=True)  47 us
    pallas_call x2, Pallas kernels, gather(): pl.pallas_call(functools.partial(gather_kernel, chunk), grid_spec=pltpu.P...  21.8 us
    psum x1, blocking collectives, on_device(): gradient = lax.psum(grad[:per_owner].reshape(-1), 'arc')  17.9 us
    pallas_call x2, Pallas kernels, pack(): pl.pallas_call(functools.partial(pack_kernel, chunk), grid_spec=pltpu.Pre...  12.6 us
    all_to_all x1, starting transfers between devices, on_device(): lax.all_to_all(small, 'tile', split_axis=0, concat_axis=0, tiled=True)  8.58 us
    pallas_call x2, Pallas kernels, final(): pl.pallas_call(final_kernel, grid=(part // step,), in_specs=in_specs, out...  7.28 us
  transfers between devices with their start and end apart: 4, of which 3 were waited for; matrix products, arithmetic and copies ran while one was open for 2% of the time, Pallas kernels for 9%

profile of v3, /device:TPU:1, one launch (start us, length us, event | category | flops | bytes accessed | tf_op | source)
XLA Modules:
  0.0 254.7 jit_solution(4600176064700499119)
XLA Ops:
  7.2 0.7 multiply_add_fusion
  7.9 0.1 copy.65
  8.0 0.1 reshape.372.refs_0_
  8.0 0.0 copy-start
  8.0 0.7 fusion.27
  8.7 0.6 broadcast_in_dim.5
  9.4 8.6 %all-to-all-start = ((f32[32,4,128]{2,1,0:T(4,128)}), f32[32,4,128]{2,1,0:T(4,128)S(1)}, u32[]{:S(2)}, u32[]{:S(2)}) async-start(f32[32,4,128]{2,1,0:T(4,128)} %broadcast_in_dim.5), calls=%async_computation | async-start | bytes 131072 | tf_op jit(solution)/shard_map/all_to_all | solution.py:296
  17.9 0.8 copy.90
  18.7 0.6 reshape.374.owner_ref
  19.3 3.4 %prepare.1 = (bf16[32,128,128]{2,1,0:T(8,128)(2,1)}, s32[64]{0:T(128)}) custom-call(s32[32]{0:T(128)} %reshape.374.owner_ref, bf16[8,128,512]{2,1,0:T(8,128)(2,1)} %design_ref.1), custom_call_target="tpu_custom_call" | custom-call | tf_op jit(solution)/shard_map/prepare/pallas_call | solution.py:44
  22.7 2.6 %all-to-all-done = f32[32,4,128]{2,1,0:T(4,128)S(1)} async-done(((f32[32,4,128]{2,1,0:T(4,128)}), f32[32,4,128]{2,1,0:T(4,128)S(1)}, u32[]{:S(2)}, u32[]{:S(2)}) %all-to-all-start) | async-done | bytes 65568 | tf_op jit(solution)/shard_map/all_to_all | solution.py:296
  25.3 0.6 reshape.375.refs_5_
  26.0 0.0 copy-done
  26.0 6.9 %shard_map.95 = (bf16[32,128,128]{2,1,0:T(8,128)(2,1)}, bf16[8,16,128]{2,1,0:T(8,128)(2,1)}, bf16[64,272,128]{2,1,0:T(8,128)(2,1)}) custom-call(s32[64]{0:T(128)} %get-tuple-element.11.table_ref, s32[32]{0:T(128)} %copy-done, f32[8]{0:T(128)} %refs_1_.1, bf16[32,128,128]{2,1,0:T(8,128)(2,1)} %get-tuple-element.12.refs_2_, f32[8,128]{1,0:T(8,128)} %refs_3_.1, ...), custom_call_target="tpu_custom_call" | custom-call | tf_op jit(solution)/shard_map/pallas_call | solution.py:141
  32.8 4.8 %all-to-all-start.1 = ((bf16[32,2,272,128]{3,2,1,0:T(8,128)(2,1)}), bf16[32,2,272,128]{3,2,1,0:T(8,128)(2,1)}, u32[]{:S(2)}, u32[]{:S(2)}) async-start(bf16[32,2,272,128]{3,2,1,0:T(8,128)(2,1)} %bitcast.61), calls=%async_computation.1 | async-start | bytes 8912896 | tf_op jit(solution)/shard_map/all_to_all | solution.py:307
  37.7 0.0 reduce-scatter.5.cloned.1.call-start
  37.8 0.1 copy.67
  37.9 0.1 copy.76
  38.0 0.1 copy.75
  38.1 0.1 copy.77
  38.2 0.1 copy.83
  38.3 0.1 copy.69
  38.4 0.1 broadcast_remainder_fusion
  38.5 0.1 copy.82
  38.5 0.1 copy.84
  38.6 0.1 copy.70
  38.7 0.1 copy.68
  38.8 0.2 multiply_reduce_fusion
  39.0 0.1 fusion.28
  39.1 0.3 fusion.4
  39.5 0.1 copy.89
  39.6 0.7 reshape.373.table_ref
  40.3 5.7 %shard_map.96 = bf16[64,256,128]{2,1,0:T(8,128)(2,1)} custom-call(s32[64]{0:T(128)} %get-tuple-element.11.table_ref, bf16[32,128,128]{2,1,0:T(8,128)(2,1)} %get-tuple-element.14.refs_0_, bf16[8,16,128]{2,1,0:T(8,128)(2,1)} %get-tuple-element.15.refs_1_), custom_call_target="tpu_custom_call" | custom-call | tf_op jit(solution)/shard_map/pallas_call | solution.py:141
  46.0 47.0 %all-to-all-done.1 = bf16[32,2,272,128]{3,2,1,0:T(8,128)(2,1)} async-done(((bf16[32,2,272,128]{3,2,1,0:T(8,128)(2,1)}), bf16[32,2,272,128]{3,2,1,0:T(8,128)(2,1)}, u32[]{:S(2)}, u32[]{:S(2)}) %all-to-all-start.1) | async-done | bytes 4456480 | tf_op jit(solution)/shard_map/all_to_all | solution.py:307
  93.0 9.9 %shard_map.98 = bf16[288,48,128]{2,1,0:T(8,128)(2,1)} custom-call(s32[320]{0:T(512)} %reshape.373.table_ref, bf16[64,272,128]{2,1,0:T(8,128)(2,1)} %bitcast.26.refs_0_), custom_call_target="tpu_custom_call" | custom-call | tf_op jit(solution)/shard_map/pallas_call | solution.py:237
  102.9 0.0 reduce-scatter.5.cloned.1.call-update
  102.9 0.0 reduce-scatter.3.cloned.1.call-start
  103.0 57.9 %all_to_all.15 = bf16[32,2,256,128]{3,2,1,0:T(8,128)(2,1)} all-to-all(bf16[32,2,256,128]{3,2,1,0:T(8,128)(2,1)} %bitcast.55), channel_id=1, replica_groups=mesh['arc'=8,'tile'=32] {'tile'}, dimensions={0} | all-to-all | bytes 8388608 | tf_op jit(solution)/shard_map/all_to_all | solution.py:307
  160.9 11.9 %shard_map.97 = (bf16[288,80,128]{2,1,0:T(8,128)(2,1)}, f32[8,128]{1,0:T(8,128)}) custom-call(s32[320]{0:T(512)} %reshape.373.table_ref, bf16[64,272,128]{2,1,0:T(8,128)(2,1)} %bitcast.26.refs_0_, bf16[64,256,128]{2,1,0:T(8,128)(2,1)} %bitcast.54), custom_call_target="tpu_custom_call" | custom-call | tf_op jit(solution)/shard_map/pallas_call | solution.py:237
  172.8 0.0 copy-start.1
  172.8 0.0 reduce-scatter.3.cloned.1.call-update
  172.8 0.7 copy-done.1
  173.5 17.9 %psum.7 = f32[384]{0:T(512)} all-reduce(f32[384]{0:T(512)S(1)} %slice_bitcast_fusion), channel_id=1, replica_groups=mesh['arc'=8,'tile'=32] {'arc'}, use_global_device_ids=true, to_apply=%region_9.10 | all-reduce | flops 384 | bytes 3072 | tf_op jit(solution)/shard_map/psum | solution.py:342
  191.4 0.0 reduce-scatter.5.cloned.1.call-done
  191.4 3.1 %shard_map.99.refs_0_ = f32[12,128,384]{2,1,0:T(8,128)} custom-call(f32[12,128,384]{2,1,0:T(8,128)} %bitcast.57, bf16[3,12,48,128]{3,2,1,0:T(8,128)(2,1)} %bitcast.63), custom_call_target="tpu_custom_call" | custom-call | tf_op jit(solution)/shard_map/pallas_call | solution.py:273
  194.5 49.1 %reduce-scatter.3.cloned.1.call-done = bf16[1,3,12,80,128]{4,3,2,1,0:T(8,128)(2,1)} async-done(((bf16[8,3,12,80,128]{4,3,2,1,0:T(8,128)(2,1)}), bf16[1,3,12,80,128]{4,3,2,1,0:T(8,128)(2,1)}) %reduce-scatter.3.cloned.1.call-update) | async-done | bytes 737296 | tf_op jit(solution)/shard_map/reduce_scatter | solution.py:341
  243.6 4.2 %shard_map.100 = f32[12,128,384]{2,1,0:T(8,128)} custom-call(f32[12,128,384]{2,1,0:T(8,128)} %bitcast.58, bf16[3,12,80,128]{3,2,1,0:T(8,128)(2,1)} %bitcast.62, f32[12,128,384]{2,1,0:T(8,128)} %shard_map.99.refs_0_), custom_call_target="tpu_custom_call", output_to_operand_aliasing={{}: (2, {})} | custom-call | tf_op jit(solution)/shard_map/pallas_call | solution.py:273
  (18 shorter events, 0.3 us)
Async XLA Ops:
  8.0 17.9 %copy-start = (s32[32]{0:T(128)}, s32[32]{0:T(128)S(1)}, u32[]{:S(2)}) copy-start(s32[32]{0:T(128)S(1)} %reshape.372.refs_0_) | copy-start | bytes 388
  9.4 16.0 %all-to-all-start = ((f32[32,4,128]{2,1,0:T(4,128)}), f32[32,4,128]{2,1,0:T(4,128)S(1)}, u32[]{:S(2)}, u32[]{:S(2)}) async-start(f32[32,4,128]{2,1,0:T(4,128)} %broadcast_in_dim.5), calls=%async_computation | async-start | bytes 131072 | tf_op jit(solution)/shard_map/all_to_all | solution.py:296
  32.8 60.2 %all-to-all-start.1 = ((bf16[32,2,272,128]{3,2,1,0:T(8,128)(2,1)}), bf16[32,2,272,128]{3,2,1,0:T(8,128)(2,1)}, u32[]{:S(2)}, u32[]{:S(2)}) async-start(bf16[32,2,272,128]{3,2,1,0:T(8,128)(2,1)} %bitcast.61), calls=%async_computation.1 | async-start | bytes 8912896 | tf_op jit(solution)/shard_map/all_to_all | solution.py:307
  37.7 153.8 %reduce-scatter.5.cloned.1.call-start = ((), (), s32[]{:S(2)}) async-start(), calls=%async_computation.6 | async-start | bytes 3981312 | tf_op jit(solution)/shard_map/reduce_scatter | solution.py:337
  102.9 140.7 %reduce-scatter.3.cloned.1.call-start = ((), (), s32[]{:S(2)}) async-start(), calls=%async_computation.5 | async-start | bytes 6635520 | tf_op jit(solution)/shard_map/reduce_scatter | solution.py:341
  172.8 0.7 copy-start.1
Sparse Core Ops, SparseCore 0:
  103.0 51.4 reduce-scatter.4
  172.9 70.6 reduce-scatter.2

commit v4 on v3

--- a/solution.py
+++ b/solution.py
@@ -15,6 +15,7 @@
 PARTS = (48, 80)
 UNROLL = 8
 BATCH = 6
+ENTRY = 8
 F32 = jnp.float32
 BF16 = jnp.bfloat16
 NT = (((1,), (1,)), ((), ()))
@@ -150,11 +151,61 @@
     )(table, *args)
 
 
+def route_kernel(per_owner, n_arc, row_tiles, items, where_ref, all_ref, out_ref):
+    ids = all_ref[:, per_owner, :].astype(jnp.int32)
+    lane = lax.broadcasted_iota(jnp.int32, ids.shape, 1)
+    own, arc = where_ref[0], where_ref[1]
+    first = own * per_owner
+    sub = ids - first
+    hit = (sub >= 0) & (sub < per_owner) & (lane < items)
+    taken = hit.astype(F32)
+    k = lax.broadcasted_iota(jnp.int32, (TW, TW), 0)
+    upper = (k < lax.broadcasted_iota(jnp.int32, (TW, TW), 1)).astype(F32)
+    rank = jnp.dot(taken, upper, preferred_element_type=F32)
+    half = row_tiles // 2
+    columns = [sub]
+    for r in range(4):
+        ahead = pltpu.roll(ids, TW - r, 1) if r else ids
+        behind = pltpu.roll(ids, 4 - r, 1) if r else ids
+        tile = jnp.where(lane % 4 + r < 4, ahead, behind)
+        high = jnp.zeros_like(tile)
+        for a in range(1, n_arc):
+            high += (tile >= a * row_tiles).astype(jnp.int32)
+        row = tile - high * row_tiles
+        side = (row >= half).astype(jnp.int32)
+        distance = high - arc
+        distance = jnp.where(distance < 0, distance + n_arc, distance)
+        columns.append(((distance * 2 + side) * per_owner + sub) * half + row - side * half)
+    dead = [per_owner] + [n_arc * row_tiles * per_owner] * 4
+    out = jnp.zeros(out_ref.shape, F32)
+    at = lax.broadcasted_iota(jnp.int32, out_ref.shape, 1)
+    for slot in range(SLOTS):
+        pick = jnp.where(rank == slot, taken, 0.0)
+        live = jnp.sum(pick, axis=1, keepdims=True)
+        for c, column in enumerate(columns):
+            value = jnp.sum(pick * column.astype(F32), axis=1, keepdims=True)
+            value += (1.0 - live) * dead[c]
+            out = jnp.where(at == slot * ENTRY + c, value, out)
+    out_ref[...] = out.astype(jnp.int32)
+
+
+def route(where, everyone, per_owner, n_arc, row_tiles, items):
+    n_owner = everyone.shape[0]
+    vmem = pl.BlockSpec(memory_space=pltpu.VMEM)
+    return pl.pallas_call(
+        functools.partial(route_kernel, per_owner, n_arc, row_tiles, items),
+        in_specs=[pl.BlockSpec(memory_space=pltpu.SMEM), vmem],
+        out_specs=vmem,
+        out_shape=jax.ShapeDtypeStruct((n_owner, SLOTS * ENTRY), jnp.int32),
+        name="route",
+    )(where, everyone)
+
+
 def gather_kernel(chunk, table_ref, *refs):
     last = chunk == len(PARTS) - 1
     main_ref = refs[0]
     side_ref = refs[0] if chunk == 0 else refs[1]
-    panel_ref = refs[1 if chunk == 0 else 2]
+    panel_ref, up_ref, down_ref = refs[1 if chunk == 0 else 2 :][:3]
     grad_ref = refs[-4] if last else None
     acc_ref, cast_ref, sems = refs[-3:]
     group = main_ref.shape[0]
@@ -186,7 +237,7 @@
                 ]
             )
         for u, (side, diag) in enumerate(prods):
-            item = (step * group + g0 + u) * 5
+            item = (step * group + g0 + u) * ENTRY
             acc_ref[table_ref[item + 1]] += diag
             for r in range(3):
                 acc_ref[table_ref[item + 2 + r]] += side[
@@ -197,10 +248,11 @@
 
     @pl.when(step == pl.num_programs(0) - 1)
     def _():
-        pieces = sems.shape[0]
-        piece = cast_ref.shape[0] // pieces
+        n_arc = sems.shape[0] - 1
+        piece = cast_ref.shape[0] // n_arc
+        half = piece // 2
         copies = []
-        for p in range(pieces):
+        for n, p in enumerate([n_arc // 2] + [p for p in range(n_arc) if p != n_arc // 2]):
 
             @pl.loop(0, piece // BATCH)
             def _(i):
@@ -208,24 +260,33 @@
                     at = p * piece + i * BATCH + k
                     cast_ref[at] = acc_ref[at].astype(BF16)
 
-            rows = pl.ds(p * piece, piece)
-            copies.append(
-                pltpu.make_async_copy(cast_ref.at[rows], panel_ref.at[rows], sems.at[p])
-            )
-            copies[-1].start()
+            if n == 0:
+                moves = [
+                    (pl.ds(p * piece, half), up_ref, n_arc),
+                    (pl.ds(p * piece + half, half), down_ref, p),
+                ]
+            else:
+                rows = pl.ds(p * piece, piece)
+                moves = [(rows, panel_ref.at[rows], p)]
+            for rows, target, sem in moves:
+                copies.append(pltpu.make_async_copy(cast_ref.at[rows], target, sems.at[sem]))
+                copies[-1].start()
         for copy in copies:
             copy.wait()
 
 
-def gather(chunk, table, got, n_tile_slots):
+def gather(chunk, table, got, n_tile_slots, n_arc):
     part = PARTS[chunk]
     group = 8
     n_slot = got[0].shape[0]
     main_rows = got[0].shape[1] if chunk == 0 else TW
     in_specs = [pl.BlockSpec((group, main_rows, TW), lambda i, *_: (i, 0, 0))]
     args = [got[0]]
-    out_specs = [pl.BlockSpec(memory_space=pltpu.HBM)]
-    out_shape = [jax.ShapeDtypeStruct((n_tile_slots, part, TW), BF16)]
+    out_specs = [pl.BlockSpec(memory_space=pltpu.HBM)] * 3
+    half = n_tile_slots // n_arc // 2
+    out_shape = [
+        jax.ShapeDtypeStruct((n, part, TW), BF16) for n in (n_tile_slots, half, half)
+    ]
     if chunk > 0:
         in_specs.append(
             pl.BlockSpec((group, payload_rows(chunk), TW), lambda i, *_: (i, 0, 0))
@@ -244,32 +305,43 @@
             scratch_shapes=[
                 pltpu.VMEM((n_tile_slots + 1, part, TW), F32),
                 pltpu.VMEM((n_tile_slots, part, TW), BF16),
-                pltpu.SemaphoreType.DMA((4,)),
+                pltpu.SemaphoreType.DMA((n_arc + 1,)),
             ],
         ),
         out_shape=out_shape,
     )(table, *args)
 
 
-def final_kernel(prior_ref, red_ref, *refs):
+def final_kernel(prior_ref, own_ref, up_ref, down_ref, *refs):
     out_ref = refs[-1]
-    for s in range(red_ref.shape[0]):
-        cols = slice(s * TW, (s + 1) * TW)
-        out_ref[:, :, cols] = prior_ref[:, :, cols] + red_ref[s].astype(F32)
-
-
-def final(chunk, prior, red, out):
+    n_row, _, width = prior_ref.shape
+    per = width // TW
+    half = n_row // 2
+    for h in range(2):
+        for s in range(per):
+            rows = slice(h * half, (h + 1) * half)
+            cols = slice(s * TW, (s + 1) * TW)
+            tiles = slice((h * per + s) * half, (h * per + s + 1) * half)
+            out_ref[rows, :, cols] = (
+                prior_ref[rows, :, cols]
+                + own_ref[tiles].astype(F32)
+                + up_ref[tiles].astype(F32)
+                + down_ref[tiles].astype(F32)
+            )
+
+
+def final(chunk, prior, panel, up, down, out):
     begin, part = sum(PARTS[:chunk]), PARTS[chunk]
     step = 16
     n_row, _, width = prior.shape
-    per = red.shape[0]
+    per = up.shape[0]
     spec = pl.BlockSpec((n_row, step, width), lambda i: (0, begin // step + i, 0))
-    args, in_specs, alias = [prior, red], [spec], {}
-    in_specs.append(pl.BlockSpec((per, n_row, step, TW), lambda i: (0, 0, i, 0)))
+    tiles = pl.BlockSpec((per, step, TW), lambda i: (0, i, 0))
+    args, in_specs, alias = [prior, panel, up, down], [spec] + [tiles] * 3, {}
     if out is not None:
         args.append(out)
         in_specs.append(pl.BlockSpec(memory_space=pl.ANY))
-        alias = {2: 0}
+        alias = {4: 0}
     return pl.pallas_call(
         final_kernel,
         grid=(part // step,),
@@ -280,6 +352,42 @@
     )(*args)
 
 
+def ring(panel, up, down, grad, n_arc):
+    piece = panel.shape[0] // n_arc
+    half = piece // 2
+    far = n_arc // 2
+    rising = [(i, (i + 1) % n_arc) for i in range(n_arc)]
+    falling = [((i + 1) % n_arc, i) for i in range(n_arc)]
+    own = lambda p, a, b: panel[p * piece + a : p * piece + b]
+    add = lambda x, y: (x.astype(F32) + y.astype(F32)).astype(BF16)
+    for s in range(far):
+        if s == 1:
+            up = jnp.concatenate([add(own(far - 1, 0, half), up), own(far - 1, half, piece)])
+            down = jnp.concatenate(
+                [own(far + 1, 0, half), add(own(far + 1, half, piece), down)]
+            )
+        elif s > 1:
+            up = add(own(far - s, 0, piece), up)
+            down = add(own(far + s, 0, piece), down)
+        if grad is None:
+            up, down = lax.optimization_barrier((up, down))
+        else:
+            up, down, grad = lax.optimization_barrier((up, down, grad))
+        up = lax.ppermute(up, "arc", rising)
+        down = lax.ppermute(down, "arc", falling)
+        if grad is None:
+            up, down = lax.optimization_barrier((up, down))
+        else:
+            other = grad
+            if 1 << s < n_arc:
+                swap = [(i, i ^ (1 << s)) for i in range(n_arc)]
+                other = lax.ppermute(grad, "arc", swap)
+            up, down, other = lax.optimization_barrier((up, down, other))
+            if 1 << s < n_arc:
+                grad = grad + other
+    return up, down, grad
+
+
 def on_device(design, observed, obs_type, owner_of, sub_of, sigma_table, solution, prior):
     n_owner = lax.axis_size("tile")
     n_arc = lax.axis_size("arc")
@@ -288,6 +396,7 @@
     tile_count = per_owner * n_owner
     row_tiles = tile_count // n_arc
     own_index = lax.axis_index("tile")
+    arc_index = lax.axis_index("arc")
 
     tile_ids = (owner_of * per_owner + sub_of).reshape(blocks * 4)
     small = jnp.concatenate([solution, tile_ids.astype(F32)])
@@ -295,7 +404,6 @@
     small = jnp.broadcast_to(small, (n_owner, 4, TW))
     everyone = lax.all_to_all(small, "tile", split_axis=0, concat_axis=0, tiled=True)
     sol = everyone[:, :per_owner].reshape(tile_count, TW)
-    all_ids = everyone[:, per_owner, : blocks * 4].astype(jnp.int32)
 
     dt, slots = prepare(owner_of.reshape(-1), design, n_owner)
     wt, head, payload = pack(
@@ -308,42 +416,24 @@
         return g.reshape(n_owner * SLOTS, *p.shape[2:])
 
     spare = tile_count * per_owner
-    hit = (all_ids // per_owner == own_index).astype(jnp.int32)
-    items = blocks * 4
-    lower = (jnp.arange(items)[:, None] < jnp.arange(items)[None, :]).astype(jnp.int32)
-    rank = jnp.sum(hit[:, :, None] * lower[None], axis=1)
-    pick = hit[:, None, :] * (rank[:, None, :] == jnp.arange(SLOTS)[None, :, None]).astype(
-        jnp.int32
-    )
-    dead = 1 - jnp.sum(pick, axis=2)
-    sub = all_ids % per_owner
-    grid = all_ids.reshape(n_owner, blocks, 4)
-    columns = [jnp.sum(pick * sub[:, None, :], axis=2) + dead * per_owner]
-    for r in range(4):
-        ids = jnp.roll(grid, -r, axis=2).reshape(n_owner, items)
-        place = (
-            (ids // row_tiles) * (per_owner * row_tiles) + sub * row_tiles + ids % row_tiles
-        )
-        columns.append(jnp.sum(pick * place[:, None, :], axis=2) + dead * spare)
-    table = jnp.stack(columns, axis=2).reshape(-1)
-
-    got, reds = [], []
+    where = jnp.stack([own_index, arc_index]).astype(jnp.int32)
+    table = route(where, everyone, per_owner, n_arc, row_tiles, blocks * 4).reshape(-1)
+
+    got = []
     first = send(payload)
     (payload,) = pack(1, slots, wt, head)
-    first, payload = lax.optimization_barrier((first, payload))
+    first, payload, table = lax.optimization_barrier((first, payload, table))
     got.append(first)
-    (panel,) = gather(0, table, got, spare)
-    panel = panel.reshape(n_arc, per_owner, row_tiles, PARTS[0], TW)
-    reds.append(lax.psum_scatter(panel, "arc", scatter_dimension=0, tiled=True)[0])
+    panel0, up, down = gather(0, table, got, spare, n_arc)
     got.append(send(payload))
-    panel, grad = gather(1, table, got, spare)
-    panel = panel.reshape(n_arc, per_owner, row_tiles, PARTS[1], TW)
-    reds.append(lax.psum_scatter(panel, "arc", scatter_dimension=0, tiled=True)[0])
-    gradient = lax.psum(grad[:per_owner].reshape(-1), "arc")
+    up0, down0, _ = ring(panel0, up, down, None, n_arc)
+    panel1, up, down, grad = gather(1, table, got, spare, n_arc)
+    up1, down1, grad = ring(panel1, up, down, grad, n_arc)
+    gradient = grad[:per_owner].reshape(-1)
 
     prior = prior.reshape(row_tiles, TW, per_owner * TW)
-    out = final(0, prior, reds[0], None)
-    out = final(1, prior, reds[1], out)
+    out = final(0, prior, panel0, up0, down0, None)
+    out = final(1, prior, panel1, up1, down1, out)
     return out.reshape(row_tiles * TW, per_owner * TW), gradient
 
 

time: 256 us -> 277 us (1.082)
  starting transfers between devices: 13.5 us -> 39.7 us
  blocking collectives: 75.8 us -> 57.9 us
  waiting for transfers between devices: 98.8 us -> 113 us
  between operations: 14.2 us -> 0.87 us
  local copies, waits for them, and re-layouts: 5.09 us -> 9.21 us
  other arithmetic: 2.23 us -> 5.1 us
  Pallas kernels: 45 us -> 47.8 us
    ppermute x0 -> x19, waiting for transfers between devices: none -> 64.5 us  [the longest x8 38.8 us: ring(): up = lax.ppermute(up, 'arc', rising)]
    reduce_scatter x2 -> x0, waiting for transfers between devices: 49.1 us -> none  [on_device(): lax.psum_scatter(panel, 'arc', scatter_dimension=0, tiled=True)[0]]
    ppermute x0 -> x19, starting transfers between devices: none -> 26.3 us  [the longest x8 22.2 us: ring(): down = lax.ppermute(down, 'arc', falling)]
    psum x1 -> x0, blocking collectives: 17.9 us -> none  [on_device(): gradient = lax.psum(grad[:per_owner].reshape(-1), 'arc')]
    convert_element_type x3 -> x6, other arithmetic: 0.04 us -> 2.84 us  [ring(): add = lambda x, y: (x.astype(F32) + y.astype(F32)).astype(BF16)]
  transfers between devices with their start and end apart: 4 -> 21, of which waited for: 3 -> 6; matrix products, arithmetic and copies ran while one was open for 2% -> 3% of each run, Pallas kernels for 9% -> 9%
where the time goes in v4:
time: 277 us; the launch traced here: 273 us
  waiting for transfers between devices  113 us (41%)
  blocking collectives  57.9 us (21%)
  Pallas kernels  47.8 us (17%)
  starting transfers between devices  39.7 us (14%)
  local copies, waits for them, and re-layouts  9.21 us (3%)
  other arithmetic  5.1 us (2%)
    all_to_all x1, blocking collectives, send(): g = lax.all_to_all(p, 'tile', split_axis=0, concat_axis=0, tiled=True)  57.9 us
    all_to_all x1, waiting for transfers between devices, send(): g = lax.all_to_all(p, 'tile', split_axis=0, concat_axis=0, tiled=True)  45.8 us
    ppermute x8, waiting for transfers between devices, ring(): up = lax.ppermute(up, 'arc', rising)  38.8 us
    ppermute x3, waiting for transfers between devices, ring(): other = lax.ppermute(grad, 'arc', swap)  25.7 us
    ppermute x8, starting transfers between devices, ring(): down = lax.ppermute(down, 'arc', falling)  22.2 us
    pallas_call x2, Pallas kernels, gather(): pl.pallas_call(functools.partial(gather_kernel, chunk), grid_spec=pltpu.P...  21.9 us
    pallas_call x2, Pallas kernels, pack(): pl.pallas_call(functools.partial(pack_kernel, chunk), grid_spec=pltpu.Pre...  12.5 us
    all_to_all x1, starting transfers between devices, on_device(): lax.all_to_all(small, 'tile', split_axis=0, concat_axis=0, tiled=True)  8.58 us
  transfers between devices with their start and end apart: 21, of which 6 were waited for; matrix products, arithmetic and copies ran while one was open for 3% of the time, Pallas kernels for 9%

profile of v4, /device:TPU:1, one launch (start us, length us, event | category | flops | bytes accessed | tf_op | source)
XLA Modules:
  0.0 273.5 jit_solution(4523133837309684151)
XLA Ops:
  0.6 0.7 multiply_add_fusion
  1.3 0.1 copy.14
  1.4 0.1 reshape.41.refs_0_
  1.5 0.7 fusion
  2.2 0.6 broadcast_in_dim.8
  2.8 8.6 %all-to-all-start = ((f32[32,4,128]{2,1,0:T(4,128)}), f32[32,4,128]{2,1,0:T(4,128)S(1)}, u32[]{:S(2)}, u32[]{:S(2)}) async-start(f32[32,4,128]{2,1,0:T(4,128)} %broadcast_in_dim.8), calls=%async_computation | async-start | bytes 131072 | tf_op jit(solution)/shard_map/all_to_all | solution.py:405
  11.4 0.8 copy.13
  12.2 0.6 reshape.40.owner_ref
  12.8 3.4 %prepare.1 = (bf16[32,128,128]{2,1,0:T(8,128)(2,1)}, s32[64]{0:T(128)}) custom-call(s32[32]{0:T(128)} %reshape.40.owner_ref, bf16[8,128,512]{2,1,0:T(8,128)(2,1)} %design_ref.1), custom_call_target="tpu_custom_call" | custom-call | tf_op jit(solution)/shard_map/prepare/pallas_call | solution.py:45
  16.2 2.6 all-to-all-done.all_ref
  18.8 0.6 reshape.42.refs_5_
  19.4 6.9 %shard_map.95 = (bf16[32,128,128]{2,1,0:T(8,128)(2,1)}, bf16[8,16,128]{2,1,0:T(8,128)(2,1)}, bf16[64,272,128]{2,1,0:T(8,128)(2,1)}) custom-call(s32[64]{0:T(128)} %get-tuple-element.56.table_ref, s32[32]{0:T(128)} %copy-done.7, f32[8]{0:T(128)} %refs_1_.1, bf16[32,128,128]{2,1,0:T(8,128)(2,1)} %get-tuple-element.57.refs_2_, f32[8,128]{1,0:T(8,128)} %refs_3_.1, ...), custom_call_target="tpu_custom_call" | custom-call | tf_op jit(solution)/shard_map/pallas_call | solution.py:142
  26.3 4.8 %all-to-all-start.1 = ((bf16[32,2,272,128]{3,2,1,0:T(8,128)(2,1)}), bf16[32,2,272,128]{3,2,1,0:T(8,128)(2,1)}, u32[]{:S(2)}, u32[]{:S(2)}) async-start(bf16[32,2,272,128]{3,2,1,0:T(8,128)(2,1)} %bitcast.20), calls=%async_computation.1 | async-start | bytes 8912896 | tf_op jit(solution)/shard_map/all_to_all | solution.py:415
  31.2 0.6 pad_add_fusion.where_ref
  31.8 1.9 route.1
  33.7 1.4 reshape.45.table_ref
  35.0 5.7 %shard_map.96 = bf16[64,256,128]{2,1,0:T(8,128)(2,1)} custom-call(s32[64]{0:T(128)} %get-tuple-element.56.table_ref, bf16[32,128,128]{2,1,0:T(8,128)(2,1)} %get-tuple-element.59.refs_0_, bf16[8,16,128]{2,1,0:T(8,128)(2,1)} %get-tuple-element.60.refs_1_), custom_call_target="tpu_custom_call" | custom-call | tf_op jit(solution)/shard_map/pallas_call | solution.py:142
  40.7 45.8 %all-to-all-done.1 = bf16[32,2,272,128]{3,2,1,0:T(8,128)(2,1)} async-done(((bf16[32,2,272,128]{3,2,1,0:T(8,128)(2,1)}), bf16[32,2,272,128]{3,2,1,0:T(8,128)(2,1)}, u32[]{:S(2)}, u32[]{:S(2)}) %all-to-all-start.1) | async-done | bytes 4456480 | tf_op jit(solution)/shard_map/all_to_all | solution.py:415
  86.5 57.9 %all_to_all.15 = bf16[32,2,256,128]{3,2,1,0:T(8,128)(2,1)} all-to-all(bf16[32,2,256,128]{3,2,1,0:T(8,128)(2,1)} %bitcast.16), channel_id=1, replica_groups=mesh['arc'=8,'tile'=32] {'tile'}, dimensions={0} | all-to-all | bytes 8388608 | tf_op jit(solution)/shard_map/all_to_all | solution.py:415
  144.4 11.8 %shard_map.97 = (bf16[288,80,128]{2,1,0:T(8,128)(2,1)}, bf16[18,80,128]{2,1,0:T(8,128)(2,1)}, bf16[18,80,128]{2,1,0:T(8,128)(2,1)}, f32[8,128]{1,0:T(8,128)}) custom-call(s32[512]{0:T(512)} %reshape.45.table_ref, bf16[64,272,128]{2,1,0:T(8,128)(2,1)} %bitcast.3.refs_0_, bf16[64,256,128]{2,1,0:T(8,128)(2,1)} %bitcast.15), custom_call_target="tpu_custom_call" | custom-call | tf_op jit(solution)/shard_map/pallas_call | solution.py:298
  156.3 1.7 collective-permute-start
  158.0 4.0 %collective-permute-start.1 = (bf16[18,80,128]{2,1,0:T(8,128)(2,1)}, bf16[18,80,128]{2,1,0:T(8,128)(2,1)S(1)}, u32[]{:S(2)}, u32[]{:S(2)}) collective-permute-start(bf16[18,80,128]{2,1,0:T(8,128)(2,1)} %get-tuple-element.69), channel_id=1, source_target_pairs={{32,0},{64,32},{96,64},{128,96},{160,128},{192,160},{224,192},{0,2... | collective-permute-start | bytes 1105928 | tf_op jit(solution)/shard_map/ppermute | solution.py:377
  162.1 10.0 %shard_map.98 = (bf16[288,48,128]{2,1,0:T(8,128)(2,1)}, bf16[18,48,128]{2,1,0:T(8,128)(2,1)}, bf16[18,48,128]{2,1,0:T(8,128)(2,1)}) custom-call(s32[512]{0:T(512)} %reshape.45.table_ref, bf16[64,272,128]{2,1,0:T(8,128)(2,1)} %bitcast.3.refs_0_), custom_call_target="tpu_custom_call" | custom-call | tf_op jit(solution)/shard_map/pallas_call | solution.py:298
  172.1 0.1 collective-permute-start.11
  172.2 2.7 collective-permute-start.12
  174.9 0.0 collective-permute-start.2
  174.9 1.1 fusion.1
  176.0 3.1 %collective-permute-done.2 = f32[8,128]{1,0:T(8,128)S(1)} collective-permute-done((f32[8,128]{1,0:T(8,128)S(1)}, f32[8,128]{1,0:T(8,128)S(1)}, u32[]{:S(2)}, u32[]{:S(2)}) %collective-permute-start.2) | collective-permute-done | bytes 4128 | tf_op jit(solution)/shard_map/ppermute | solution.py:384
  179.2 1.5 add_convert_fusion.8
  180.7 0.2 pad_maximum_fusion
  180.8 0.3 collective-permute-start.3
  181.1 2.5 collective-permute-start.4
  183.6 0.1 add_convert_fusion.10
  183.8 0.1 pad_maximum_fusion.2
  183.9 0.4 collective-permute-start.13
  184.3 2.4 collective-permute-start.14
  186.6 0.3 collective-permute-start.5
  186.9 22.5 %collective-permute-done.5 = f32[8,128]{1,0:T(8,128)S(1)} collective-permute-done((f32[8,128]{1,0:T(8,128)S(1)}, f32[8,128]{1,0:T(8,128)S(1)}, u32[]{:S(2)}, u32[]{:S(2)}) %collective-permute-start.5) | collective-permute-done | bytes 4128 | tf_op jit(solution)/shard_map/ppermute | solution.py:384
  209.4 0.0 collective-permute-done.3
  209.4 0.0 collective-permute-done.4
  209.4 0.4 add_convert_fusion.2
  209.8 0.2 collective-permute-start.6
  210.0 2.6 collective-permute-start.7
  212.6 0.0 collective-permute-done.13
  212.6 0.0 collective-permute-done.14
  212.6 0.2 add_convert_fusion.6
  212.8 0.1 collective-permute-start.15
  212.9 2.7 collective-permute-start.16
  215.6 1.0 collective-permute-start.8
  216.6 19.4 %collective-permute-done.15 = bf16[36,48,128]{2,1,0:T(8,128)(2,1)S(1)} collective-permute-done((bf16[36,48,128]{2,1,0:T(8,128)(2,1)S(1)}, bf16[36,48,128]{2,1,0:T(8,128)(2,1)S(1)}, u32[]{:S(2)}, u32[]{:S(2)}) %collective-permute-start.15) | collective-permute-done | bytes 442400 | tf_op jit(solution)/shard_map/ppermute | solution.py:376
  236.0 0.4 add_convert_fusion
  236.4 0.1 collective-permute-start.9
  236.5 2.7 collective-permute-start.10
  239.2 0.2 add_convert_fusion.4
  239.4 0.1 collective-permute-start.17
  239.5 2.7 collective-permute-start.18
  242.2 19.4 %collective-permute-done.17.up_ref = bf16[36,48,128]{2,1,0:T(8,128)(2,1)S(1)} collective-permute-done((bf16[36,48,128]{2,1,0:T(8,128)(2,1)S(1)}, bf16[36,48,128]{2,1,0:T(8,128)(2,1)S(1)}, u32[]{:S(2)}, u32[]{:S(2)}) %collective-permute-start.17) | collective-permute-done | bytes 442400 | tf_op jit(solution)/shard_map/ppermute | solution.py:376
  261.6 0.8 copy-done.4
  262.3 0.8 copy-done.5
  263.1 3.4 %shard_map.99.refs_0_ = f32[12,128,384]{2,1,0:T(8,128)} custom-call(f32[12,128,384]{2,1,0:T(8,128)} %bitcast.17, bf16[288,48,128]{2,1,0:T(8,128)(2,1)} %get-tuple-element.91.own_ref, bf16[36,48,128]{2,1,0:T(8,128)(2,1)} %copy-done.4, bf16[36,48,128]{2,1,0:T(8,128)(2,1)} %copy-done.5), custom_call_target="tpu_custom_call" | custom-call | tf_op jit(solution)/shard_map/pallas_call | solution.py:345
  266.4 0.6 slice_bitcast_fusion
  267.0 0.9 copy-done.1
  267.9 0.9 copy-done.2
  268.8 4.7 %shard_map.100 = f32[12,128,384]{2,1,0:T(8,128)} custom-call(f32[12,128,384]{2,1,0:T(8,128)} %bitcast.18, bf16[288,80,128]{2,1,0:T(8,128)(2,1)} %get-tuple-element.64.own_ref, bf16[36,80,128]{2,1,0:T(8,128)(2,1)} %copy-done.1, bf16[36,80,128]{2,1,0:T(8,128)(2,1)} %copy-done.2, f32[12,128,384]{2,1,0:T(8,128)} %shard_map.99.refs_0_), custom_call_target="tpu_custom_call", output_to_operand_aliasing={{}: (4, {})} | custom-call | tf_op jit(solution)/shard_map/pallas_call | solution.py:345
  (33 shorter events, 0.1 us)
Async XLA Ops:
  1.5 17.9 %copy-start.7 = (s32[32]{0:T(128)}, s32[32]{0:T(128)S(1)}, u32[]{:S(2)}) copy-start(s32[32]{0:T(128)S(1)} %reshape.41.refs_0_) | copy-start | bytes 388
  2.8 15.9 %all-to-all-start = ((f32[32,4,128]{2,1,0:T(4,128)}), f32[32,4,128]{2,1,0:T(4,128)S(1)}, u32[]{:S(2)}, u32[]{:S(2)}) async-start(f32[32,4,128]{2,1,0:T(4,128)} %broadcast_in_dim.8), calls=%async_computation | async-start | bytes 131072 | tf_op jit(solution)/shard_map/all_to_all | solution.py:405
  18.8 7.5 %copy-start.3 = (f32[32,4,128]{2,1,0:T(4,128)}, f32[32,4,128]{2,1,0:T(4,128)S(1)}, u32[]{:S(2)}) copy-start(f32[32,4,128]{2,1,0:T(4,128)S(1)} %all-to-all-done.all_ref) | copy-start | bytes 196612
  26.3 60.2 %all-to-all-start.1 = ((bf16[32,2,272,128]{3,2,1,0:T(8,128)(2,1)}), bf16[32,2,272,128]{3,2,1,0:T(8,128)(2,1)}, u32[]{:S(2)}, u32[]{:S(2)}) async-start(bf16[32,2,272,128]{3,2,1,0:T(8,128)(2,1)} %bitcast.20), calls=%async_computation.1 | async-start | bytes 8912896 | tf_op jit(solution)/shard_map/all_to_all | solution.py:415
  156.3 18.6 %copy-start.6 = (f32[8,128]{1,0:T(8,128)S(1)}, f32[8,128]{1,0:T(8,128)}, u32[]{:S(2)}) copy-start(f32[8,128]{1,0:T(8,128)} %get-tuple-element.70) | copy-start | bytes 12292
  156.3 22.9 %collective-permute-start = (bf16[18,80,128]{2,1,0:T(8,128)(2,1)}, bf16[18,80,128]{2,1,0:T(8,128)(2,1)S(1)}, u32[]{:S(2)}, u32[]{:S(2)}) collective-permute-start(bf16[18,80,128]{2,1,0:T(8,128)(2,1)} %get-tuple-element.68), channel_id=1, source_target_pairs={{0,32},{32,64},{64,96},{96,128},{128,160},{160,192},{192,224},{224... | collective-permute-start | bytes 1105928 | tf_op jit(solution)/shard_map/ppermute | solution.py:376
  158.0 21.2 %collective-permute-start.1 = (bf16[18,80,128]{2,1,0:T(8,128)(2,1)}, bf16[18,80,128]{2,1,0:T(8,128)(2,1)S(1)}, u32[]{:S(2)}, u32[]{:S(2)}) collective-permute-start(bf16[18,80,128]{2,1,0:T(8,128)(2,1)} %get-tuple-element.69), channel_id=1, source_target_pairs={{32,0},{64,32},{96,64},{128,96},{160,128},{192,160},{224,192},{0,2... | collective-permute-start | bytes 1105928 | tf_op jit(solution)/shard_map/ppermute | solution.py:377
  162.0 47.4 %slice-start = ((s8[5898240]{0:T(1024)(128)(4,1)}), s8[1703936]{0:T(1024)(128)(4,1)S(1)}, s32[]{:S(2)}) async-start(s8[5898240]{0:T(1024)(128)(4,1)} %bitcast.13), calls=%async_computation.3 | async-start | bytes 3407872
  172.1 11.5 %collective-permute-start.11 = (bf16[18,48,128]{2,1,0:T(8,128)(2,1)}, bf16[18,48,128]{2,1,0:T(8,128)(2,1)S(1)}, u32[]{:S(2)}, u32[]{:S(2)}) collective-permute-start(bf16[18,48,128]{2,1,0:T(8,128)(2,1)} %get-tuple-element.94), channel_id=1, source_target_pairs={{0,32},{32,64},{64,96},{96,128},{128,160},{160,192},{192,224},{224... | collective-permute-start | bytes 663560 | tf_op jit(solution)/shard_map/ppermute | solution.py:376
  172.2 11.4 %collective-permute-start.12 = (bf16[18,48,128]{2,1,0:T(8,128)(2,1)}, bf16[18,48,128]{2,1,0:T(8,128)(2,1)S(1)}, u32[]{:S(2)}, u32[]{:S(2)}) collective-permute-start(bf16[18,48,128]{2,1,0:T(8,128)(2,1)} %get-tuple-element.95), channel_id=1, source_target_pairs={{32,0},{64,32},{96,64},{128,96},{160,128},{192,160},{224,192},{0,2... | collective-permute-start | bytes 663560 | tf_op jit(solution)/shard_map/ppermute | solution.py:377
  174.9 4.3 %collective-permute-start.2 = (f32[8,128]{1,0:T(8,128)S(1)}, f32[8,128]{1,0:T(8,128)S(1)}, u32[]{:S(2)}, u32[]{:S(2)}) collective-permute-start(f32[8,128]{1,0:T(8,128)S(1)} %copy-done.6), channel_id=1, source_target_pairs={{0,32},{32,0},{64,96},{96,64},{128,160},{160,128},{192,224},{224,1... | collective-permute-start | bytes 12296 | tf_op jit(solution)/shard_map/ppermute | solution.py:384
  179.2 4.4 %copy-start = (bf16[288,48,128]{2,1,0:T(8,128)(2,1)S(1)}, bf16[288,48,128]{2,1,0:T(8,128)(2,1)}, u32[]{:S(2)}) copy-start(bf16[288,48,128]{2,1,0:T(8,128)(2,1)} %get-tuple-element.91.own_ref) | copy-start | bytes 10616836
  179.2 30.2 %slice-start.1 = ((s8[5898240]{0:T(1024)(128)(4,1)}), s8[4194304]{0:T(1024)(128)(4,1)S(1)}, s32[]{:S(2)}) async-start(s8[5898240]{0:T(1024)(128)(4,1)} %bitcast.13), calls=%async_computation.4 | async-start | bytes 8388608
  180.8 28.6 %collective-permute-start.3 = (bf16[36,80,128]{2,1,0:T(8,128)(2,1)S(1)}, bf16[36,80,128]{2,1,0:T(8,128)(2,1)S(1)}, u32[]{:S(2)}, u32[]{:S(2)}) collective-permute-start(bf16[36,80,128]{2,1,0:T(8,128)(2,1)S(1)} %get-tuple-element.74), channel_id=1, source_target_pairs={{0,32},{32,64},{64,96},{96,128},{128,160},{160,192},{192,224},{224... | collective-permute-start | bytes 2211848 | tf_op jit(solution)/shard_map/ppermute | solution.py:376
  181.1 28.3 %collective-permute-start.4 = (bf16[36,80,128]{2,1,0:T(8,128)(2,1)S(1)}, bf16[36,80,128]{2,1,0:T(8,128)(2,1)S(1)}, u32[]{:S(2)}, u32[]{:S(2)}) collective-permute-start(bf16[36,80,128]{2,1,0:T(8,128)(2,1)S(1)} %get-tuple-element.75), channel_id=1, source_target_pairs={{32,0},{64,32},{96,64},{128,96},{160,128},{192,160},{224,192},{0,2... | collective-permute-start | bytes 2211848 | tf_op jit(solution)/shard_map/ppermute | solution.py:377
  183.9 28.7 %collective-permute-start.13 = (bf16[36,48,128]{2,1,0:T(8,128)(2,1)S(1)}, bf16[36,48,128]{2,1,0:T(8,128)(2,1)S(1)}, u32[]{:S(2)}, u32[]{:S(2)}) collective-permute-start(bf16[36,48,128]{2,1,0:T(8,128)(2,1)S(1)} %get-tuple-element.98), channel_id=1, source_target_pairs={{0,32},{32,64},{64,96},{96,128},{128,160},{160,192},{192,224},{224... | collective-permute-start | bytes 1327112 | tf_op jit(solution)/shard_map/ppermute | solution.py:376
  184.3 28.4 %collective-permute-start.14 = (bf16[36,48,128]{2,1,0:T(8,128)(2,1)S(1)}, bf16[36,48,128]{2,1,0:T(8,128)(2,1)S(1)}, u32[]{:S(2)}, u32[]{:S(2)}) collective-permute-start(bf16[36,48,128]{2,1,0:T(8,128)(2,1)S(1)} %get-tuple-element.99), channel_id=1, source_target_pairs={{32,0},{64,32},{96,64},{128,96},{160,128},{192,160},{224,192},{0,2... | collective-permute-start | bytes 1327112 | tf_op jit(solution)/shard_map/ppermute | solution.py:377
  186.6 22.8 %collective-permute-start.5 = (f32[8,128]{1,0:T(8,128)S(1)}, f32[8,128]{1,0:T(8,128)S(1)}, u32[]{:S(2)}, u32[]{:S(2)}) collective-permute-start(f32[8,128]{1,0:T(8,128)S(1)} %add.53), channel_id=1, source_target_pairs={{0,64},{32,96},{64,0},{96,32},{128,192},{160,224},{192,128},{224,1... | collective-permute-start | bytes 12296 | tf_op jit(solution)/shard_map/ppermute | solution.py:384
  209.8 26.2 %collective-permute-start.6 = (bf16[36,80,128]{2,1,0:T(8,128)(2,1)S(1)}, bf16[36,80,128]{2,1,0:T(8,128)(2,1)S(1)}, u32[]{:S(2)}, u32[]{:S(2)}) collective-permute-start(bf16[36,80,128]{2,1,0:T(8,128)(2,1)S(1)} %get-tuple-element.80), channel_id=1, source_target_pairs={{0,32},{32,64},{64,96},{96,128},{128,160},{160,192},{192,224},{224... | collective-permute-start | bytes 2211848 | tf_op jit(solution)/shard_map/ppermute | solution.py:376
  210.0 26.0 %collective-permute-start.7 = (bf16[36,80,128]{2,1,0:T(8,128)(2,1)S(1)}, bf16[36,80,128]{2,1,0:T(8,128)(2,1)S(1)}, u32[]{:S(2)}, u32[]{:S(2)}) collective-permute-start(bf16[36,80,128]{2,1,0:T(8,128)(2,1)S(1)} %get-tuple-element.81), channel_id=1, source_target_pairs={{32,0},{64,32},{96,64},{128,96},{160,128},{192,160},{224,192},{0,2... | collective-permute-start | bytes 2211848 | tf_op jit(solution)/shard_map/ppermute | solution.py:377
  212.8 23.2 %collective-permute-start.15 = (bf16[36,48,128]{2,1,0:T(8,128)(2,1)S(1)}, bf16[36,48,128]{2,1,0:T(8,128)(2,1)S(1)}, u32[]{:S(2)}, u32[]{:S(2)}) collective-permute-start(bf16[36,48,128]{2,1,0:T(8,128)(2,1)S(1)} %get-tuple-element.102), channel_id=1, source_target_pairs={{0,32},{32,64},{64,96},{96,128},{128,160},{160,192},{192,224},{224... | collective-permute-start | bytes 1327112 | tf_op jit(solution)/shard_map/ppermute | solution.py:376
  212.9 23.1 %collective-permute-start.16 = (bf16[36,48,128]{2,1,0:T(8,128)(2,1)S(1)}, bf16[36,48,128]{2,1,0:T(8,128)(2,1)S(1)}, u32[]{:S(2)}, u32[]{:S(2)}) collective-permute-start(bf16[36,48,128]{2,1,0:T(8,128)(2,1)S(1)} %get-tuple-element.103), channel_id=1, source_target_pairs={{32,0},{64,32},{96,64},{128,96},{160,128},{192,160},{224,192},{0,2... | collective-permute-start | bytes 1327112 | tf_op jit(solution)/shard_map/ppermute | solution.py:377
  215.6 20.4 %collective-permute-start.8 = (f32[8,128]{1,0:T(8,128)S(1)}, f32[8,128]{1,0:T(8,128)S(1)}, u32[]{:S(2)}, u32[]{:S(2)}) collective-permute-start(f32[8,128]{1,0:T(8,128)S(1)} %add.56), channel_id=1, source_target_pairs={{0,128},{32,160},{64,192},{96,224},{128,0},{160,32},{192,64},{224,... | collective-permute-start | bytes 12296 | tf_op jit(solution)/shard_map/ppermute | solution.py:384
  236.4 30.6 %collective-permute-start.9 = (bf16[36,80,128]{2,1,0:T(8,128)(2,1)S(1)}, bf16[36,80,128]{2,1,0:T(8,128)(2,1)S(1)}, u32[]{:S(2)}, u32[]{:S(2)}) collective-permute-start(bf16[36,80,128]{2,1,0:T(8,128)(2,1)S(1)} %get-tuple-element.86), channel_id=1, source_target_pairs={{0,32},{32,64},{64,96},{96,128},{128,160},{160,192},{192,224},{224... | collective-permute-start | bytes 2211848 | tf_op jit(solution)/shard_map/ppermute | solution.py:376
  236.5 30.5 %collective-permute-start.10 = (bf16[36,80,128]{2,1,0:T(8,128)(2,1)S(1)}, bf16[36,80,128]{2,1,0:T(8,128)(2,1)S(1)}, u32[]{:S(2)}, u32[]{:S(2)}) collective-permute-start(bf16[36,80,128]{2,1,0:T(8,128)(2,1)S(1)} %get-tuple-element.87), channel_id=1, source_target_pairs={{32,0},{64,32},{96,64},{128,96},{160,128},{192,160},{224,192},{0,2... | collective-permute-start | bytes 2211848 | tf_op jit(solution)/shard_map/ppermute | solution.py:377
  239.4 22.1 %collective-permute-start.17 = (bf16[36,48,128]{2,1,0:T(8,128)(2,1)S(1)}, bf16[36,48,128]{2,1,0:T(8,128)(2,1)S(1)}, u32[]{:S(2)}, u32[]{:S(2)}) collective-permute-start(bf16[36,48,128]{2,1,0:T(8,128)(2,1)S(1)} %get-tuple-element.106), channel_id=1, source_target_pairs={{0,32},{32,64},{64,96},{96,128},{128,160},{160,192},{192,224},{224... | collective-permute-start | bytes 1327112 | tf_op jit(solution)/shard_map/ppermute | solution.py:376
  239.5 22.1 %collective-permute-start.18 = (bf16[36,48,128]{2,1,0:T(8,128)(2,1)S(1)}, bf16[36,48,128]{2,1,0:T(8,128)(2,1)S(1)}, u32[]{:S(2)}, u32[]{:S(2)}) collective-permute-start(bf16[36,48,128]{2,1,0:T(8,128)(2,1)S(1)} %get-tuple-element.107), channel_id=1, source_target_pairs={{32,0},{64,32},{96,64},{128,96},{160,128},{192,160},{224,192},{0,2... | collective-permute-start | bytes 1327112 | tf_op jit(solution)/shard_map/ppermute | solution.py:377
  261.6 0.8 copy-start.4
  262.3 0.8 copy-start.5
  267.0 0.9 copy-start.1
  267.9 0.9 copy-start.2

commit v5 on v4

--- a/solution.py
+++ b/solution.py
@@ -12,7 +12,7 @@
 TW = 128
 SLOTS = 2
 HEAD = 16
-PARTS = (48, 80)
+PARTS = (64, 64)
 UNROLL = 8
 BATCH = 6
 ENTRY = 8
@@ -205,7 +205,7 @@
     last = chunk == len(PARTS) - 1
     main_ref = refs[0]
     side_ref = refs[0] if chunk == 0 else refs[1]
-    panel_ref, up_ref, down_ref = refs[1 if chunk == 0 else 2 :][:3]
+    panels, firsts = refs[1 if chunk == 0 else 2 :][:2], refs[1 if chunk == 0 else 2 :][2:6]
     grad_ref = refs[-4] if last else None
     acc_ref, cast_ref, sems = refs[-3:]
     group = main_ref.shape[0]
@@ -248,11 +248,14 @@
 
     @pl.when(step == pl.num_programs(0) - 1)
     def _():
-        n_arc = sems.shape[0] - 1
+        n_arc = sems.shape[0] // 2
+        far = n_arc // 2
         piece = cast_ref.shape[0] // n_arc
         half = piece // 2
+        alone = {(far, 0): 0, (far, 1): 1, (far + 1, 0): 2, (far - 1, 1): 3}
+        near = [far, far + 1, far - 1]
         copies = []
-        for n, p in enumerate([n_arc // 2] + [p for p in range(n_arc) if p != n_arc // 2]):
+        for p in near + [p for p in range(n_arc) if p not in near]:
 
             @pl.loop(0, piece // BATCH)
             def _(i):
@@ -260,16 +263,14 @@
                     at = p * piece + i * BATCH + k
                     cast_ref[at] = acc_ref[at].astype(BF16)
 
-            if n == 0:
-                moves = [
-                    (pl.ds(p * piece, half), up_ref, n_arc),
-                    (pl.ds(p * piece + half, half), down_ref, p),
-                ]
-            else:
-                rows = pl.ds(p * piece, piece)
-                moves = [(rows, panel_ref.at[rows], p)]
-            for rows, target, sem in moves:
-                copies.append(pltpu.make_async_copy(cast_ref.at[rows], target, sems.at[sem]))
+            for h in range(2):
+                rows = pl.ds(p * piece + h * half, half)
+                target = panels[h].at[pl.ds(p * half, half)]
+                if (p, h) in alone:
+                    target = firsts[alone[p, h]]
+                copies.append(
+                    pltpu.make_async_copy(cast_ref.at[rows], target, sems.at[2 * p + h])
+                )
                 copies[-1].start()
         for copy in copies:
             copy.wait()
@@ -282,10 +283,10 @@
     main_rows = got[0].shape[1] if chunk == 0 else TW
     in_specs = [pl.BlockSpec((group, main_rows, TW), lambda i, *_: (i, 0, 0))]
     args = [got[0]]
-    out_specs = [pl.BlockSpec(memory_space=pltpu.HBM)] * 3
+    out_specs = [pl.BlockSpec(memory_space=pltpu.HBM)] * 6
     half = n_tile_slots // n_arc // 2
     out_shape = [
-        jax.ShapeDtypeStruct((n, part, TW), BF16) for n in (n_tile_slots, half, half)
+        jax.ShapeDtypeStruct((n, part, TW), BF16) for n in [half * n_arc] * 2 + [half] * 4
     ]
     if chunk > 0:
         in_specs.append(
@@ -305,23 +306,24 @@
             scratch_shapes=[
                 pltpu.VMEM((n_tile_slots + 1, part, TW), F32),
                 pltpu.VMEM((n_tile_slots, part, TW), BF16),
-                pltpu.SemaphoreType.DMA((n_arc + 1,)),
+                pltpu.SemaphoreType.DMA((2 * n_arc,)),
             ],
         ),
         out_shape=out_shape,
     )(table, *args)
 
 
-def final_kernel(prior_ref, own_ref, up_ref, down_ref, *refs):
+def final_kernel(prior_ref, *refs):
     out_ref = refs[-1]
     n_row, _, width = prior_ref.shape
     per = width // TW
     half = n_row // 2
     for h in range(2):
+        own_ref, up_ref, down_ref = refs[3 * h : 3 * h + 3]
         for s in range(per):
             rows = slice(h * half, (h + 1) * half)
             cols = slice(s * TW, (s + 1) * TW)
-            tiles = slice((h * per + s) * half, (h * per + s + 1) * half)
+            tiles = slice(s * half, (s + 1) * half)
             out_ref[rows, :, cols] = (
                 prior_ref[rows, :, cols]
                 + own_ref[tiles].astype(F32)
@@ -330,18 +332,19 @@
             )
 
 
-def final(chunk, prior, panel, up, down, out):
+def final(chunk, prior, sums, out):
     begin, part = sum(PARTS[:chunk]), PARTS[chunk]
     step = 16
     n_row, _, width = prior.shape
-    per = up.shape[0]
+    per = sums[1].shape[0]
     spec = pl.BlockSpec((n_row, step, width), lambda i: (0, begin // step + i, 0))
     tiles = pl.BlockSpec((per, step, TW), lambda i: (0, i, 0))
-    args, in_specs, alias = [prior, panel, up, down], [spec] + [tiles] * 3, {}
+    args, alias = [prior, *sums], {}
+    in_specs = [spec] + [tiles] * 6
     if out is not None:
         args.append(out)
         in_specs.append(pl.BlockSpec(memory_space=pl.ANY))
-        alias = {4: 0}
+        alias = {len(args) - 1: 0}
     return pl.pallas_call(
         final_kernel,
         grid=(part // step,),
@@ -352,40 +355,40 @@
     )(*args)
 
 
-def ring(panel, up, down, grad, n_arc):
-    piece = panel.shape[0] // n_arc
-    half = piece // 2
+def ring(panels, firsts, grad, n_arc):
+    half = panels[0].shape[0] // n_arc
     far = n_arc // 2
     rising = [(i, (i + 1) % n_arc) for i in range(n_arc)]
     falling = [((i + 1) % n_arc, i) for i in range(n_arc)]
-    own = lambda p, a, b: panel[p * piece + a : p * piece + b]
     add = lambda x, y: (x.astype(F32) + y.astype(F32)).astype(BF16)
+    state = [[firsts[0], None], [None, firsts[1]]]
     for s in range(far):
-        if s == 1:
-            up = jnp.concatenate([add(own(far - 1, 0, half), up), own(far - 1, half, piece)])
-            down = jnp.concatenate(
-                [own(far + 1, 0, half), add(own(far + 1, half, piece), down)]
-            )
-        elif s > 1:
-            up = add(own(far - s, 0, piece), up)
-            down = add(own(far + s, 0, piece), down)
-        if grad is None:
-            up, down = lax.optimization_barrier((up, down))
-        else:
-            up, down, grad = lax.optimization_barrier((up, down, grad))
-        up = lax.ppermute(up, "arc", rising)
-        down = lax.ppermute(down, "arc", falling)
-        if grad is None:
-            up, down = lax.optimization_barrier((up, down))
-        else:
-            other = grad
-            if 1 << s < n_arc:
+        for h in range(2):
+            up, down = state[h]
+            own = lambda p: panels[h][p * half : (p + 1) * half]
+            if s > h:
+                up = add(own(far - s), up)
+            elif s == 1:
+                up = firsts[3]
+            if s > 1 - h:
+                down = add(own(far + s), down)
+            elif s == 1:
+                down = firsts[2]
+            paired = h == 0 and grad is not None and 1 << s < n_arc
+            extra = [grad] if paired else []
+            up, down, *extra = lax.optimization_barrier((up, down, *extra))
+            if up is not None:
+                up = lax.ppermute(up, "arc", rising)
+            if down is not None:
+                down = lax.ppermute(down, "arc", falling)
+            if paired:
                 swap = [(i, i ^ (1 << s)) for i in range(n_arc)]
-                other = lax.ppermute(grad, "arc", swap)
-            up, down, other = lax.optimization_barrier((up, down, other))
-            if 1 << s < n_arc:
-                grad = grad + other
-    return up, down, grad
+                extra = [lax.ppermute(extra[0], "arc", swap)]
+            up, down, *extra = lax.optimization_barrier((up, down, *extra))
+            if paired:
+                grad = grad + extra[0]
+            state[h] = [up, down]
+    return [panels[0], *state[0], panels[1], *state[1]], grad
 
 
 def on_device(design, observed, obs_type, owner_of, sub_of, sigma_table, solution, prior):
@@ -424,16 +427,16 @@
     (payload,) = pack(1, slots, wt, head)
     first, payload, table = lax.optimization_barrier((first, payload, table))
     got.append(first)
-    panel0, up, down = gather(0, table, got, spare, n_arc)
+    outs = gather(0, table, got, spare, n_arc)
     got.append(send(payload))
-    up0, down0, _ = ring(panel0, up, down, None, n_arc)
-    panel1, up, down, grad = gather(1, table, got, spare, n_arc)
-    up1, down1, grad = ring(panel1, up, down, grad, n_arc)
+    sums0, _ = ring(outs[:2], outs[2:6], None, n_arc)
+    *outs, grad = gather(1, table, got, spare, n_arc)
+    sums1, grad = ring(outs[:2], outs[2:6], grad, n_arc)
     gradient = grad[:per_owner].reshape(-1)
 
     prior = prior.reshape(row_tiles, TW, per_owner * TW)
-    out = final(0, prior, panel0, up0, down0, None)
-    out = final(1, prior, panel1, up1, down1, out)
+    out = final(0, prior, sums0, None)
+    out = final(1, prior, sums1, out)
     return out.reshape(row_tiles * TW, per_owner * TW), gradient
 
 

time: 277 us -> 239 us (0.86)
  blocking collectives: 57.9 us -> 0 us
  starting transfers between devices: 39.7 us -> 66.5 us
  waiting for transfers between devices: 113 us -> 99.2 us
  other arithmetic: 5.1 us -> 13.1 us
    all_to_all x1 -> x0, blocking collectives: 57.9 us -> none  [send(): g = lax.all_to_all(p, 'tile', split_axis=0, concat_axis=0, tiled=True)]
    ppermute x8 -> x14, waiting for transfers between devices: 38.8 us -> 20.4 us  [ring(): up = lax.ppermute(up, 'arc', rising)]
    ppermute x8 -> x14, starting transfers between devices: 22.2 us -> 39.4 us  [ring(): down = lax.ppermute(down, 'arc', falling)]
    ppermute x3, waiting for transfers between devices: 25.7 us -> 9.3 us  [ring(): extra = [lax.ppermute(extra[0], 'arc', swap)]]
    all_to_all x1 -> x2, waiting for transfers between devices: 45.8 us -> 59.3 us  [send(): g = lax.all_to_all(p, 'tile', split_axis=0, concat_axis=0, tiled=True)]
    all_to_all x1 -> x2, starting transfers between devices: 4.85 us -> 14.4 us  [send(): g = lax.all_to_all(p, 'tile', split_axis=0, concat_axis=0, tiled=True)]
    convert_element_type x6 -> x12, other arithmetic: 2.84 us -> 11.1 us  [ring(): add = lambda x, y: (x.astype(F32) + y.astype(F32)).astype(BF16)]
    ppermute x8 -> x14, waiting for transfers between devices: 0.02 us -> 7.61 us  [ring(): down = lax.ppermute(down, 'arc', falling)]
  transfers between devices with their start and end apart: 21 -> 34, of which waited for: 6 -> 17; matrix products, arithmetic and copies ran while one was open for 3% -> 6% of each run, Pallas kernels for 9% -> 16%
where the time goes in v5:
time: 239 us; the launch traced here: 236 us
  waiting for transfers between devices  99.2 us (42%)
  starting transfers between devices  66.5 us (28%)
  Pallas kernels  47.6 us (20%)
  other arithmetic  13.1 us (5%)
  local copies, waits for them, and re-layouts  8.73 us (4%)
    all_to_all x2, waiting for transfers between devices, send(): g = lax.all_to_all(p, 'tile', split_axis=0, concat_axis=0, tiled=True)  59.3 us
    ppermute x14, starting transfers between devices, ring(): down = lax.ppermute(down, 'arc', falling)  39.4 us
    pallas_call x2, Pallas kernels, gather(): pl.pallas_call(functools.partial(gather_kernel, chunk), grid_spec=pltpu.P...  22.1 us
    ppermute x14, waiting for transfers between devices, ring(): up = lax.ppermute(up, 'arc', rising)  20.4 us
    all_to_all x2, starting transfers between devices, send(): g = lax.all_to_all(p, 'tile', split_axis=0, concat_axis=0, tiled=True)  14.4 us
    pallas_call x2, Pallas kernels, pack(): pl.pallas_call(functools.partial(pack_kernel, chunk), grid_spec=pltpu.Pre...  12.5 us
    convert_element_type x12, other arithmetic, ring(): add = lambda x, y: (x.astype(F32) + y.astype(F32)).astype(BF16)  11.1 us
    ppermute x3, waiting for transfers between devices, ring(): extra = [lax.ppermute(extra[0], 'arc', swap)]  9.3 us
  transfers between devices with their start and end apart: 34, of which 17 were waited for; matrix products, arithmetic and copies ran while one was open for 6% of the time, Pallas kernels for 16%

profile of v5, /device:TPU:1, one launch (start us, length us, event | category | flops | bytes accessed | tf_op | source)
XLA Modules:
  0.0 236.1 jit_solution(3328172269240872644)
XLA Ops:
  0.6 0.7 multiply_add_fusion
  1.5 0.7 fusion
  2.2 0.6 broadcast_in_dim.8
  2.8 8.6 %all-to-all-start = ((f32[32,4,128]{2,1,0:T(4,128)}), f32[32,4,128]{2,1,0:T(4,128)S(1)}, u32[]{:S(2)}, u32[]{:S(2)}) async-start(f32[32,4,128]{2,1,0:T(4,128)} %broadcast_in_dim.8), calls=%async_computation | async-start | bytes 131072 | tf_op jit(solution)/shard_map/all_to_all | solution.py:408
  11.4 0.8 copy.13
  12.2 0.6 reshape.40.owner_ref
  12.8 3.4 %prepare.1 = (bf16[32,128,128]{2,1,0:T(8,128)(2,1)}, s32[64]{0:T(128)}) custom-call(s32[32]{0:T(128)} %reshape.40.owner_ref, bf16[8,128,512]{2,1,0:T(8,128)(2,1)} %design_ref.1), custom_call_target="tpu_custom_call" | custom-call | tf_op jit(solution)/shard_map/prepare/pallas_call | solution.py:45
  16.2 2.6 %all-to-all-done.all_ref = f32[32,4,128]{2,1,0:T(4,128)S(1)} async-done(((f32[32,4,128]{2,1,0:T(4,128)}), f32[32,4,128]{2,1,0:T(4,128)S(1)}, u32[]{:S(2)}, u32[]{:S(2)}) %all-to-all-start) | async-done | bytes 65568 | tf_op jit(solution)/shard_map/all_to_all | solution.py:408
  18.8 0.6 reshape.42.refs_5_
  19.4 7.0 %shard_map.95 = (bf16[32,128,128]{2,1,0:T(8,128)(2,1)}, bf16[8,16,128]{2,1,0:T(8,128)(2,1)}, bf16[64,320,128]{2,1,0:T(8,128)(2,1)}) custom-call(s32[64]{0:T(128)} %get-tuple-element.79.table_ref, s32[32]{0:T(128)} %copy-done.13, f32[8]{0:T(128)} %refs_1_.1, bf16[32,128,128]{2,1,0:T(8,128)(2,1)} %get-tuple-element.80.refs_2_, f32[8,128]{1,0:T(8,128)} %refs_3_.1, ...), custom_call_target="tpu_custom_call" | custom-call | tf_op jit(solution)/shard_map/pallas_call | solution.py:142
  26.4 4.9 %all-to-all-start.1 = ((bf16[32,2,320,128]{3,2,1,0:T(8,128)(2,1)}), bf16[32,2,320,128]{3,2,1,0:T(8,128)(2,1)}, u32[]{:S(2)}, u32[]{:S(2)}) async-start(bf16[32,2,320,128]{3,2,1,0:T(8,128)(2,1)} %bitcast.18), calls=%async_computation.1 | async-start | bytes 10485760 | tf_op jit(solution)/shard_map/all_to_all | solution.py:418
  31.3 0.6 pad_add_fusion.where_ref
  31.9 1.9 route.1
  33.8 1.4 reshape.45.table_ref
  35.2 5.5 %shard_map.96 = bf16[64,208,128]{2,1,0:T(8,128)(2,1)} custom-call(s32[64]{0:T(128)} %get-tuple-element.79.table_ref, bf16[32,128,128]{2,1,0:T(8,128)(2,1)} %get-tuple-element.82.refs_0_, bf16[8,16,128]{2,1,0:T(8,128)(2,1)} %get-tuple-element.83.refs_1_), custom_call_target="tpu_custom_call" | custom-call | tf_op jit(solution)/shard_map/pallas_call | solution.py:142
  40.7 55.1 %all-to-all-done.1 = bf16[32,2,320,128]{3,2,1,0:T(8,128)(2,1)} async-done(((bf16[32,2,320,128]{3,2,1,0:T(8,128)(2,1)}), bf16[32,2,320,128]{3,2,1,0:T(8,128)(2,1)}, u32[]{:S(2)}, u32[]{:S(2)}) %all-to-all-start.1) | async-done | bytes 5242912 | tf_op jit(solution)/shard_map/all_to_all | solution.py:418
  95.8 9.6 %all-to-all-start.2 = ((bf16[32,2,208,128]{3,2,1,0:T(8,128)(2,1)}), bf16[32,2,208,128]{3,2,1,0:T(8,128)(2,1)S(1)}, u32[]{:S(2)}, u32[]{:S(2)}) async-start(bf16[32,2,208,128]{3,2,1,0:T(8,128)(2,1)} %bitcast.14), calls=%async_computation.2 | async-start | bytes 6815744 | tf_op jit(solution)/shard_map/all_to_all | solution.py:418
  105.4 10.5 %shard_map.98 = (bf16[144,64,128]{2,1,0:T(8,128)(2,1)}, bf16[144,64,128]{2,1,0:T(8,128)(2,1)}, bf16[18,64,128]{2,1,0:T(8,128)(2,1)}, bf16[18,64,128]{2,1,0:T(8,1...) custom-call(s32[512]{0:T(512)} %reshape.45.table_ref, bf16[64,320,128]{2,1,0:T(8,128)(2,1)} %bitcast.3.refs_0_), custom_call_target="tpu_custom_call" | custom-call | tf_op jit(solution)/shard_map/pallas_call | solution.py:299
  115.9 5.7 %collective-permute-start.24 = (bf16[18,64,128]{2,1,0:T(8,128)(2,1)}, bf16[18,64,128]{2,1,0:T(8,128)(2,1)S(1)}, u32[]{:S(2)}, u32[]{:S(2)}) collective-permute-start(bf16[18,64,128]{2,1,0:T(8,128)(2,1)} %get-tuple-element.142), channel_id=1, source_target_pairs={{32,0},{64,32},{96,64},{128,96},{160,128},{192,160},{224,192},{0,2... | collective-permute-start | bytes 884744 | tf_op jit(solution)/shard_map/ppermute | solution.py:383
  121.6 6.4 %collective-permute-done.24 = bf16[18,64,128]{2,1,0:T(8,128)(2,1)S(1)} collective-permute-done((bf16[18,64,128]{2,1,0:T(8,128)(2,1)}, bf16[18,64,128]{2,1,0:T(8,128)(2,1)S(1)}, u32[]{:S(2)}, u32[]{:S(2)}) %collective-permute-start.24) | collective-permute-done | bytes 294944 | tf_op jit(solution)/shard_map/ppermute | solution.py:383
  128.0 1.0 add_convert_fusion.4
  129.2 3.4 %collective-permute-start.26 = (bf16[18,64,128]{2,1,0:T(8,128)(2,1)S(1)}, bf16[18,64,128]{2,1,0:T(8,128)(2,1)S(1)}, u32[]{:S(2)}, u32[]{:S(2)}) collective-permute-start(bf16[18,64,128]{2,1,0:T(8,128)(2,1)S(1)} %add_convert_fusion.4), channel_id=1, source_target_pairs={{32,0},{64,32},{96,64},{128,96},{160,128},{192,160},{224,192},{0,2... | collective-permute-start | bytes 884744 | tf_op jit(solution)/shard_map/ppermute | solution.py:383
  132.6 1.8 add_convert_fusion.9
  134.3 2.7 %collective-permute-start.19 = (bf16[18,64,128]{2,1,0:T(8,128)(2,1)}, bf16[18,64,128]{2,1,0:T(8,128)(2,1)}, u32[]{:S(2)}, u32[]{:S(2)}) collective-permute-start(bf16[18,64,128]{2,1,0:T(8,128)(2,1)} %get-tuple-element.129), channel_id=1, source_target_pairs={{32,0},{64,32},{96,64},{128,96},{160,128},{192,160},{224,192},{0,2... | collective-permute-start | bytes 884744 | tf_op jit(solution)/shard_map/ppermute | solution.py:383
  137.0 2.0 collective-permute-done.25
  139.0 2.1 add_convert_fusion.2
  141.1 2.7 %collective-permute-start.28 = (bf16[18,64,128]{2,1,0:T(8,128)(2,1)}, bf16[18,64,128]{2,1,0:T(8,128)(2,1)}, u32[]{:S(2)}, u32[]{:S(2)}) collective-permute-start(bf16[18,64,128]{2,1,0:T(8,128)(2,1)} %get-tuple-element.148), channel_id=1, source_target_pairs={{32,0},{64,32},{96,64},{128,96},{160,128},{192,160},{224,192},{0,2... | collective-permute-start | bytes 884744 | tf_op jit(solution)/shard_map/ppermute | solution.py:383
  143.7 4.1 %all-to-all-done.2 = bf16[32,2,208,128]{3,2,1,0:T(8,128)(2,1)S(1)} async-done(((bf16[32,2,208,128]{3,2,1,0:T(8,128)(2,1)}), bf16[32,2,208,128]{3,2,1,0:T(8,128)(2,1)S(1)}, u32[]{:S(2)}, u32[]{:S(2)}) %all-to-all-start.2) | async-done | bytes 3407904 | tf_op jit(solution)/shard_map/all_to_all | solution.py:418
  147.9 1.8 copy-done
  149.7 11.6 %shard_map.97 = (bf16[144,64,128]{2,1,0:T(8,128)(2,1)}, bf16[144,64,128]{2,1,0:T(8,128)(2,1)}, bf16[18,64,128]{2,1,0:T(8,128)(2,1)}, bf16[18,64,128]{2,1,0:T(8,1...) custom-call(s32[512]{0:T(512)} %reshape.45.table_ref, ...), custom_call_target="tpu_custom_call" | custom-call | tf_op jit(solution)/shard_map/pallas_call | solution.py:299
  161.3 5.7 %collective-permute-start.10 = (bf16[18,64,128]{2,1,0:T(8,128)(2,1)}, bf16[18,64,128]{2,1,0:T(8,128)(2,1)S(1)}, u32[]{:S(2)}, u32[]{:S(2)}) collective-permute-start(bf16[18,64,128]{2,1,0:T(8,128)(2,1)} %get-tuple-element.112), channel_id=1, source_target_pairs={{32,0},{64,32},{96,64},{128,96},{160,128},{192,160},{224,192},{0,2... | collective-permute-start | bytes 884744 | tf_op jit(solution)/shard_map/ppermute | solution.py:383
  166.9 0.3 collective-permute-start
  167.2 1.6 add_convert_fusion.7
  168.9 2.7 %collective-permute-start.21 = (bf16[18,64,128]{2,1,0:T(8,128)(2,1)S(1)}, bf16[18,64,128]{2,1,0:T(8,128)(2,1)S(1)}, u32[]{:S(2)}, u32[]{:S(2)}) collective-permute-start(bf16[18,64,128]{2,1,0:T(8,128)(2,1)S(1)} %get-tuple-element.133), channel_id=1, source_target_pairs={{32,0},{64,32},{96,64},{128,96},{160,128},{192,160},{224,192},{0,2... | collective-permute-start | bytes 884744 | tf_op jit(solution)/shard_map/ppermute | solution.py:383
  171.6 1.1 collective-permute-done.10
  172.7 1.0 add_convert_fusion.14
  173.8 0.4 collective-permute-start.11
  174.2 5.1 %collective-permute-done.1 = f32[8,128]{1,0:T(8,128)S(1)} collective-permute-done((f32[8,128]{1,0:T(8,128)}, f32[8,128]{1,0:T(8,128)S(1)}, u32[]{:S(2)}, u32[]{:S(2)}) %collective-permute-start.1) | collective-permute-done | bytes 4128 | tf_op jit(solution)/shard_map/ppermute | solution.py:386
  179.3 2.6 %collective-permute-start.12 = (bf16[18,64,128]{2,1,0:T(8,128)(2,1)S(1)}, bf16[18,64,128]{2,1,0:T(8,128)(2,1)S(1)}, u32[]{:S(2)}, u32[]{:S(2)}) collective-permute-start(bf16[18,64,128]{2,1,0:T(8,128)(2,1)S(1)} %add_convert_fusion.14), channel_id=1, source_target_pairs={{32,0},{64,32},{96,64},{128,96},{160,128},{192,160},{224,192},{0,2... | collective-permute-start | bytes 884744 | tf_op jit(solution)/shard_map/ppermute | solution.py:383
  182.3 2.5 %collective-permute-start.3 = (bf16[18,64,128]{2,1,0:T(8,128)(2,1)S(1)}, bf16[18,64,128]{2,1,0:T(8,128)(2,1)S(1)}, u32[]{:S(2)}, u32[]{:S(2)}) collective-permute-start(bf16[18,64,128]{2,1,0:T(8,128)(2,1)S(1)} %copy-done.14), channel_id=1, source_target_pairs={{32,0},{64,32},{96,64},{128,96},{160,128},{192,160},{224,192},{0,2... | collective-permute-start | bytes 884744 | tf_op jit(solution)/shard_map/ppermute | solution.py:383
  184.8 1.4 add_convert_fusion
  186.3 2.3 collective-permute-done.11
  188.9 2.7 %collective-permute-start.14 = (bf16[18,64,128]{2,1,0:T(8,128)(2,1)S(1)}, bf16[18,64,128]{2,1,0:T(8,128)(2,1)S(1)}, u32[]{:S(2)}, u32[]{:S(2)}) collective-permute-start(bf16[18,64,128]{2,1,0:T(8,128)(2,1)S(1)} %get-tuple-element.118), channel_id=1, source_target_pairs={{32,0},{64,32},{96,64},{128,96},{160,128},{192,160},{224,192},{0,2... | collective-permute-start | bytes 884744 | tf_op jit(solution)/shard_map/ppermute | solution.py:383
  191.6 1.4 collective-permute-done.4
  193.1 1.9 collective-permute-done.2
  195.3 2.7 %collective-permute-start.6 = (bf16[18,64,128]{2,1,0:T(8,128)(2,1)S(1)}, bf16[18,64,128]{2,1,0:T(8,128)(2,1)S(1)}, u32[]{:S(2)}, u32[]{:S(2)}) collective-permute-start(bf16[18,64,128]{2,1,0:T(8,128)(2,1)S(1)} %get-tuple-element.102), channel_id=1, source_target_pairs={{32,0},{64,32},{96,64},{128,96},{160,128},{192,160},{224,192},{0,2... | collective-permute-start | bytes 884744 | tf_op jit(solution)/shard_map/ppermute | solution.py:383
  197.9 1.6 collective-permute-start.7
  199.6 1.3 add_convert_fusion.5
  200.8 0.4 collective-permute-done.13
  201.3 2.7 %collective-permute-start.30 = (bf16[18,64,128]{2,1,0:T(8,128)(2,1)S(1)}, bf16[18,64,128]{2,1,0:T(8,128)(2,1)S(1)}, u32[]{:S(2)}, u32[]{:S(2)}) collective-permute-start(bf16[18,64,128]{2,1,0:T(8,128)(2,1)S(1)} %get-tuple-element.152), channel_id=1, source_target_pairs={{32,0},{64,32},{96,64},{128,96},{160,128},{192,160},{224,192},{0,2... | collective-permute-start | bytes 884744 | tf_op jit(solution)/shard_map/ppermute | solution.py:383
  204.0 2.7 %collective-permute-done.7 = f32[8,128]{1,0:T(8,128)S(1)} collective-permute-done((f32[8,128]{1,0:T(8,128)S(1)}, f32[8,128]{1,0:T(8,128)S(1)}, u32[]{:S(2)}, u32[]{:S(2)}) %collective-permute-start.7) | collective-permute-done | bytes 4128 | tf_op jit(solution)/shard_map/ppermute | solution.py:386
  206.9 2.7 %collective-permute-start.23 = (bf16[18,64,128]{2,1,0:T(8,128)(2,1)S(1)}, bf16[18,64,128]{2,1,0:T(8,128)(2,1)S(1)}, u32[]{:S(2)}, u32[]{:S(2)}) collective-permute-start(bf16[18,64,128]{2,1,0:T(8,128)(2,1)S(1)} %get-tuple-element.137), channel_id=1, source_target_pairs={{32,0},{64,32},{96,64},{128,96},{160,128},{192,160},{224,192},{0,2... | collective-permute-start | bytes 884744 | tf_op jit(solution)/shard_map/ppermute | solution.py:383
  209.9 2.6 %collective-permute-done.29.refs_4_ = bf16[18,64,128]{2,1,0:T(8,128)(2,1)S(1)} collective-permute-done((bf16[18,64,128]{2,1,0:T(8,128)(2,1)S(1)}, bf16[18,64,128]{2,1,0:T(8,128)(2,1)S(1)}, u32[]{:S(2)}, u32[]{:S(2)}) %collective-permute-start.29) | collective-permute-done | bytes 294944 | tf_op jit(solution)/shard_map/ppermute | solution.py:381
  212.7 1.3 collective-permute-start.8
  213.9 4.2 %collective-permute-done.22.refs_1_ = bf16[18,64,128]{2,1,0:T(8,128)(2,1)S(1)} collective-permute-done((bf16[18,64,128]{2,1,0:T(8,128)(2,1)S(1)}, bf16[18,64,128]{2,1,0:T(8,128)(2,1)S(1)}, u32[]{:S(2)}, u32[]{:S(2)}) %collective-permute-start.22) | collective-permute-done | bytes 294944 | tf_op jit(solution)/shard_map/ppermute | solution.py:381
  218.1 0.6 collective-permute-start.9
  218.9 0.6 copy-done.11
  219.5 3.8 %shard_map.99.refs_6_ = f32[12,128,384]{2,1,0:T(8,128)} custom-call(f32[12,128,384]{2,1,0:T(8,128)} %bitcast.15, bf16[144,64,128]{2,1,0:T(8,128)(2,1)} %get-tuple-element.125.refs_0_, bf16[18,64,128]{2,1,0:T(8,128)(2,1)} %copy-done.10, bf16[18,64,128]{2,1,0:T(8,128)(2,1)} %copy-done.11, bf16[144,64,128]{2,1,0:T(8,128)(2,1)} %get-tuple-element.140.refs_3_, ...), custom_call_target="tpu_custom_call" | custom-call | tf_op jit(solution)/shard_map/pallas_call | solution.py:348
  223.3 0.6 slice_bitcast_fusion
  223.9 0.5 collective-permute-done.15.refs_4_
  224.5 6.3 %collective-permute-done.8.refs_1_ = bf16[18,64,128]{2,1,0:T(8,128)(2,1)S(1)} collective-permute-done((bf16[18,64,128]{2,1,0:T(8,128)(2,1)S(1)}, bf16[18,64,128]{2,1,0:T(8,128)(2,1)S(1)}, u32[]{:S(2)}, u32[]{:S(2)}) %collective-permute-start.8) | collective-permute-done | bytes 294944 | tf_op jit(solution)/shard_map/ppermute | solution.py:381
  230.8 0.7 copy-done.6
  231.5 0.7 copy-done.7
  232.3 3.8 %shard_map.100 = f32[12,128,384]{2,1,0:T(8,128)} custom-call(f32[12,128,384]{2,1,0:T(8,128)} %bitcast.16, bf16[144,64,128]{2,1,0:T(8,128)(2,1)} %get-tuple-element.87.refs_0_, bf16[18,64,128]{2,1,0:T(8,128)(2,1)} %copy-done.6, bf16[18,64,128]{2,1,0:T(8,128)(2,1)} %copy-done.7, ...), custom_call_target="tpu_custom_call", output_to_operand_aliasing={{}: (7, {})} | custom-call | tf_op jit(solution)/shard_map/pallas_call | solution.py:348
  (69 shorter events, 2.2 us)
Async XLA Ops:
  1.5 17.9 %copy-start.13 = (s32[32]{0:T(128)}, s32[32]{0:T(128)S(1)}, u32[]{:S(2)}) copy-start(s32[32]{0:T(128)S(1)} %reshape.41.refs_0_) | copy-start | bytes 388
  2.8 15.9 %all-to-all-start = ((f32[32,4,128]{2,1,0:T(4,128)}), f32[32,4,128]{2,1,0:T(4,128)S(1)}, u32[]{:S(2)}, u32[]{:S(2)}) async-start(f32[32,4,128]{2,1,0:T(4,128)} %broadcast_in_dim.8), calls=%async_computation | async-start | bytes 131072 | tf_op jit(solution)/shard_map/all_to_all | solution.py:408
  18.8 7.6 %copy-start.3 = (f32[32,4,128]{2,1,0:T(4,128)}, f32[32,4,128]{2,1,0:T(4,128)S(1)}, u32[]{:S(2)}) copy-start(f32[32,4,128]{2,1,0:T(4,128)S(1)} %all-to-all-done.all_ref) | copy-start | bytes 196612
  26.4 69.4 %all-to-all-start.1 = ((bf16[32,2,320,128]{3,2,1,0:T(8,128)(2,1)}), bf16[32,2,320,128]{3,2,1,0:T(8,128)(2,1)}, u32[]{:S(2)}, u32[]{:S(2)}) async-start(bf16[32,2,320,128]{3,2,1,0:T(8,128)(2,1)} %bitcast.18), calls=%async_computation.1 | async-start | bytes 10485760 | tf_op jit(solution)/shard_map/all_to_all | solution.py:418
  95.8 52.1 %all-to-all-start.2 = ((bf16[32,2,208,128]{3,2,1,0:T(8,128)(2,1)}), bf16[32,2,208,128]{3,2,1,0:T(8,128)(2,1)S(1)}, u32[]{:S(2)}, u32[]{:S(2)}) async-start(bf16[32,2,208,128]{3,2,1,0:T(8,128)(2,1)} %bitcast.14), calls=%async_computation.2 | async-start | bytes 6815744 | tf_op jit(solution)/shard_map/all_to_all | solution.py:418
  115.9 12.1 %collective-permute-start.24 = (bf16[18,64,128]{2,1,0:T(8,128)(2,1)}, bf16[18,64,128]{2,1,0:T(8,128)(2,1)S(1)}, u32[]{:S(2)}, u32[]{:S(2)}) collective-permute-start(bf16[18,64,128]{2,1,0:T(8,128)(2,1)} %get-tuple-element.142), channel_id=1, source_target_pairs={{32,0},{64,32},{96,64},{128,96},{160,128},{192,160},{224,192},{0,2... | collective-permute-start | bytes 884744 | tf_op jit(solution)/shard_map/ppermute | solution.py:383
  121.6 11.0 %collective-permute-start.17 = (bf16[18,64,128]{2,1,0:T(8,128)(2,1)}, bf16[18,64,128]{2,1,0:T(8,128)(2,1)S(1)}, u32[]{:S(2)}, u32[]{:S(2)}) collective-permute-start(bf16[18,64,128]{2,1,0:T(8,128)(2,1)} %get-tuple-element.126), channel_id=1, source_target_pairs={{0,32},{32,64},{64,96},{96,128},{128,160},{160,192},{192,224},{224... | collective-permute-start | bytes 884744 | tf_op jit(solution)/shard_map/ppermute | solution.py:381
  129.1 9.9 %collective-permute-start.25 = (bf16[18,64,128]{2,1,0:T(8,128)(2,1)}, bf16[18,64,128]{2,1,0:T(8,128)(2,1)S(1)}, u32[]{:S(2)}, u32[]{:S(2)}) collective-permute-start(bf16[18,64,128]{2,1,0:T(8,128)(2,1)} %get-tuple-element.143), channel_id=1, source_target_pairs={{0,32},{32,64},{64,96},{96,128},{128,160},{160,192},{192,224},{224... | collective-permute-start | bytes 884744 | tf_op jit(solution)/shard_map/ppermute | solution.py:381
  129.2 9.8 %collective-permute-start.26 = (bf16[18,64,128]{2,1,0:T(8,128)(2,1)S(1)}, bf16[18,64,128]{2,1,0:T(8,128)(2,1)S(1)}, u32[]{:S(2)}, u32[]{:S(2)}) collective-permute-start(bf16[18,64,128]{2,1,0:T(8,128)(2,1)S(1)} %add_convert_fusion.4), channel_id=1, source_target_pairs={{32,0},{64,32},{96,64},{128,96},{160,128},{192,160},{224,192},{0,2... | collective-permute-start | bytes 884744 | tf_op jit(solution)/shard_map/ppermute | solution.py:383
  134.3 32.6 %collective-permute-start.18 = (bf16[18,64,128]{2,1,0:T(8,128)(2,1)}, bf16[18,64,128]{2,1,0:T(8,128)(2,1)}, u32[]{:S(2)}, u32[]{:S(2)}) collective-permute-start(bf16[18,64,128]{2,1,0:T(8,128)(2,1)} %add_convert_fusion.9), channel_id=1, source_target_pairs={{0,32},{32,64},{64,96},{96,128},{128,160},{160,192},{192,224},{224... | collective-permute-start | bytes 884744 | tf_op jit(solution)/shard_map/ppermute | solution.py:381
  134.3 32.6 %collective-permute-start.19 = (bf16[18,64,128]{2,1,0:T(8,128)(2,1)}, bf16[18,64,128]{2,1,0:T(8,128)(2,1)}, u32[]{:S(2)}, u32[]{:S(2)}) collective-permute-start(bf16[18,64,128]{2,1,0:T(8,128)(2,1)} %get-tuple-element.129), channel_id=1, source_target_pairs={{32,0},{64,32},{96,64},{128,96},{160,128},{192,160},{224,192},{0,2... | collective-permute-start | bytes 884744 | tf_op jit(solution)/shard_map/ppermute | solution.py:383
  141.1 27.8 %collective-permute-start.27 = (bf16[18,64,128]{2,1,0:T(8,128)(2,1)}, bf16[18,64,128]{2,1,0:T(8,128)(2,1)}, u32[]{:S(2)}, u32[]{:S(2)}) collective-permute-start(bf16[18,64,128]{2,1,0:T(8,128)(2,1)} %get-tuple-element.147), channel_id=1, source_target_pairs={{0,32},{32,64},{64,96},{96,128},{128,160},{160,192},{192,224},{224... | collective-permute-start | bytes 884744 | tf_op jit(solution)/shard_map/ppermute | solution.py:381
  141.1 30.5 %collective-permute-start.28 = (bf16[18,64,128]{2,1,0:T(8,128)(2,1)}, bf16[18,64,128]{2,1,0:T(8,128)(2,1)}, u32[]{:S(2)}, u32[]{:S(2)}) collective-permute-start(bf16[18,64,128]{2,1,0:T(8,128)(2,1)} %get-tuple-element.148), channel_id=1, source_target_pairs={{32,0},{64,32},{96,64},{128,96},{160,128},{192,160},{224,192},{0,2... | collective-permute-start | bytes 884744 | tf_op jit(solution)/shard_map/ppermute | solution.py:383
  147.9 1.8 copy-start
  161.2 20.7 %copy-start.1 = (bf16[144,64,128]{2,1,0:T(8,128)(2,1)S(1)}, bf16[144,64,128]{2,1,0:T(8,128)(2,1)}, u32[]{:S(2)}) copy-start(bf16[144,64,128]{2,1,0:T(8,128)(2,1)} %get-tuple-element.87.refs_0_) | copy-start | bytes 7077892
  161.3 20.8 %copy-start.12 = (f32[8,128]{1,0:T(8,128)S(1)}, f32[8,128]{1,0:T(8,128)}, u32[]{:S(2)}) copy-start(f32[8,128]{1,0:T(8,128)} %get-tuple-element.91) | copy-start | bytes 12292
  161.3 21.0 %copy-start.14 = (bf16[18,64,128]{2,1,0:T(8,128)(2,1)S(1)}, bf16[18,64,128]{2,1,0:T(8,128)(2,1)}, u32[]{:S(2)}) copy-start(bf16[18,64,128]{2,1,0:T(8,128)(2,1)} %get-tuple-element.96) | copy-start | bytes 884740
  161.3 11.4 %collective-permute-start.10 = (bf16[18,64,128]{2,1,0:T(8,128)(2,1)}, bf16[18,64,128]{2,1,0:T(8,128)(2,1)S(1)}, u32[]{:S(2)}, u32[]{:S(2)}) collective-permute-start(bf16[18,64,128]{2,1,0:T(8,128)(2,1)} %get-tuple-element.112), channel_id=1, source_target_pairs={{32,0},{64,32},{96,64},{128,96},{160,128},{192,160},{224,192},{0,2... | collective-permute-start | bytes 884744 | tf_op jit(solution)/shard_map/ppermute | solution.py:383
  166.9 21.7 %copy-start.2 = (bf16[144,64,128]{2,1,0:T(8,128)(2,1)S(1)}, bf16[144,64,128]{2,1,0:T(8,128)(2,1)}, u32[]{:S(2)}) copy-start(bf16[144,64,128]{2,1,0:T(8,128)(2,1)} %get-tuple-element.110.refs_3_) | copy-start | bytes 7077892
  166.9 15.0 %collective-permute-start = (bf16[18,64,128]{2,1,0:T(8,128)(2,1)}, bf16[18,64,128]{2,1,0:T(8,128)(2,1)S(1)}, u32[]{:S(2)}, u32[]{:S(2)}) collective-permute-start(bf16[18,64,128]{2,1,0:T(8,128)(2,1)} %get-tuple-element.90), channel_id=1, source_target_pairs={{0,32},{32,64},{64,96},{96,128},{128,160},{160,192},{192,224},{224... | collective-permute-start | bytes 884744 | tf_op jit(solution)/shard_map/ppermute | solution.py:381
  168.8 13.5 %collective-permute-start.20 = (bf16[18,64,128]{2,1,0:T(8,128)(2,1)S(1)}, bf16[18,64,128]{2,1,0:T(8,128)(2,1)S(1)}, u32[]{:S(2)}, u32[]{:S(2)}) collective-permute-start(bf16[18,64,128]{2,1,0:T(8,128)(2,1)S(1)} %get-tuple-element.132), channel_id=1, source_target_pairs={{0,32},{32,64},{64,96},{96,128},{128,160},{160,192},{192,224},{224... | collective-permute-start | bytes 884744 | tf_op jit(solution)/shard_map/ppermute | solution.py:381
  168.9 17.3 %collective-permute-start.21 = (bf16[18,64,128]{2,1,0:T(8,128)(2,1)S(1)}, bf16[18,64,128]{2,1,0:T(8,128)(2,1)S(1)}, u32[]{:S(2)}, u32[]{:S(2)}) collective-permute-start(bf16[18,64,128]{2,1,0:T(8,128)(2,1)S(1)} %get-tuple-element.133), channel_id=1, source_target_pairs={{32,0},{64,32},{96,64},{128,96},{160,128},{192,160},{224,192},{0,2... | collective-permute-start | bytes 884744 | tf_op jit(solution)/shard_map/ppermute | solution.py:383
  171.6 7.7 %collective-permute-start.1 = (f32[8,128]{1,0:T(8,128)}, f32[8,128]{1,0:T(8,128)S(1)}, u32[]{:S(2)}, u32[]{:S(2)}) collective-permute-start(f32[8,128]{1,0:T(8,128)} %get-tuple-element.91), channel_id=1, source_target_pairs={{0,32},{32,0},{64,96},{96,64},{128,160},{160,128},{192,224},{224,1... | collective-permute-start | bytes 12296 | tf_op jit(solution)/shard_map/ppermute | solution.py:386
  173.8 14.9 %collective-permute-start.11 = (bf16[18,64,128]{2,1,0:T(8,128)(2,1)}, bf16[18,64,128]{2,1,0:T(8,128)(2,1)S(1)}, u32[]{:S(2)}, u32[]{:S(2)}) collective-permute-start(bf16[18,64,128]{2,1,0:T(8,128)(2,1)} %get-tuple-element.113), channel_id=1, source_target_pairs={{0,32},{32,64},{64,96},{96,128},{128,160},{160,192},{192,224},{224... | collective-permute-start | bytes 884744 | tf_op jit(solution)/shard_map/ppermute | solution.py:381
  179.3 9.4 %collective-permute-start.12 = (bf16[18,64,128]{2,1,0:T(8,128)(2,1)S(1)}, bf16[18,64,128]{2,1,0:T(8,128)(2,1)S(1)}, u32[]{:S(2)}, u32[]{:S(2)}) collective-permute-start(bf16[18,64,128]{2,1,0:T(8,128)(2,1)S(1)} %add_convert_fusion.14), channel_id=1, source_target_pairs={{32,0},{64,32},{96,64},{128,96},{160,128},{192,160},{224,192},{0,2... | collective-permute-start | bytes 884744 | tf_op jit(solution)/shard_map/ppermute | solution.py:383
  182.0 12.9 %collective-permute-start.2 = (bf16[18,64,128]{2,1,0:T(8,128)(2,1)S(1)}, bf16[18,64,128]{2,1,0:T(8,128)(2,1)S(1)}, u32[]{:S(2)}, u32[]{:S(2)}) collective-permute-start(bf16[18,64,128]{2,1,0:T(8,128)(2,1)S(1)} %add_convert_fusion.19), channel_id=1, source_target_pairs={{0,32},{32,64},{64,96},{96,128},{128,160},{160,192},{192,224},{224... | collective-permute-start | bytes 884744 | tf_op jit(solution)/shard_map/ppermute | solution.py:381
  182.3 12.6 %collective-permute-start.3 = (bf16[18,64,128]{2,1,0:T(8,128)(2,1)S(1)}, bf16[18,64,128]{2,1,0:T(8,128)(2,1)S(1)}, u32[]{:S(2)}, u32[]{:S(2)}) collective-permute-start(bf16[18,64,128]{2,1,0:T(8,128)(2,1)S(1)} %copy-done.14), channel_id=1, source_target_pairs={{32,0},{64,32},{96,64},{128,96},{160,128},{192,160},{224,192},{0,2... | collective-permute-start | bytes 884744 | tf_op jit(solution)/shard_map/ppermute | solution.py:383
  186.2 6.8 %collective-permute-start.4 = (f32[8,128]{1,0:T(8,128)S(1)}, f32[8,128]{1,0:T(8,128)S(1)}, u32[]{:S(2)}, u32[]{:S(2)}) collective-permute-start(f32[8,128]{1,0:T(8,128)S(1)} %add.76), channel_id=1, source_target_pairs={{0,64},{32,96},{64,0},{96,32},{128,192},{160,224},{192,128},{224,1... | collective-permute-start | bytes 12296 | tf_op jit(solution)/shard_map/ppermute | solution.py:386
  188.9 12.4 %collective-permute-start.13 = (bf16[18,64,128]{2,1,0:T(8,128)(2,1)S(1)}, bf16[18,64,128]{2,1,0:T(8,128)(2,1)S(1)}, u32[]{:S(2)}, u32[]{:S(2)}) collective-permute-start(bf16[18,64,128]{2,1,0:T(8,128)(2,1)S(1)} %get-tuple-element.117), channel_id=1, source_target_pairs={{0,32},{32,64},{64,96},{96,128},{128,160},{160,192},{192,224},{224... | collective-permute-start | bytes 884744 | tf_op jit(solution)/shard_map/ppermute | solution.py:381
  188.9 12.3 %collective-permute-start.14 = (bf16[18,64,128]{2,1,0:T(8,128)(2,1)S(1)}, bf16[18,64,128]{2,1,0:T(8,128)(2,1)S(1)}, u32[]{:S(2)}, u32[]{:S(2)}) collective-permute-start(bf16[18,64,128]{2,1,0:T(8,128)(2,1)S(1)} %get-tuple-element.118), channel_id=1, source_target_pairs={{32,0},{64,32},{96,64},{128,96},{160,128},{192,160},{224,192},{0,2... | collective-permute-start | bytes 884744 | tf_op jit(solution)/shard_map/ppermute | solution.py:383
  195.2 11.7 %collective-permute-start.5 = (bf16[18,64,128]{2,1,0:T(8,128)(2,1)S(1)}, bf16[18,64,128]{2,1,0:T(8,128)(2,1)S(1)}, u32[]{:S(2)}, u32[]{:S(2)}) collective-permute-start(bf16[18,64,128]{2,1,0:T(8,128)(2,1)S(1)} %get-tuple-element.101), channel_id=1, source_target_pairs={{0,32},{32,64},{64,96},{96,128},{128,160},{160,192},{192,224},{224... | collective-permute-start | bytes 884744 | tf_op jit(solution)/shard_map/ppermute | solution.py:381
  195.3 14.4 %collective-permute-start.6 = (bf16[18,64,128]{2,1,0:T(8,128)(2,1)S(1)}, bf16[18,64,128]{2,1,0:T(8,128)(2,1)S(1)}, u32[]{:S(2)}, u32[]{:S(2)}) collective-permute-start(bf16[18,64,128]{2,1,0:T(8,128)(2,1)S(1)} %get-tuple-element.102), channel_id=1, source_target_pairs={{32,0},{64,32},{96,64},{128,96},{160,128},{192,160},{224,192},{0,2... | collective-permute-start | bytes 884744 | tf_op jit(solution)/shard_map/ppermute | solution.py:383
  197.9 8.8 %collective-permute-start.7 = (f32[8,128]{1,0:T(8,128)S(1)}, f32[8,128]{1,0:T(8,128)S(1)}, u32[]{:S(2)}, u32[]{:S(2)}) collective-permute-start(f32[8,128]{1,0:T(8,128)S(1)} %add.79), channel_id=1, source_target_pairs={{0,128},{32,160},{64,192},{96,224},{128,0},{160,32},{192,64},{224,... | collective-permute-start | bytes 12296 | tf_op jit(solution)/shard_map/ppermute | solution.py:386
  201.3 11.2 %collective-permute-start.29 = (bf16[18,64,128]{2,1,0:T(8,128)(2,1)S(1)}, bf16[18,64,128]{2,1,0:T(8,128)(2,1)S(1)}, u32[]{:S(2)}, u32[]{:S(2)}) collective-permute-start(bf16[18,64,128]{2,1,0:T(8,128)(2,1)S(1)} %get-tuple-element.151), channel_id=1, source_target_pairs={{0,32},{32,64},{64,96},{96,128},{128,160},{160,192},{192,224},{224... | collective-permute-start | bytes 884744 | tf_op jit(solution)/shard_map/ppermute | solution.py:381
  201.3 11.4 %collective-permute-start.30 = (bf16[18,64,128]{2,1,0:T(8,128)(2,1)S(1)}, bf16[18,64,128]{2,1,0:T(8,128)(2,1)S(1)}, u32[]{:S(2)}, u32[]{:S(2)}) collective-permute-start(bf16[18,64,128]{2,1,0:T(8,128)(2,1)S(1)} %get-tuple-element.152), channel_id=1, source_target_pairs={{32,0},{64,32},{96,64},{128,96},{160,128},{192,160},{224,192},{0,2... | collective-permute-start | bytes 884744 | tf_op jit(solution)/shard_map/ppermute | solution.py:383
  206.7 11.4 %collective-permute-start.22 = (bf16[18,64,128]{2,1,0:T(8,128)(2,1)S(1)}, bf16[18,64,128]{2,1,0:T(8,128)(2,1)S(1)}, u32[]{:S(2)}, u32[]{:S(2)}) collective-permute-start(bf16[18,64,128]{2,1,0:T(8,128)(2,1)S(1)} %get-tuple-element.136), channel_id=1, source_target_pairs={{0,32},{32,64},{64,96},{96,128},{128,160},{160,192},{192,224},{224... | collective-permute-start | bytes 884744 | tf_op jit(solution)/shard_map/ppermute | solution.py:381
  206.9 11.8 %collective-permute-start.23 = (bf16[18,64,128]{2,1,0:T(8,128)(2,1)S(1)}, bf16[18,64,128]{2,1,0:T(8,128)(2,1)S(1)}, u32[]{:S(2)}, u32[]{:S(2)}) collective-permute-start(bf16[18,64,128]{2,1,0:T(8,128)(2,1)S(1)} %get-tuple-element.137), channel_id=1, source_target_pairs={{32,0},{64,32},{96,64},{128,96},{160,128},{192,160},{224,192},{0,2... | collective-permute-start | bytes 884744 | tf_op jit(solution)/shard_map/ppermute | solution.py:383
  209.7 14.8 %collective-permute-start.15 = (bf16[18,64,128]{2,1,0:T(8,128)(2,1)S(1)}, bf16[18,64,128]{2,1,0:T(8,128)(2,1)S(1)}, u32[]{:S(2)}, u32[]{:S(2)}) collective-permute-start(bf16[18,64,128]{2,1,0:T(8,128)(2,1)S(1)} %get-tuple-element.121), channel_id=1, source_target_pairs={{0,32},{32,64},{64,96},{96,128},{128,160},{160,192},{192,224},{224... | collective-permute-start | bytes 884744 | tf_op jit(solution)/shard_map/ppermute | solution.py:381
  212.5 6.3 %copy-start.8 = (bf16[18,64,128]{2,1,0:T(8,128)(2,1)}, bf16[18,64,128]{2,1,0:T(8,128)(2,1)S(1)}, u32[]{:S(2)}) copy-start(bf16[18,64,128]{2,1,0:T(8,128)(2,1)S(1)} %collective-permute-done.29.refs_4_) | copy-start | bytes 884740
  212.5 12.0 %collective-permute-start.16 = (bf16[18,64,128]{2,1,0:T(8,128)(2,1)S(1)}, bf16[18,64,128]{2,1,0:T(8,128)(2,1)S(1)}, u32[]{:S(2)}, u32[]{:S(2)}) collective-permute-start(bf16[18,64,128]{2,1,0:T(8,128)(2,1)S(1)} %get-tuple-element.122), channel_id=1, source_target_pairs={{32,0},{64,32},{96,64},{128,96},{160,128},{192,160},{224,192},{0,2... | collective-permute-start | bytes 884744 | tf_op jit(solution)/shard_map/ppermute | solution.py:383
  212.7 6.1 %copy-start.9 = (bf16[18,64,128]{2,1,0:T(8,128)(2,1)}, bf16[18,64,128]{2,1,0:T(8,128)(2,1)S(1)}, u32[]{:S(2)}) copy-start(bf16[18,64,128]{2,1,0:T(8,128)(2,1)S(1)} %collective-permute-done.30.refs_5_) | copy-start | bytes 884740
  212.7 18.1 %collective-permute-start.8 = (bf16[18,64,128]{2,1,0:T(8,128)(2,1)S(1)}, bf16[18,64,128]{2,1,0:T(8,128)(2,1)S(1)}, u32[]{:S(2)}, u32[]{:S(2)}) collective-permute-start(bf16[18,64,128]{2,1,0:T(8,128)(2,1)S(1)} %get-tuple-element.106), channel_id=1, source_target_pairs={{0,32},{32,64},{64,96},{96,128},{128,160},{160,192},{192,224},{224... | collective-permute-start | bytes 884744 | tf_op jit(solution)/shard_map/ppermute | solution.py:381
  218.1 0.7 copy-start.10
  218.1 12.6 %collective-permute-start.9 = (bf16[18,64,128]{2,1,0:T(8,128)(2,1)S(1)}, bf16[18,64,128]{2,1,0:T(8,128)(2,1)S(1)}, u32[]{:S(2)}, u32[]{:S(2)}) collective-permute-start(bf16[18,64,128]{2,1,0:T(8,128)(2,1)S(1)} %get-tuple-element.107), channel_id=1, source_target_pairs={{32,0},{64,32},{96,64},{128,96},{160,128},{192,160},{224,192},{0,2... | collective-permute-start | bytes 884744 | tf_op jit(solution)/shard_map/ppermute | solution.py:383
  218.8 0.7 copy-start.11
  224.5 6.3 %copy-start.4 = (bf16[18,64,128]{2,1,0:T(8,128)(2,1)}, bf16[18,64,128]{2,1,0:T(8,128)(2,1)S(1)}, u32[]{:S(2)}) copy-start(bf16[18,64,128]{2,1,0:T(8,128)(2,1)S(1)} %collective-permute-done.15.refs_4_) | copy-start | bytes 884740
  224.5 6.3 %copy-start.5 = (bf16[18,64,128]{2,1,0:T(8,128)(2,1)}, bf16[18,64,128]{2,1,0:T(8,128)(2,1)S(1)}, u32[]{:S(2)}) copy-start(bf16[18,64,128]{2,1,0:T(8,128)(2,1)S(1)} %collective-permute-done.16.refs_5_) | copy-start | bytes 884740
  230.8 0.7 copy-start.6
  231.5 0.7 copy-start.7

commit v6 on v5

--- a/solution.py
+++ b/solution.py
@@ -61,8 +61,10 @@
     for k in range(sigma_ref.shape[0]):
         spread = jnp.where(type_ref[...] == k, sigma_ref[k], spread)
     row = lax.broadcasted_iota(jnp.int32, (8, TW), 0)
+    line = lax.broadcasted_iota(jnp.int32, (blocks, TW), 0)
+    predicted = jnp.zeros((blocks, TW), F32)
     for b in range(blocks):
-        predicted = jnp.zeros((8, TW), F32)
+        parts = []
         for l in range(4):
             s = jnp.broadcast_to(sol_ref[pl.ds(ids_ref[b * 4 + l], 1), :], (8, TW))
             hi = s.astype(BF16).astype(F32)
@@ -70,15 +72,19 @@
             low = s - hi - mid
             terms = jnp.where(row == 0, hi, jnp.where(row == 1, mid, low))
             terms = jnp.where(row < 3, terms, 0.0).astype(BF16)
-            predicted += jnp.dot(terms, dt_ref[b * 4 + l], preferred_element_type=F32)
-        predicted = jnp.sum(predicted, axis=0, keepdims=True)
-        residual = observed_ref[b : b + 1] - predicted
-        spr = spread[b : b + 1]
-        scaled = jnp.abs(residual) / spr
-        root = jnp.sqrt(HUBER / jnp.maximum(scaled, HUBER)) / spr
-        head_ref[b, 0:1, :] = (root * residual).astype(BF16)
+            parts.append(jnp.dot(terms, dt_ref[b * 4 + l], preferred_element_type=F32))
+        total = (parts[0] + parts[1]) + (parts[2] + parts[3])
+        total = jnp.sum(total, axis=0, keepdims=True)
+        predicted = jnp.where(line == b, total, predicted)
+    residual = observed_ref[...] - predicted
+    scaled = jnp.abs(residual) / spread
+    root = jnp.sqrt(HUBER / jnp.maximum(scaled, HUBER)) / spread
+    target = root * residual
+    for b in range(blocks):
+        head_ref[b, 0:1, :] = target[b : b + 1].astype(BF16)
         for l in range(4):
-            wt_ref[b * 4 + l] = (root * dt_ref[b * 4 + l].astype(F32)).astype(BF16)
+            tile = dt_ref[b * 4 + l].astype(F32)
+            wt_ref[b * 4 + l] = (root[b : b + 1] * tile).astype(BF16)
 
 
 def pack_kernel(chunk, table_ref, *refs):
@@ -122,7 +128,7 @@
 
 def pack(chunk, table, *args):
     n_slot = table.shape[0]
-    group = 8
+    group = 16
     rows = payload_rows(chunk)
     whole = lambda x: pl.BlockSpec(x.shape, lambda i, *_: (0,) * len(x.shape))
     out_specs = [pl.BlockSpec((group, rows, TW), lambda i, *_: (i, 0, 0))]
@@ -224,11 +230,14 @@
             for k in range(BATCH):
                 acc_ref[i * BATCH + k] = jnp.zeros(acc_ref.shape[1:], F32)
 
-    for g0 in range(0, group, UNROLL):
+    @pl.loop(0, group // UNROLL)
+    def _(batch):
         prods = []
-        for g in range(g0, g0 + UNROLL):
+        for u in range(UNROLL):
+            g = batch * UNROLL + u
             own = main_ref[g, 0:TW, :]
-            side = side_ref[g, top : top + skip + 3 * part, :]
+            at = g if chunk == 0 else step * group + g
+            side = side_ref[at, top : top + skip + 3 * part, :]
             diag = main_ref[g, begin : begin + part, :]
             prods.append(
                 [
@@ -237,7 +246,7 @@
                 ]
             )
         for u, (side, diag) in enumerate(prods):
-            item = (step * group + g0 + u) * ENTRY
+            item = (step * group + batch * UNROLL + u) * ENTRY
             acc_ref[table_ref[item + 1]] += diag
             for r in range(3):
                 acc_ref[table_ref[item + 2 + r]] += side[
@@ -278,7 +287,7 @@
 
 def gather(chunk, table, got, n_tile_slots, n_arc):
     part = PARTS[chunk]
-    group = 8
+    group = 16
     n_slot = got[0].shape[0]
     main_rows = got[0].shape[1] if chunk == 0 else TW
     in_specs = [pl.BlockSpec((group, main_rows, TW), lambda i, *_: (i, 0, 0))]
@@ -289,10 +298,8 @@
         jax.ShapeDtypeStruct((n, part, TW), BF16) for n in [half * n_arc] * 2 + [half] * 4
     ]
     if chunk > 0:
-        in_specs.append(
-            pl.BlockSpec((group, payload_rows(chunk), TW), lambda i, *_: (i, 0, 0))
-        )
-        args.append(got[chunk])
+        in_specs.append(pl.BlockSpec(memory_space=pltpu.VMEM))
+        args.append(pltpu.with_memory_space_constraint(got[chunk], pltpu.VMEM))
     if chunk == len(PARTS) - 1:
         out_specs.append(pl.BlockSpec((8, TW), lambda i, *_: (0, 0)))
         out_shape.append(jax.ShapeDtypeStruct((8, TW), F32))
@@ -315,9 +322,10 @@
 
 def final_kernel(prior_ref, *refs):
     out_ref = refs[-1]
-    n_row, _, width = prior_ref.shape
+    n_row, step, width = prior_ref.shape
     per = width // TW
     half = n_row // 2
+    at = pl.ds(pl.multiple_of(pl.program_id(0) * step, step), step)
     for h in range(2):
         own_ref, up_ref, down_ref = refs[3 * h : 3 * h + 3]
         for s in range(per):
@@ -327,8 +335,8 @@
             out_ref[rows, :, cols] = (
                 prior_ref[rows, :, cols]
                 + own_ref[tiles].astype(F32)
-                + up_ref[tiles].astype(F32)
-                + down_ref[tiles].astype(F32)
+                + up_ref[tiles, at, :].astype(F32)
+                + down_ref[tiles, at, :].astype(F32)
             )
 
 
@@ -339,8 +347,14 @@
     per = sums[1].shape[0]
     spec = pl.BlockSpec((n_row, step, width), lambda i: (0, begin // step + i, 0))
     tiles = pl.BlockSpec((per, step, TW), lambda i: (0, i, 0))
+    kept = pl.BlockSpec(memory_space=pltpu.VMEM)
+    if out is not None:
+        sums = [
+            x if i % 3 == 0 else pltpu.with_memory_space_constraint(x, pltpu.VMEM)
+            for i, x in enumerate(sums)
+        ]
     args, alias = [prior, *sums], {}
-    in_specs = [spec] + [tiles] * 6
+    in_specs = [spec] + [tiles, kept, kept] * 2
     if out is not None:
         args.append(out)
         in_specs.append(pl.BlockSpec(memory_space=pl.ANY))
@@ -374,20 +388,16 @@
                 down = add(own(far + s), down)
             elif s == 1:
                 down = firsts[2]
-            paired = h == 0 and grad is not None and 1 << s < n_arc
-            extra = [grad] if paired else []
-            up, down, *extra = lax.optimization_barrier((up, down, *extra))
+            up, down = lax.optimization_barrier((up, down))
             if up is not None:
                 up = lax.ppermute(up, "arc", rising)
             if down is not None:
                 down = lax.ppermute(down, "arc", falling)
-            if paired:
-                swap = [(i, i ^ (1 << s)) for i in range(n_arc)]
-                extra = [lax.ppermute(extra[0], "arc", swap)]
-            up, down, *extra = lax.optimization_barrier((up, down, *extra))
-            if paired:
-                grad = grad + extra[0]
+            up, down = lax.optimization_barrier((up, down))
             state[h] = [up, down]
+        if grad is not None and 1 << s < n_arc:
+            swap = [(i, i ^ (1 << s)) for i in range(n_arc)]
+            grad = grad + lax.ppermute(grad, "arc", swap)
     return [panels[0], *state[0], panels[1], *state[1]], grad
 
 

time: 239 us -> 234 us (0.979)
  Pallas kernels: 47.6 us -> 42.4 us
  local copies, waits for them, and re-layouts: 8.73 us -> 4.79 us
  waiting for transfers between devices: 99.2 us -> 103 us
    ppermute x14, waiting for transfers between devices: 20.4 us -> 35 us  [ring(): up = lax.ppermute(up, 'arc', rising)]
    ppermute x14, waiting for transfers between devices: 7.61 us -> 0.04 us  [ring(): down = lax.ppermute(down, 'arc', falling)]
    ppermute x3, waiting for transfers between devices: 9.3 us -> 3.85 us  [ring(): grad = grad + lax.ppermute(grad, 'arc', swap)]
    unnamed x31 -> x21, local copies, waits for them, and re-layouts: 4.74 us -> 0.8 us
    ppermute x14, starting transfers between devices: 39.4 us -> 36.2 us  [ring(): down = lax.ppermute(down, 'arc', falling)]
    pallas_call x2, Pallas kernels: 22.1 us -> 18.9 us  [gather(): pl.pallas_call(functools.partial(gather_kernel, chunk), grid_spec=pltpu.P...]
    ppermute x3, starting transfers between devices: 1.72 us -> 4.28 us  [ring(): grad = grad + lax.ppermute(grad, 'arc', swap)]
    all_to_all x2, waiting for transfers between devices: 59.3 us -> 61.6 us  [send(): g = lax.all_to_all(p, 'tile', split_axis=0, concat_axis=0, tiled=True)]
  transfers between devices with their start and end apart: 34 -> 34, of which waited for: 17 -> 14; matrix products, arithmetic and copies ran while one was open for 6% -> 6% of each run, Pallas kernels for 16% -> 14%
where the time goes in v6:
time: 234 us; the launch traced here: 232 us
  waiting for transfers between devices  103 us (44%)
  starting transfers between devices  67.7 us (29%)
  Pallas kernels  42.4 us (18%)
  other arithmetic  13 us (6%)
  local copies, waits for them, and re-layouts  4.79 us (2%)
    all_to_all x2, waiting for transfers between devices, send(): g = lax.all_to_all(p, 'tile', split_axis=0, concat_axis=0, tiled=True)  61.6 us
    ppermute x14, starting transfers between devices, ring(): down = lax.ppermute(down, 'arc', falling)  36.2 us
    ppermute x14, waiting for transfers between devices, ring(): up = lax.ppermute(up, 'arc', rising)  35 us
    pallas_call x2, Pallas kernels, gather(): pl.pallas_call(functools.partial(gather_kernel, chunk), grid_spec=pltpu.P...  18.9 us
    all_to_all x2, starting transfers between devices, send(): g = lax.all_to_all(p, 'tile', split_axis=0, concat_axis=0, tiled=True)  14.5 us
    convert_element_type x12, other arithmetic, ring(): add = lambda x, y: (x.astype(F32) + y.astype(F32)).astype(BF16)  11 us
    pallas_call x2, Pallas kernels, pack(): pl.pallas_call(functools.partial(pack_kernel, chunk), grid_spec=pltpu.Pre...  10.5 us
    all_to_all x1, starting transfers between devices, on_device(): lax.all_to_all(small, 'tile', split_axis=0, concat_axis=0, tiled=True)  8.58 us
  transfers between devices with their start and end apart: 34, of which 14 were waited for; matrix products, arithmetic and copies ran while one was open for 6% of the time, Pallas kernels for 14%

profile of v6, /device:TPU:1, one launch (start us, length us, event | category | flops | bytes accessed | tf_op | source)
XLA Modules:
  0.0 232.0 jit_solution(12948199890698652085)
XLA Ops:
  0.6 0.7 multiply_add_fusion
  1.5 0.7 fusion
  2.2 0.6 broadcast_in_dim.8
  2.8 8.6 %all-to-all-start = ((f32[32,4,128]{2,1,0:T(4,128)}), f32[32,4,128]{2,1,0:T(4,128)S(1)}, u32[]{:S(2)}, u32[]{:S(2)}) async-start(f32[32,4,128]{2,1,0:T(4,128)} %broadcast_in_dim.8), calls=%async_computation | async-start | bytes 131072 | tf_op jit(solution)/shard_map/all_to_all | solution.py:418
  11.4 0.8 copy.13
  12.2 0.6 reshape.40.owner_ref
  12.8 3.4 %prepare.1 = (bf16[32,128,128]{2,1,0:T(8,128)(2,1)}, s32[64]{0:T(128)}) custom-call(s32[32]{0:T(128)} %reshape.40.owner_ref, bf16[8,128,512]{2,1,0:T(8,128)(2,1)} %design_ref.1), custom_call_target="tpu_custom_call" | custom-call | tf_op jit(solution)/shard_map/prepare/pallas_call | solution.py:45
  16.2 2.6 %all-to-all-done.all_ref = f32[32,4,128]{2,1,0:T(4,128)S(1)} async-done(((f32[32,4,128]{2,1,0:T(4,128)}), f32[32,4,128]{2,1,0:T(4,128)S(1)}, u32[]{:S(2)}, u32[]{:S(2)}) %all-to-all-start) | async-done | bytes 65568 | tf_op jit(solution)/shard_map/all_to_all | solution.py:418
  18.8 0.6 reshape.42.refs_5_
  19.4 6.1 %shard_map.95 = (bf16[32,128,128]{2,1,0:T(8,128)(2,1)}, bf16[8,16,128]{2,1,0:T(8,128)(2,1)}, bf16[64,320,128]{2,1,0:T(8,128)(2,1)}) custom-call(s32[64]{0:T(128)} %get-tuple-element.71.table_ref, s32[32]{0:T(128)} %copy-done.8, f32[8]{0:T(128)} %refs_1_.1, bf16[32,128,128]{2,1,0:T(8,128)(2,1)} %get-tuple-element.72.refs_2_, f32[8,128]{1,0:T(8,128)} %refs_3_.1, ...), custom_call_target="tpu_custom_call" | custom-call | tf_op jit(solution)/shard_map/pallas_call | solution.py:148
  25.5 4.9 %all-to-all-start.1 = ((bf16[32,2,320,128]{3,2,1,0:T(8,128)(2,1)}), bf16[32,2,320,128]{3,2,1,0:T(8,128)(2,1)}, u32[]{:S(2)}, u32[]{:S(2)}) async-start(bf16[32,2,320,128]{3,2,1,0:T(8,128)(2,1)} %bitcast.18), calls=%async_computation.1 | async-start | bytes 10485760 | tf_op jit(solution)/shard_map/all_to_all | solution.py:428
  30.4 0.6 pad_add_fusion.where_ref
  31.0 1.9 route.1
  32.9 1.4 reshape.45.table_ref
  34.2 4.4 %shard_map.96 = bf16[64,208,128]{2,1,0:T(8,128)(2,1)} custom-call(s32[64]{0:T(128)} %get-tuple-element.71.table_ref, bf16[32,128,128]{2,1,0:T(8,128)(2,1)} %get-tuple-element.74.refs_0_, bf16[8,16,128]{2,1,0:T(8,128)(2,1)} %get-tuple-element.75.refs_1_), custom_call_target="tpu_custom_call" | custom-call | tf_op jit(solution)/shard_map/pallas_call | solution.py:148
  38.7 56.2 %all-to-all-done.1 = bf16[32,2,320,128]{3,2,1,0:T(8,128)(2,1)} async-done(((bf16[32,2,320,128]{3,2,1,0:T(8,128)(2,1)}), bf16[32,2,320,128]{3,2,1,0:T(8,128)(2,1)}, u32[]{:S(2)}, u32[]{:S(2)}) %all-to-all-start.1) | async-done | bytes 5242912 | tf_op jit(solution)/shard_map/all_to_all | solution.py:428
  94.9 9.6 %all-to-all-start.2 = ((bf16[32,2,208,128]{3,2,1,0:T(8,128)(2,1)}), bf16[32,2,208,128]{3,2,1,0:T(8,128)(2,1)S(1)}, u32[]{:S(2)}, u32[]{:S(2)}) async-start(bf16[32,2,208,128]{3,2,1,0:T(8,128)(2,1)} %bitcast.14), calls=%async_computation.2 | async-start | bytes 6815744 | tf_op jit(solution)/shard_map/all_to_all | solution.py:428
  104.5 9.2 %shard_map.98 = (bf16[144,64,128]{2,1,0:T(8,128)(2,1)}, bf16[144,64,128]{2,1,0:T(8,128)(2,1)}, bf16[18,64,128]{2,1,0:T(8,128)(2,1)}, bf16[18,64,128]{2,1,0:T(8,1...) custom-call(s32[512]{0:T(512)} %reshape.45.table_ref, bf16[64,320,128]{2,1,0:T(8,128)(2,1)} %bitcast.3.refs_0_), custom_call_target="tpu_custom_call" | custom-call | tf_op jit(solution)/shard_map/pallas_call | solution.py:306
  113.7 1.7 collective-permute-start.14
  115.4 4.0 %collective-permute-start.21 = (bf16[18,64,128]{2,1,0:T(8,128)(2,1)}, bf16[18,64,128]{2,1,0:T(8,128)(2,1)S(1)}, u32[]{:S(2)}, u32[]{:S(2)}) collective-permute-start(bf16[18,64,128]{2,1,0:T(8,128)(2,1)} %get-tuple-element.126), channel_id=1, source_target_pairs={{32,0},{64,32},{96,64},{128,96},{160,128},{192,160},{224,192},{0,2... | collective-permute-start | bytes 884744 | tf_op jit(solution)/shard_map/ppermute | solution.py:395
  119.4 7.3 %collective-permute-done.14 = bf16[18,64,128]{2,1,0:T(8,128)(2,1)S(1)} collective-permute-done((bf16[18,64,128]{2,1,0:T(8,128)(2,1)}, bf16[18,64,128]{2,1,0:T(8,128)(2,1)S(1)}, u32[]{:S(2)}, u32[]{:S(2)}) %collective-permute-start.14) | collective-permute-done | bytes 294944 | tf_op jit(solution)/shard_map/ppermute | solution.py:393
  126.7 1.0 add_convert_fusion.9
  127.8 2.7 %collective-permute-start.16 = (bf16[18,64,128]{2,1,0:T(8,128)(2,1)}, bf16[18,64,128]{2,1,0:T(8,128)(2,1)S(1)}, u32[]{:S(2)}, u32[]{:S(2)}) collective-permute-start(bf16[18,64,128]{2,1,0:T(8,128)(2,1)} %get-tuple-element.113), channel_id=1, source_target_pairs={{32,0},{64,32},{96,64},{128,96},{160,128},{192,160},{224,192},{0,2... | collective-permute-start | bytes 884744 | tf_op jit(solution)/shard_map/ppermute | solution.py:395
  130.5 1.8 add_convert_fusion.4
  132.3 2.7 %collective-permute-start.23 = (bf16[18,64,128]{2,1,0:T(8,128)(2,1)}, bf16[18,64,128]{2,1,0:T(8,128)(2,1)}, u32[]{:S(2)}, u32[]{:S(2)}) collective-permute-start(bf16[18,64,128]{2,1,0:T(8,128)(2,1)} %add_convert_fusion.4), channel_id=1, source_target_pairs={{32,0},{64,32},{96,64},{128,96},{160,128},{192,160},{224,192},{0,2... | collective-permute-start | bytes 884744 | tf_op jit(solution)/shard_map/ppermute | solution.py:395
  134.9 1.8 collective-permute-done.15
  136.8 2.1 add_convert_fusion.7
  138.8 2.7 %collective-permute-start.18 = (bf16[18,64,128]{2,1,0:T(8,128)(2,1)}, bf16[18,64,128]{2,1,0:T(8,128)(2,1)}, u32[]{:S(2)}, u32[]{:S(2)}) collective-permute-start(bf16[18,64,128]{2,1,0:T(8,128)(2,1)} %get-tuple-element.117), channel_id=1, source_target_pairs={{32,0},{64,32},{96,64},{128,96},{160,128},{192,160},{224,192},{0,2... | collective-permute-start | bytes 884744 | tf_op jit(solution)/shard_map/ppermute | solution.py:395
  141.5 5.4 %all-to-all-done.2 = bf16[32,2,208,128]{3,2,1,0:T(8,128)(2,1)S(1)} async-done(((bf16[32,2,208,128]{3,2,1,0:T(8,128)(2,1)}), bf16[32,2,208,128]{3,2,1,0:T(8,128)(2,1)S(1)}, u32[]{:S(2)}, u32[]{:S(2)}) %all-to-all-start.2) | async-done | bytes 3407904 | tf_op jit(solution)/shard_map/all_to_all | solution.py:428
  147.0 9.8 %shard_map.97 = (bf16[144,64,128]{2,1,0:T(8,128)(2,1)}, bf16[144,64,128]{2,1,0:T(8,128)(2,1)}, bf16[18,64,128]{2,1,0:T(8,128)(2,1)}, bf16[18,64,128]{2,1,0:T(8,1...) custom-call(s32[512]{0:T(512)} %reshape.45.table_ref, ...), custom_call_target="tpu_custom_call" | custom-call | tf_op jit(solution)/shard_map/pallas_call | solution.py:306
  156.7 1.7 collective-permute-start
  158.5 4.2 %collective-permute-start.7 = (bf16[18,64,128]{2,1,0:T(8,128)(2,1)}, bf16[18,64,128]{2,1,0:T(8,128)(2,1)S(1)}, u32[]{:S(2)}, u32[]{:S(2)}) collective-permute-start(bf16[18,64,128]{2,1,0:T(8,128)(2,1)} %get-tuple-element.96), channel_id=1, source_target_pairs={{32,0},{64,32},{96,64},{128,96},{160,128},{192,160},{224,192},{0,2... | collective-permute-start | bytes 884744 | tf_op jit(solution)/shard_map/ppermute | solution.py:395
  162.7 1.4 add_convert_fusion.2
  164.2 2.7 %collective-permute-start.25 = (bf16[18,64,128]{2,1,0:T(8,128)(2,1)S(1)}, bf16[18,64,128]{2,1,0:T(8,128)(2,1)S(1)}, u32[]{:S(2)}, u32[]{:S(2)}) collective-permute-start(bf16[18,64,128]{2,1,0:T(8,128)(2,1)S(1)} %get-tuple-element.132), channel_id=1, source_target_pairs={{32,0},{64,32},{96,64},{128,96},{160,128},{192,160},{224,192},{0,2... | collective-permute-start | bytes 884744 | tf_op jit(solution)/shard_map/ppermute | solution.py:395
  166.9 2.2 collective-permute-done
  169.1 1.0 add_convert_fusion.19
  170.2 2.7 %collective-permute-start.2 = (bf16[18,64,128]{2,1,0:T(8,128)(2,1)}, bf16[18,64,128]{2,1,0:T(8,128)(2,1)S(1)}, u32[]{:S(2)}, u32[]{:S(2)}) collective-permute-start(bf16[18,64,128]{2,1,0:T(8,128)(2,1)} %get-tuple-element.83), channel_id=1, source_target_pairs={{32,0},{64,32},{96,64},{128,96},{160,128},{192,160},{224,192},{0,2... | collective-permute-start | bytes 884744 | tf_op jit(solution)/shard_map/ppermute | solution.py:395
  173.1 2.3 collective-permute-done.24
  175.4 1.2 collective-permute-start.9
  176.6 1.4 add_convert_fusion.5
  178.0 0.4 collective-permute-start.28
  178.4 3.3 %collective-permute-done.1 = bf16[18,64,128]{2,1,0:T(8,128)(2,1)S(1)} collective-permute-done((bf16[18,64,128]{2,1,0:T(8,128)(2,1)S(1)}, bf16[18,64,128]{2,1,0:T(8,128)(2,1)S(1)}, u32[]{:S(2)}, u32[]{:S(2)}) %collective-permute-start.1) | collective-permute-done | bytes 294944 | tf_op jit(solution)/shard_map/ppermute | solution.py:393
  181.7 0.2 add_convert_fusion.17
  182.0 2.8 %collective-permute-start.4 = (bf16[18,64,128]{2,1,0:T(8,128)(2,1)S(1)}, bf16[18,64,128]{2,1,0:T(8,128)(2,1)S(1)}, u32[]{:S(2)}, u32[]{:S(2)}) collective-permute-start(bf16[18,64,128]{2,1,0:T(8,128)(2,1)S(1)} %get-tuple-element.87), channel_id=1, source_target_pairs={{32,0},{64,32},{96,64},{128,96},{160,128},{192,160},{224,192},{0,2... | collective-permute-start | bytes 884744 | tf_op jit(solution)/shard_map/ppermute | solution.py:395
  184.8 3.2 %collective-permute-done.8 = bf16[18,64,128]{2,1,0:T(8,128)(2,1)S(1)} collective-permute-done((bf16[18,64,128]{2,1,0:T(8,128)(2,1)S(1)}, bf16[18,64,128]{2,1,0:T(8,128)(2,1)S(1)}, u32[]{:S(2)}, u32[]{:S(2)}) %collective-permute-start.8) | collective-permute-done | bytes 294944 | tf_op jit(solution)/shard_map/ppermute | solution.py:393
  188.0 0.2 add_convert_fusion.12
  188.3 2.8 %collective-permute-start.11 = (bf16[18,64,128]{2,1,0:T(8,128)(2,1)S(1)}, bf16[18,64,128]{2,1,0:T(8,128)(2,1)S(1)}, u32[]{:S(2)}, u32[]{:S(2)}) collective-permute-start(bf16[18,64,128]{2,1,0:T(8,128)(2,1)S(1)} %get-tuple-element.102), channel_id=1, source_target_pairs={{32,0},{64,32},{96,64},{128,96},{160,128},{192,160},{224,192},{0,2... | collective-permute-start | bytes 884744 | tf_op jit(solution)/shard_map/ppermute | solution.py:395
  191.1 1.3 add_convert_fusion
  192.5 1.9 collective-permute-done.3
  194.3 1.3 collective-permute-start.20
  195.6 0.2 collective-permute-start.26
  195.8 0.2 add_convert_fusion.15
  196.0 4.6 %collective-permute-done.10 = bf16[18,64,128]{2,1,0:T(8,128)(2,1)S(1)} collective-permute-done((bf16[18,64,128]{2,1,0:T(8,128)(2,1)S(1)}, bf16[18,64,128]{2,1,0:T(8,128)(2,1)S(1)}, u32[]{:S(2)}, u32[]{:S(2)}) %collective-permute-start.10) | collective-permute-done | bytes 294944 | tf_op jit(solution)/shard_map/ppermute | solution.py:393
  200.7 1.3 collective-permute-start.27
  202.0 0.2 add_convert_fusion.10
  202.2 4.8 %collective-permute-done.19.refs_1_ = bf16[18,64,128]{2,1,0:T(8,128)(2,1)S(1)} collective-permute-done((bf16[18,64,128]{2,1,0:T(8,128)(2,1)S(1)}, bf16[18,64,128]{2,1,0:T(8,128)(2,1)S(1)}, u32[]{:S(2)}, u32[]{:S(2)}) %collective-permute-start.19) | collective-permute-done | bytes 294944 | tf_op jit(solution)/shard_map/ppermute | solution.py:393
  207.0 2.7 %collective-permute-start.6 = (bf16[18,64,128]{2,1,0:T(8,128)(2,1)S(1)}, bf16[18,64,128]{2,1,0:T(8,128)(2,1)S(1)}, u32[]{:S(2)}, u32[]{:S(2)}) collective-permute-start(bf16[18,64,128]{2,1,0:T(8,128)(2,1)S(1)} %get-tuple-element.91), channel_id=1, source_target_pairs={{32,0},{64,32},{96,64},{128,96},{160,128},{192,160},{224,192},{0,2... | collective-permute-start | bytes 884744 | tf_op jit(solution)/shard_map/ppermute | solution.py:395
  209.7 3.6 %collective-permute-done.26.refs_4_ = bf16[18,64,128]{2,1,0:T(8,128)(2,1)S(1)} collective-permute-done((bf16[18,64,128]{2,1,0:T(8,128)(2,1)S(1)}, bf16[18,64,128]{2,1,0:T(8,128)(2,1)S(1)}, u32[]{:S(2)}, u32[]{:S(2)}) %collective-permute-start.26) | collective-permute-done | bytes 294944 | tf_op jit(solution)/shard_map/ppermute | solution.py:393
  213.3 2.7 %collective-permute-start.13 = (bf16[18,64,128]{2,1,0:T(8,128)(2,1)S(1)}, bf16[18,64,128]{2,1,0:T(8,128)(2,1)S(1)}, u32[]{:S(2)}, u32[]{:S(2)}) collective-permute-start(bf16[18,64,128]{2,1,0:T(8,128)(2,1)S(1)} %get-tuple-element.106), channel_id=1, source_target_pairs={{32,0},{64,32},{96,64},{128,96},{160,128},{192,160},{224,192},{0,2... | collective-permute-start | bytes 884744 | tf_op jit(solution)/shard_map/ppermute | solution.py:395
  216.0 3.8 %collective-permute-start.30 = (f32[8,128]{1,0:T(8,128)S(1)}, f32[8,128]{1,0:T(8,128)S(1)}, u32[]{:S(2)}, u32[]{:S(2)}) collective-permute-start(f32[8,128]{1,0:T(8,128)S(1)} %add.96), channel_id=1, source_target_pairs={{0,128},{32,160},{64,192},{96,224},{128,0},{160,32},{192,64},{224,... | collective-permute-start | bytes 12296 | tf_op jit(solution)/shard_map/ppermute | solution.py:400
  219.9 4.0 %shard_map.99.refs_6_ = f32[12,128,384]{2,1,0:T(8,128)} custom-call(f32[12,128,384]{2,1,0:T(8,128)} %bitcast.15, bf16[144,64,128]{2,1,0:T(8,128)(2,1)} %get-tuple-element.109.refs_0_, bf16[18,64,128]{2,1,0:T(8,128)(2,1)} %copy-done.3, bf16[18,64,128]{2,1,0:T(8,128)(2,1)} %copy-done.4, bf16[144,64,128]{2,1,0:T(8,128)(2,1)} %get-tuple-element.124.refs_3_, ...), custom_call_target="tpu_custom_call" | custom-call | tf_op jit(solution)/shard_map/pallas_call | solution.py:362
  223.9 3.8 %collective-permute-done.30 = f32[8,128]{1,0:T(8,128)S(1)} collective-permute-done((f32[8,128]{1,0:T(8,128)S(1)}, f32[8,128]{1,0:T(8,128)S(1)}, u32[]{:S(2)}, u32[]{:S(2)}) %collective-permute-start.30) | collective-permute-done | bytes 4128 | tf_op jit(solution)/shard_map/ppermute | solution.py:400
  227.7 0.6 slice_bitcast_fusion
  228.3 3.6 %shard_map.100 = f32[12,128,384]{2,1,0:T(8,128)} custom-call(f32[12,128,384]{2,1,0:T(8,128)} %bitcast.16, bf16[144,64,128]{2,1,0:T(8,128)(2,1)} %get-tuple-element.79.refs_0_, bf16[18,64,128]{2,1,0:T(8,128)(2,1)S(1)} %collective-permute-done.5.refs_1_, bf16[18,64,128]{2,1,0:T(8,128)(2,1)S(1)} %collective-permute-done.6.refs_2_, ...), custom_call_target="tpu_custom_call", output_to_operand_aliasing={{}: (7, {})} | custom-call | tf_op jit(solution)/shard_map/pallas_call | solution.py:362
  (59 shorter events, 1.0 us)
Async XLA Ops:
  1.5 17.9 %copy-start.8 = (s32[32]{0:T(128)}, s32[32]{0:T(128)S(1)}, u32[]{:S(2)}) copy-start(s32[32]{0:T(128)S(1)} %reshape.41.refs_0_) | copy-start | bytes 388
  2.8 15.9 %all-to-all-start = ((f32[32,4,128]{2,1,0:T(4,128)}), f32[32,4,128]{2,1,0:T(4,128)S(1)}, u32[]{:S(2)}, u32[]{:S(2)}) async-start(f32[32,4,128]{2,1,0:T(4,128)} %broadcast_in_dim.8), calls=%async_computation | async-start | bytes 131072 | tf_op jit(solution)/shard_map/all_to_all | solution.py:418
  18.8 6.7 %copy-start.2 = (f32[32,4,128]{2,1,0:T(4,128)}, f32[32,4,128]{2,1,0:T(4,128)S(1)}, u32[]{:S(2)}) copy-start(f32[32,4,128]{2,1,0:T(4,128)S(1)} %all-to-all-done.all_ref) | copy-start | bytes 196612
  25.5 69.4 %all-to-all-start.1 = ((bf16[32,2,320,128]{3,2,1,0:T(8,128)(2,1)}), bf16[32,2,320,128]{3,2,1,0:T(8,128)(2,1)}, u32[]{:S(2)}, u32[]{:S(2)}) async-start(bf16[32,2,320,128]{3,2,1,0:T(8,128)(2,1)} %bitcast.18), calls=%async_computation.1 | async-start | bytes 10485760 | tf_op jit(solution)/shard_map/all_to_all | solution.py:428
  94.9 52.1 %all-to-all-start.2 = ((bf16[32,2,208,128]{3,2,1,0:T(8,128)(2,1)}), bf16[32,2,208,128]{3,2,1,0:T(8,128)(2,1)S(1)}, u32[]{:S(2)}, u32[]{:S(2)}) async-start(bf16[32,2,208,128]{3,2,1,0:T(8,128)(2,1)} %bitcast.14), calls=%async_computation.2 | async-start | bytes 6815744 | tf_op jit(solution)/shard_map/all_to_all | solution.py:428
  113.7 13.0 %collective-permute-start.14 = (bf16[18,64,128]{2,1,0:T(8,128)(2,1)}, bf16[18,64,128]{2,1,0:T(8,128)(2,1)S(1)}, u32[]{:S(2)}, u32[]{:S(2)}) collective-permute-start(bf16[18,64,128]{2,1,0:T(8,128)(2,1)} %get-tuple-element.110), channel_id=1, source_target_pairs={{0,32},{32,64},{64,96},{96,128},{128,160},{160,192},{192,224},{224... | collective-permute-start | bytes 884744 | tf_op jit(solution)/shard_map/ppermute | solution.py:393
  115.4 15.1 %collective-permute-start.21 = (bf16[18,64,128]{2,1,0:T(8,128)(2,1)}, bf16[18,64,128]{2,1,0:T(8,128)(2,1)S(1)}, u32[]{:S(2)}, u32[]{:S(2)}) collective-permute-start(bf16[18,64,128]{2,1,0:T(8,128)(2,1)} %get-tuple-element.126), channel_id=1, source_target_pairs={{32,0},{64,32},{96,64},{128,96},{160,128},{192,160},{224,192},{0,2... | collective-permute-start | bytes 884744 | tf_op jit(solution)/shard_map/ppermute | solution.py:395
  127.7 9.0 %collective-permute-start.15 = (bf16[18,64,128]{2,1,0:T(8,128)(2,1)S(1)}, bf16[18,64,128]{2,1,0:T(8,128)(2,1)S(1)}, u32[]{:S(2)}, u32[]{:S(2)}) collective-permute-start(bf16[18,64,128]{2,1,0:T(8,128)(2,1)S(1)} %add_convert_fusion.9), channel_id=1, source_target_pairs={{0,32},{32,64},{64,96},{96,128},{128,160},{160,192},{192,224},{224... | collective-permute-start | bytes 884744 | tf_op jit(solution)/shard_map/ppermute | solution.py:393
  127.8 9.0 %collective-permute-start.16 = (bf16[18,64,128]{2,1,0:T(8,128)(2,1)}, bf16[18,64,128]{2,1,0:T(8,128)(2,1)S(1)}, u32[]{:S(2)}, u32[]{:S(2)}) collective-permute-start(bf16[18,64,128]{2,1,0:T(8,128)(2,1)} %get-tuple-element.113), channel_id=1, source_target_pairs={{32,0},{64,32},{96,64},{128,96},{160,128},{192,160},{224,192},{0,2... | collective-permute-start | bytes 884744 | tf_op jit(solution)/shard_map/ppermute | solution.py:395
  132.3 26.2 %collective-permute-start.22 = (bf16[18,64,128]{2,1,0:T(8,128)(2,1)}, bf16[18,64,128]{2,1,0:T(8,128)(2,1)}, u32[]{:S(2)}, u32[]{:S(2)}) collective-permute-start(bf16[18,64,128]{2,1,0:T(8,128)(2,1)} %get-tuple-element.127), channel_id=1, source_target_pairs={{0,32},{32,64},{64,96},{96,128},{128,160},{160,192},{192,224},{224... | collective-permute-start | bytes 884744 | tf_op jit(solution)/shard_map/ppermute | solution.py:393
  132.3 26.2 %collective-permute-start.23 = (bf16[18,64,128]{2,1,0:T(8,128)(2,1)}, bf16[18,64,128]{2,1,0:T(8,128)(2,1)}, u32[]{:S(2)}, u32[]{:S(2)}) collective-permute-start(bf16[18,64,128]{2,1,0:T(8,128)(2,1)} %add_convert_fusion.4), channel_id=1, source_target_pairs={{32,0},{64,32},{96,64},{128,96},{160,128},{192,160},{224,192},{0,2... | collective-permute-start | bytes 884744 | tf_op jit(solution)/shard_map/ppermute | solution.py:395
  138.8 25.4 %collective-permute-start.17 = (bf16[18,64,128]{2,1,0:T(8,128)(2,1)}, bf16[18,64,128]{2,1,0:T(8,128)(2,1)}, u32[]{:S(2)}, u32[]{:S(2)}) collective-permute-start(bf16[18,64,128]{2,1,0:T(8,128)(2,1)} %get-tuple-element.116), channel_id=1, source_target_pairs={{0,32},{32,64},{64,96},{96,128},{128,160},{160,192},{192,224},{224... | collective-permute-start | bytes 884744 | tf_op jit(solution)/shard_map/ppermute | solution.py:393
  138.8 28.0 %collective-permute-start.18 = (bf16[18,64,128]{2,1,0:T(8,128)(2,1)}, bf16[18,64,128]{2,1,0:T(8,128)(2,1)}, u32[]{:S(2)}, u32[]{:S(2)}) collective-permute-start(bf16[18,64,128]{2,1,0:T(8,128)(2,1)} %get-tuple-element.117), channel_id=1, source_target_pairs={{32,0},{64,32},{96,64},{128,96},{160,128},{192,160},{224,192},{0,2... | collective-permute-start | bytes 884744 | tf_op jit(solution)/shard_map/ppermute | solution.py:395
  156.7 16.2 %copy-start.1 = (bf16[144,64,128]{2,1,0:T(8,128)(2,1)S(1)}, bf16[144,64,128]{2,1,0:T(8,128)(2,1)}, u32[]{:S(2)}) copy-start(bf16[144,64,128]{2,1,0:T(8,128)(2,1)} %get-tuple-element.94.refs_3_) | copy-start | bytes 7077892
  156.7 16.2 %copy-start.9 = (bf16[18,64,128]{2,1,0:T(8,128)(2,1)S(1)}, bf16[18,64,128]{2,1,0:T(8,128)(2,1)}, u32[]{:S(2)}) copy-start(bf16[18,64,128]{2,1,0:T(8,128)(2,1)} %get-tuple-element.97) | copy-start | bytes 884740
  156.7 12.3 %collective-permute-start = (bf16[18,64,128]{2,1,0:T(8,128)(2,1)}, bf16[18,64,128]{2,1,0:T(8,128)(2,1)S(1)}, u32[]{:S(2)}, u32[]{:S(2)}) collective-permute-start(bf16[18,64,128]{2,1,0:T(8,128)(2,1)} %get-tuple-element.80), channel_id=1, source_target_pairs={{0,32},{32,64},{64,96},{96,128},{128,160},{160,192},{192,224},{224... | collective-permute-start | bytes 884744 | tf_op jit(solution)/shard_map/ppermute | solution.py:393
  158.5 19.6 %copy-start.7 = (f32[8,128]{1,0:T(8,128)S(1)}, f32[8,128]{1,0:T(8,128)}, u32[]{:S(2)}) copy-start(f32[8,128]{1,0:T(8,128)} %get-tuple-element.139) | copy-start | bytes 12292
  158.5 23.2 %copy-start = (bf16[144,64,128]{2,1,0:T(8,128)(2,1)S(1)}, bf16[144,64,128]{2,1,0:T(8,128)(2,1)}, u32[]{:S(2)}) copy-start(bf16[144,64,128]{2,1,0:T(8,128)(2,1)} %get-tuple-element.79.refs_0_) | copy-start | bytes 7077892
  158.5 14.4 %collective-permute-start.7 = (bf16[18,64,128]{2,1,0:T(8,128)(2,1)}, bf16[18,64,128]{2,1,0:T(8,128)(2,1)S(1)}, u32[]{:S(2)}, u32[]{:S(2)}) collective-permute-start(bf16[18,64,128]{2,1,0:T(8,128)(2,1)} %get-tuple-element.96), channel_id=1, source_target_pairs={{32,0},{64,32},{96,64},{128,96},{160,128},{192,160},{224,192},{0,2... | collective-permute-start | bytes 884744 | tf_op jit(solution)/shard_map/ppermute | solution.py:395
  164.1 11.3 %collective-permute-start.24 = (bf16[18,64,128]{2,1,0:T(8,128)(2,1)S(1)}, bf16[18,64,128]{2,1,0:T(8,128)(2,1)S(1)}, u32[]{:S(2)}, u32[]{:S(2)}) collective-permute-start(bf16[18,64,128]{2,1,0:T(8,128)(2,1)S(1)} %get-tuple-element.131), channel_id=1, source_target_pairs={{0,32},{32,64},{64,96},{96,128},{128,160},{160,192},{192,224},{224... | collective-permute-start | bytes 884744 | tf_op jit(solution)/shard_map/ppermute | solution.py:393
  164.2 13.8 %collective-permute-start.25 = (bf16[18,64,128]{2,1,0:T(8,128)(2,1)S(1)}, bf16[18,64,128]{2,1,0:T(8,128)(2,1)S(1)}, u32[]{:S(2)}, u32[]{:S(2)}) collective-permute-start(bf16[18,64,128]{2,1,0:T(8,128)(2,1)S(1)} %get-tuple-element.132), channel_id=1, source_target_pairs={{32,0},{64,32},{96,64},{128,96},{160,128},{192,160},{224,192},{0,2... | collective-permute-start | bytes 884744 | tf_op jit(solution)/shard_map/ppermute | solution.py:395
  170.1 11.6 %collective-permute-start.1 = (bf16[18,64,128]{2,1,0:T(8,128)(2,1)S(1)}, bf16[18,64,128]{2,1,0:T(8,128)(2,1)S(1)}, u32[]{:S(2)}, u32[]{:S(2)}) collective-permute-start(bf16[18,64,128]{2,1,0:T(8,128)(2,1)S(1)} %add_convert_fusion.19), channel_id=1, source_target_pairs={{0,32},{32,64},{64,96},{96,128},{128,160},{160,192},{192,224},{224... | collective-permute-start | bytes 884744 | tf_op jit(solution)/shard_map/ppermute | solution.py:393
  170.2 11.5 %collective-permute-start.2 = (bf16[18,64,128]{2,1,0:T(8,128)(2,1)}, bf16[18,64,128]{2,1,0:T(8,128)(2,1)S(1)}, u32[]{:S(2)}, u32[]{:S(2)}) collective-permute-start(bf16[18,64,128]{2,1,0:T(8,128)(2,1)} %get-tuple-element.83), channel_id=1, source_target_pairs={{32,0},{64,32},{96,64},{128,96},{160,128},{192,160},{224,192},{0,2... | collective-permute-start | bytes 884744 | tf_op jit(solution)/shard_map/ppermute | solution.py:395
  173.0 15.0 %collective-permute-start.8 = (bf16[18,64,128]{2,1,0:T(8,128)(2,1)S(1)}, bf16[18,64,128]{2,1,0:T(8,128)(2,1)S(1)}, u32[]{:S(2)}, u32[]{:S(2)}) collective-permute-start(bf16[18,64,128]{2,1,0:T(8,128)(2,1)S(1)} %copy-done.9), channel_id=1, source_target_pairs={{0,32},{32,64},{64,96},{96,128},{128,160},{160,192},{192,224},{224... | collective-permute-start | bytes 884744 | tf_op jit(solution)/shard_map/ppermute | solution.py:393
  175.4 12.6 %collective-permute-start.9 = (bf16[18,64,128]{2,1,0:T(8,128)(2,1)S(1)}, bf16[18,64,128]{2,1,0:T(8,128)(2,1)S(1)}, u32[]{:S(2)}, u32[]{:S(2)}) collective-permute-start(bf16[18,64,128]{2,1,0:T(8,128)(2,1)S(1)} %add_convert_fusion.14), channel_id=1, source_target_pairs={{32,0},{64,32},{96,64},{128,96},{160,128},{192,160},{224,192},{0,2... | collective-permute-start | bytes 884744 | tf_op jit(solution)/shard_map/ppermute | solution.py:395
  178.0 14.3 %collective-permute-start.28 = (f32[8,128]{1,0:T(8,128)S(1)}, f32[8,128]{1,0:T(8,128)S(1)}, u32[]{:S(2)}, u32[]{:S(2)}) collective-permute-start(f32[8,128]{1,0:T(8,128)S(1)} %copy-done.7), channel_id=1, source_target_pairs={{0,32},{32,0},{64,96},{96,64},{128,160},{160,128},{192,224},{224,1... | collective-permute-start | bytes 12296 | tf_op jit(solution)/shard_map/ppermute | solution.py:400
  181.9 12.4 %collective-permute-start.3 = (bf16[18,64,128]{2,1,0:T(8,128)(2,1)S(1)}, bf16[18,64,128]{2,1,0:T(8,128)(2,1)S(1)}, u32[]{:S(2)}, u32[]{:S(2)}) collective-permute-start(bf16[18,64,128]{2,1,0:T(8,128)(2,1)S(1)} %get-tuple-element.86), channel_id=1, source_target_pairs={{0,32},{32,64},{64,96},{96,128},{128,160},{160,192},{192,224},{224... | collective-permute-start | bytes 884744 | tf_op jit(solution)/shard_map/ppermute | solution.py:393
  182.0 13.6 %collective-permute-start.4 = (bf16[18,64,128]{2,1,0:T(8,128)(2,1)S(1)}, bf16[18,64,128]{2,1,0:T(8,128)(2,1)S(1)}, u32[]{:S(2)}, u32[]{:S(2)}) collective-permute-start(bf16[18,64,128]{2,1,0:T(8,128)(2,1)S(1)} %get-tuple-element.87), channel_id=1, source_target_pairs={{32,0},{64,32},{96,64},{128,96},{160,128},{192,160},{224,192},{0,2... | collective-permute-start | bytes 884744 | tf_op jit(solution)/shard_map/ppermute | solution.py:395
  188.2 12.4 %collective-permute-start.10 = (bf16[18,64,128]{2,1,0:T(8,128)(2,1)S(1)}, bf16[18,64,128]{2,1,0:T(8,128)(2,1)S(1)}, u32[]{:S(2)}, u32[]{:S(2)}) collective-permute-start(bf16[18,64,128]{2,1,0:T(8,128)(2,1)S(1)} %get-tuple-element.101), channel_id=1, source_target_pairs={{0,32},{32,64},{64,96},{96,128},{128,160},{160,192},{192,224},{224... | collective-permute-start | bytes 884744 | tf_op jit(solution)/shard_map/ppermute | solution.py:393
  188.3 13.6 %collective-permute-start.11 = (bf16[18,64,128]{2,1,0:T(8,128)(2,1)S(1)}, bf16[18,64,128]{2,1,0:T(8,128)(2,1)S(1)}, u32[]{:S(2)}, u32[]{:S(2)}) collective-permute-start(bf16[18,64,128]{2,1,0:T(8,128)(2,1)S(1)} %get-tuple-element.102), channel_id=1, source_target_pairs={{32,0},{64,32},{96,64},{128,96},{160,128},{192,160},{224,192},{0,2... | collective-permute-start | bytes 884744 | tf_op jit(solution)/shard_map/ppermute | solution.py:395
  192.4 14.6 %collective-permute-start.19 = (bf16[18,64,128]{2,1,0:T(8,128)(2,1)S(1)}, bf16[18,64,128]{2,1,0:T(8,128)(2,1)S(1)}, u32[]{:S(2)}, u32[]{:S(2)}) collective-permute-start(bf16[18,64,128]{2,1,0:T(8,128)(2,1)S(1)} %get-tuple-element.120), channel_id=1, source_target_pairs={{0,32},{32,64},{64,96},{96,128},{128,160},{160,192},{192,224},{224... | collective-permute-start | bytes 884744 | tf_op jit(solution)/shard_map/ppermute | solution.py:393
  194.3 12.6 %collective-permute-start.20 = (bf16[18,64,128]{2,1,0:T(8,128)(2,1)S(1)}, bf16[18,64,128]{2,1,0:T(8,128)(2,1)S(1)}, u32[]{:S(2)}, u32[]{:S(2)}) collective-permute-start(bf16[18,64,128]{2,1,0:T(8,128)(2,1)S(1)} %get-tuple-element.121), channel_id=1, source_target_pairs={{32,0},{64,32},{96,64},{128,96},{160,128},{192,160},{224,192},{0,2... | collective-permute-start | bytes 884744 | tf_op jit(solution)/shard_map/ppermute | solution.py:395
  195.6 17.7 %collective-permute-start.26 = (bf16[18,64,128]{2,1,0:T(8,128)(2,1)S(1)}, bf16[18,64,128]{2,1,0:T(8,128)(2,1)S(1)}, u32[]{:S(2)}, u32[]{:S(2)}) collective-permute-start(bf16[18,64,128]{2,1,0:T(8,128)(2,1)S(1)} %get-tuple-element.135), channel_id=1, source_target_pairs={{0,32},{32,64},{64,96},{96,128},{128,160},{160,192},{192,224},{224... | collective-permute-start | bytes 884744 | tf_op jit(solution)/shard_map/ppermute | solution.py:393
  200.7 15.3 %collective-permute-start.27 = (bf16[18,64,128]{2,1,0:T(8,128)(2,1)S(1)}, bf16[18,64,128]{2,1,0:T(8,128)(2,1)S(1)}, u32[]{:S(2)}, u32[]{:S(2)}) collective-permute-start(bf16[18,64,128]{2,1,0:T(8,128)(2,1)S(1)} %get-tuple-element.136), channel_id=1, source_target_pairs={{32,0},{64,32},{96,64},{128,96},{160,128},{192,160},{224,192},{0,2... | collective-permute-start | bytes 884744 | tf_op jit(solution)/shard_map/ppermute | solution.py:395
  201.9 11.4 %collective-permute-start.29 = (f32[8,128]{1,0:T(8,128)S(1)}, f32[8,128]{1,0:T(8,128)S(1)}, u32[]{:S(2)}, u32[]{:S(2)}) collective-permute-start(f32[8,128]{1,0:T(8,128)S(1)} %add.95), channel_id=1, source_target_pairs={{0,64},{32,96},{64,0},{96,32},{128,192},{160,224},{192,128},{224,1... | collective-permute-start | bytes 12296 | tf_op jit(solution)/shard_map/ppermute | solution.py:400
  207.0 12.9 %copy-start.3 = (bf16[18,64,128]{2,1,0:T(8,128)(2,1)}, bf16[18,64,128]{2,1,0:T(8,128)(2,1)S(1)}, u32[]{:S(2)}) copy-start(bf16[18,64,128]{2,1,0:T(8,128)(2,1)S(1)} %collective-permute-done.19.refs_1_) | copy-start | bytes 884740
  207.0 21.3 %collective-permute-start.5 = (bf16[18,64,128]{2,1,0:T(8,128)(2,1)S(1)}, bf16[18,64,128]{2,1,0:T(8,128)(2,1)S(1)}, u32[]{:S(2)}, u32[]{:S(2)}) collective-permute-start(bf16[18,64,128]{2,1,0:T(8,128)(2,1)S(1)} %get-tuple-element.90), channel_id=1, source_target_pairs={{0,32},{32,64},{64,96},{96,128},{128,160},{160,192},{192,224},{224... | collective-permute-start | bytes 884744 | tf_op jit(solution)/shard_map/ppermute | solution.py:393
  207.0 12.9 %copy-start.4 = (bf16[18,64,128]{2,1,0:T(8,128)(2,1)}, bf16[18,64,128]{2,1,0:T(8,128)(2,1)S(1)}, u32[]{:S(2)}) copy-start(bf16[18,64,128]{2,1,0:T(8,128)(2,1)S(1)} %collective-permute-done.20.refs_2_) | copy-start | bytes 884740
  207.0 21.3 %collective-permute-start.6 = (bf16[18,64,128]{2,1,0:T(8,128)(2,1)S(1)}, bf16[18,64,128]{2,1,0:T(8,128)(2,1)S(1)}, u32[]{:S(2)}, u32[]{:S(2)}) collective-permute-start(bf16[18,64,128]{2,1,0:T(8,128)(2,1)S(1)} %get-tuple-element.91), channel_id=1, source_target_pairs={{32,0},{64,32},{96,64},{128,96},{160,128},{192,160},{224,192},{0,2... | collective-permute-start | bytes 884744 | tf_op jit(solution)/shard_map/ppermute | solution.py:395
  213.3 6.5 %copy-start.5 = (bf16[18,64,128]{2,1,0:T(8,128)(2,1)}, bf16[18,64,128]{2,1,0:T(8,128)(2,1)S(1)}, u32[]{:S(2)}) copy-start(bf16[18,64,128]{2,1,0:T(8,128)(2,1)S(1)} %collective-permute-done.26.refs_4_) | copy-start | bytes 884740
  213.3 15.0 %collective-permute-start.12 = (bf16[18,64,128]{2,1,0:T(8,128)(2,1)S(1)}, bf16[18,64,128]{2,1,0:T(8,128)(2,1)S(1)}, u32[]{:S(2)}, u32[]{:S(2)}) collective-permute-start(bf16[18,64,128]{2,1,0:T(8,128)(2,1)S(1)} %get-tuple-element.105), channel_id=1, source_target_pairs={{0,32},{32,64},{64,96},{96,128},{128,160},{160,192},{192,224},{224... | collective-permute-start | bytes 884744 | tf_op jit(solution)/shard_map/ppermute | solution.py:393
  213.3 15.0 %collective-permute-start.13 = (bf16[18,64,128]{2,1,0:T(8,128)(2,1)S(1)}, bf16[18,64,128]{2,1,0:T(8,128)(2,1)S(1)}, u32[]{:S(2)}, u32[]{:S(2)}) collective-permute-start(bf16[18,64,128]{2,1,0:T(8,128)(2,1)S(1)} %get-tuple-element.106), channel_id=1, source_target_pairs={{32,0},{64,32},{96,64},{128,96},{160,128},{192,160},{224,192},{0,2... | collective-permute-start | bytes 884744 | tf_op jit(solution)/shard_map/ppermute | solution.py:395
  216.0 3.9 %copy-start.6 = (bf16[18,64,128]{2,1,0:T(8,128)(2,1)}, bf16[18,64,128]{2,1,0:T(8,128)(2,1)S(1)}, u32[]{:S(2)}) copy-start(bf16[18,64,128]{2,1,0:T(8,128)(2,1)S(1)} %collective-permute-done.27.refs_5_) | copy-start | bytes 884740
  216.0 11.7 %collective-permute-start.30 = (f32[8,128]{1,0:T(8,128)S(1)}, f32[8,128]{1,0:T(8,128)S(1)}, u32[]{:S(2)}, u32[]{:S(2)}) collective-permute-start(f32[8,128]{1,0:T(8,128)S(1)} %add.96), channel_id=1, source_target_pairs={{0,128},{32,160},{64,192},{96,224},{128,0},{160,32},{192,64},{224,... | collective-permute-start | bytes 12296 | tf_op jit(solution)/shard_map/ppermute | solution.py:400

commit v7 on v6

--- a/solution.py
+++ b/solution.py
@@ -317,6 +317,9 @@
             ],
         ),
         out_shape=out_shape,
+        compiler_params=pltpu.CompilerParams(
+            vmem_limit_bytes=32 << 20
+        ),
     )(table, *args)
 
 
@@ -396,7 +399,7 @@
             up, down = lax.optimization_barrier((up, down))
             state[h] = [up, down]
         if grad is not None and 1 << s < n_arc:
-            swap = [(i, i ^ (1 << s)) for i in range(n_arc)]
+            swap = [(i, i ^ (far >> s)) for i in range(n_arc)]
             grad = grad + lax.ppermute(grad, "arc", swap)
     return [panels[0], *state[0], panels[1], *state[1]], grad
 

time: 234 us -> 229 us (0.979)
  waiting for transfers between devices: 103 us -> 109 us
  other arithmetic: 13 us -> 7.86 us
    convert_element_type x12, other arithmetic: 11 us -> 5.84 us  [ring(): add = lambda x, y: (x.astype(F32) + y.astype(F32)).astype(BF16)]
    ppermute x14, waiting for transfers between devices: 35 us -> 38.5 us  [ring(): up = lax.ppermute(up, 'arc', rising)]
    all_to_all x2, waiting for transfers between devices: 61.6 us -> 65.1 us  [send(): g = lax.all_to_all(p, 'tile', split_axis=0, concat_axis=0, tiled=True)]
  transfers between devices with their start and end apart: 34 -> 34, of which waited for: 14 -> 15; matrix products, arithmetic and copies ran while one was open for 6% -> 4% of each run, Pallas kernels for 14% -> 13%
where the time goes in v7:
time: 229 us
  waiting for transfers between devices  109 us (48%)
  starting transfers between devices  65.8 us (29%)
  Pallas kernels  40.4 us (18%)
  other arithmetic  7.86 us (3%)
  local copies, waits for them, and re-layouts  4.79 us (2%)
    all_to_all x2, waiting for transfers between devices, send(): g = lax.all_to_all(p, 'tile', split_axis=0, concat_axis=0, tiled=True)  65.1 us
    ppermute x14, waiting for transfers between devices, ring(): up = lax.ppermute(up, 'arc', rising)  38.5 us
    ppermute x14, starting transfers between devices, ring(): down = lax.ppermute(down, 'arc', falling)  35.1 us
    pallas_call x2, Pallas kernels, gather(): pl.pallas_call(functools.partial(gather_kernel, chunk), grid_spec=pltpu.P...  17 us
    all_to_all x2, starting transfers between devices, send(): g = lax.all_to_all(p, 'tile', split_axis=0, concat_axis=0, tiled=True)  14.5 us
    pallas_call x2, Pallas kernels, pack(): pl.pallas_call(functools.partial(pack_kernel, chunk), grid_spec=pltpu.Pre...  10.5 us
    all_to_all x1, starting transfers between devices, on_device(): lax.all_to_all(small, 'tile', split_axis=0, concat_axis=0, tiled=True)  8.58 us
    pallas_call x2, Pallas kernels, final(): pl.pallas_call(final_kernel, grid=(part // step,), in_specs=in_specs, out...  7.6 us
  transfers between devices with their start and end apart: 34, of which 15 were waited for; matrix products, arithmetic and copies ran while one was open for 4% of the time, Pallas kernels for 13%

profile of v7, /device:TPU:1, one launch (start us, length us, event | category | flops | bytes accessed | tf_op | source)
XLA Modules:
  0.0 228.6 jit_solution(7054382930425263182)
XLA Ops:
  0.6 0.7 multiply_add_fusion
  1.5 0.7 fusion
  2.2 0.6 broadcast_in_dim.8
  2.8 8.6 %all-to-all-start = ((f32[32,4,128]{2,1,0:T(4,128)}), f32[32,4,128]{2,1,0:T(4,128)S(1)}, u32[]{:S(2)}, u32[]{:S(2)}) async-start(f32[32,4,128]{2,1,0:T(4,128)} %broadcast_in_dim.8), calls=%async_computation | async-start | bytes 131072 | tf_op jit(solution)/shard_map/all_to_all | solution.py:421
  11.4 0.8 copy.13
  12.2 0.6 reshape.40.owner_ref
  12.8 3.4 %prepare.1 = (bf16[32,128,128]{2,1,0:T(8,128)(2,1)}, s32[64]{0:T(128)}) custom-call(s32[32]{0:T(128)} %reshape.40.owner_ref, bf16[8,128,512]{2,1,0:T(8,128)(2,1)} %design_ref.1), custom_call_target="tpu_custom_call" | custom-call | tf_op jit(solution)/shard_map/prepare/pallas_call | solution.py:45
  16.2 2.6 %all-to-all-done.all_ref = f32[32,4,128]{2,1,0:T(4,128)S(1)} async-done(((f32[32,4,128]{2,1,0:T(4,128)}), f32[32,4,128]{2,1,0:T(4,128)S(1)}, u32[]{:S(2)}, u32[]{:S(2)}) %all-to-all-start) | async-done | bytes 65568 | tf_op jit(solution)/shard_map/all_to_all | solution.py:421
  18.8 0.6 reshape.42.refs_5_
  19.4 6.1 %shard_map.95 = (bf16[32,128,128]{2,1,0:T(8,128)(2,1)}, bf16[8,16,128]{2,1,0:T(8,128)(2,1)}, bf16[64,320,128]{2,1,0:T(8,128)(2,1)}) custom-call(s32[64]{0:T(128)} %get-tuple-element.71.table_ref, s32[32]{0:T(128)} %copy-done.10, f32[8]{0:T(128)} %refs_1_.1, bf16[32,128,128]{2,1,0:T(8,128)(2,1)} %get-tuple-element.72.refs_2_, f32[8,128]{1,0:T(8,128)} %refs_3_.1, ...), custom_call_target="tpu_custom_call" | custom-call | tf_op jit(solution)/shard_map/pallas_call | solution.py:148
  25.5 4.9 %all-to-all-start.1 = ((bf16[32,2,320,128]{3,2,1,0:T(8,128)(2,1)}), bf16[32,2,320,128]{3,2,1,0:T(8,128)(2,1)}, u32[]{:S(2)}, u32[]{:S(2)}) async-start(bf16[32,2,320,128]{3,2,1,0:T(8,128)(2,1)} %bitcast.18), calls=%async_computation.1 | async-start | bytes 10485760 | tf_op jit(solution)/shard_map/all_to_all | solution.py:431
  30.4 0.6 pad_add_fusion.where_ref
  31.0 1.9 route.1
  32.9 0.8 reshape.45.table_ref
  33.7 4.5 %shard_map.96 = bf16[64,208,128]{2,1,0:T(8,128)(2,1)} custom-call(s32[64]{0:T(128)} %get-tuple-element.71.table_ref, bf16[32,128,128]{2,1,0:T(8,128)(2,1)} %get-tuple-element.74.refs_0_, bf16[8,16,128]{2,1,0:T(8,128)(2,1)} %get-tuple-element.75.refs_1_), custom_call_target="tpu_custom_call" | custom-call | tf_op jit(solution)/shard_map/pallas_call | solution.py:148
  38.2 56.7 %all-to-all-done.1 = bf16[32,2,320,128]{3,2,1,0:T(8,128)(2,1)} async-done(((bf16[32,2,320,128]{3,2,1,0:T(8,128)(2,1)}), bf16[32,2,320,128]{3,2,1,0:T(8,128)(2,1)}, u32[]{:S(2)}, u32[]{:S(2)}) %all-to-all-start.1) | async-done | bytes 5242912 | tf_op jit(solution)/shard_map/all_to_all | solution.py:431
  94.9 9.6 %all-to-all-start.2 = ((bf16[32,2,208,128]{3,2,1,0:T(8,128)(2,1)}), bf16[32,2,208,128]{3,2,1,0:T(8,128)(2,1)S(1)}, u32[]{:S(2)}, u32[]{:S(2)}) async-start(bf16[32,2,208,128]{3,2,1,0:T(8,128)(2,1)} %bitcast.14), calls=%async_computation.2 | async-start | bytes 6815744 | tf_op jit(solution)/shard_map/all_to_all | solution.py:431
  104.5 8.4 %shard_map.98 = (bf16[144,64,128]{2,1,0:T(8,128)(2,1)S(1)}, bf16[144,64,128]{2,1,0:T(8,128)(2,1)S(1)}, bf16[18,64,128]{2,1,0:T(8,128)(2,1)S(1)}, bf16[18,64,128]...) custom-call(s32[512]{0:T(512)S(1)} %reshape.45.table_ref, ...), custom_call_target="tpu_custom_call" | custom-call | tf_op jit(solution)/shard_map/pallas_call | solution.py:306
  112.9 1.7 collective-permute-start.14
  114.6 4.0 %collective-permute-start.21 = (bf16[18,64,128]{2,1,0:T(8,128)(2,1)S(1)}, bf16[18,64,128]{2,1,0:T(8,128)(2,1)S(1)}, u32[]{:S(2)}, u32[]{:S(2)}) collective-permute-start(bf16[18,64,128]{2,1,0:T(8,128)(2,1)S(1)} %get-tuple-element.126), channel_id=1, source_target_pairs={{32,0},{64,32},{96,64},{128,96},{160,128},{192,160},{224,192},{0,2... | collective-permute-start | bytes 884744 | tf_op jit(solution)/shard_map/ppermute | solution.py:398
  118.6 7.1 %collective-permute-done.14 = bf16[18,64,128]{2,1,0:T(8,128)(2,1)S(1)} collective-permute-done((bf16[18,64,128]{2,1,0:T(8,128)(2,1)S(1)}, bf16[18,64,128]{2,1,0:T(8,128)(2,1)S(1)}, u32[]{:S(2)}, u32[]{:S(2)}) %collective-permute-start.14) | collective-permute-done | bytes 294944 | tf_op jit(solution)/shard_map/ppermute | solution.py:396
  125.9 2.7 %collective-permute-start.16 = (bf16[18,64,128]{2,1,0:T(8,128)(2,1)S(1)}, bf16[18,64,128]{2,1,0:T(8,128)(2,1)S(1)}, u32[]{:S(2)}, u32[]{:S(2)}) collective-permute-start(bf16[18,64,128]{2,1,0:T(8,128)(2,1)S(1)} %get-tuple-element.113), channel_id=1, source_target_pairs={{32,0},{64,32},{96,64},{128,96},{160,128},{192,160},{224,192},{0,2... | collective-permute-start | bytes 884744 | tf_op jit(solution)/shard_map/ppermute | solution.py:398
  128.5 0.8 add_convert_fusion.4
  129.3 2.7 %collective-permute-start.23 = (bf16[18,64,128]{2,1,0:T(8,128)(2,1)}, bf16[18,64,128]{2,1,0:T(8,128)(2,1)}, u32[]{:S(2)}, u32[]{:S(2)}) collective-permute-start(bf16[18,64,128]{2,1,0:T(8,128)(2,1)} %add_convert_fusion.4), channel_id=1, source_target_pairs={{32,0},{64,32},{96,64},{128,96},{160,128},{192,160},{224,192},{0,2... | collective-permute-start | bytes 884744 | tf_op jit(solution)/shard_map/ppermute | solution.py:398
  132.0 2.8 %collective-permute-done.15 = bf16[18,64,128]{2,1,0:T(8,128)(2,1)S(1)} collective-permute-done((bf16[18,64,128]{2,1,0:T(8,128)(2,1)S(1)}, bf16[18,64,128]{2,1,0:T(8,128)(2,1)S(1)}, u32[]{:S(2)}, u32[]{:S(2)}) %collective-permute-start.15) | collective-permute-done | bytes 294944 | tf_op jit(solution)/shard_map/ppermute | solution.py:396
  134.8 1.0 add_convert_fusion.7
  135.9 2.7 %collective-permute-start.18 = (bf16[18,64,128]{2,1,0:T(8,128)(2,1)}, bf16[18,64,128]{2,1,0:T(8,128)(2,1)}, u32[]{:S(2)}, u32[]{:S(2)}) collective-permute-start(bf16[18,64,128]{2,1,0:T(8,128)(2,1)} %get-tuple-element.117), channel_id=1, source_target_pairs={{32,0},{64,32},{96,64},{128,96},{160,128},{192,160},{224,192},{0,2... | collective-permute-start | bytes 884744 | tf_op jit(solution)/shard_map/ppermute | solution.py:398
  138.6 8.4 %all-to-all-done.2 = bf16[32,2,208,128]{3,2,1,0:T(8,128)(2,1)S(1)} async-done(((bf16[32,2,208,128]{3,2,1,0:T(8,128)(2,1)}), bf16[32,2,208,128]{3,2,1,0:T(8,128)(2,1)S(1)}, u32[]{:S(2)}, u32[]{:S(2)}) %all-to-all-start.2) | async-done | bytes 3407904 | tf_op jit(solution)/shard_map/all_to_all | solution.py:431
  147.0 8.6 %shard_map.97 = (bf16[144,64,128]{2,1,0:T(8,128)(2,1)S(1)}, bf16[144,64,128]{2,1,0:T(8,128)(2,1)S(1)}, bf16[18,64,128]{2,1,0:T(8,128)(2,1)S(1)}, bf16[18,64,128]...) custom-call(s32[512]{0:T(512)S(1)} %reshape.45.table_ref, ...), custom_call_target="tpu_custom_call" | custom-call | tf_op jit(solution)/shard_map/pallas_call | solution.py:306
  155.6 1.9 collective-permute-start
  157.5 4.0 %collective-permute-start.7 = (bf16[18,64,128]{2,1,0:T(8,128)(2,1)S(1)}, bf16[18,64,128]{2,1,0:T(8,128)(2,1)S(1)}, u32[]{:S(2)}, u32[]{:S(2)}) collective-permute-start(bf16[18,64,128]{2,1,0:T(8,128)(2,1)S(1)} %get-tuple-element.96), channel_id=1, source_target_pairs={{32,0},{64,32},{96,64},{128,96},{160,128},{192,160},{224,192},{0,2... | collective-permute-start | bytes 884744 | tf_op jit(solution)/shard_map/ppermute | solution.py:398
  161.5 1.3 add_convert_fusion.2
  162.9 2.7 %collective-permute-start.25 = (bf16[18,64,128]{2,1,0:T(8,128)(2,1)S(1)}, bf16[18,64,128]{2,1,0:T(8,128)(2,1)S(1)}, u32[]{:S(2)}, u32[]{:S(2)}) collective-permute-start(bf16[18,64,128]{2,1,0:T(8,128)(2,1)S(1)} %get-tuple-element.132), channel_id=1, source_target_pairs={{32,0},{64,32},{96,64},{128,96},{160,128},{192,160},{224,192},{0,2... | collective-permute-start | bytes 884744 | tf_op jit(solution)/shard_map/ppermute | solution.py:398
  165.5 2.3 %collective-permute-done = bf16[18,64,128]{2,1,0:T(8,128)(2,1)S(1)} collective-permute-done((bf16[18,64,128]{2,1,0:T(8,128)(2,1)S(1)}, bf16[18,64,128]{2,1,0:T(8,128)(2,1)S(1)}, u32[]{:S(2)}, u32[]{:S(2)}) %collective-permute-start) | collective-permute-done | bytes 294944 | tf_op jit(solution)/shard_map/ppermute | solution.py:396
  168.1 2.7 %collective-permute-start.2 = (bf16[18,64,128]{2,1,0:T(8,128)(2,1)S(1)}, bf16[18,64,128]{2,1,0:T(8,128)(2,1)S(1)}, u32[]{:S(2)}, u32[]{:S(2)}) collective-permute-start(bf16[18,64,128]{2,1,0:T(8,128)(2,1)S(1)} %get-tuple-element.83), channel_id=1, source_target_pairs={{32,0},{64,32},{96,64},{128,96},{160,128},{192,160},{224,192},{0,2... | collective-permute-start | bytes 884744 | tf_op jit(solution)/shard_map/ppermute | solution.py:398
  170.9 3.3 %collective-permute-done.24 = bf16[18,64,128]{2,1,0:T(8,128)(2,1)S(1)} collective-permute-done((bf16[18,64,128]{2,1,0:T(8,128)(2,1)S(1)}, bf16[18,64,128]{2,1,0:T(8,128)(2,1)S(1)}, u32[]{:S(2)}, u32[]{:S(2)}) %collective-permute-start.24) | collective-permute-done | bytes 294944 | tf_op jit(solution)/shard_map/ppermute | solution.py:396
  174.2 1.2 collective-permute-start.9
  175.4 1.4 add_convert_fusion.5
  176.8 2.7 %collective-permute-start.28 = (f32[8,128]{1,0:T(8,128)S(1)}, f32[8,128]{1,0:T(8,128)S(1)}, u32[]{:S(2)}, u32[]{:S(2)}) collective-permute-start(f32[8,128]{1,0:T(8,128)S(1)} %get-tuple-element.139), channel_id=1, source_target_pairs={{0,128},{32,160},{64,192},{96,224},{128,0},{160,32},{192,64},{224,... | collective-permute-start | bytes 12296 | tf_op jit(solution)/shard_map/ppermute | solution.py:403
  179.5 1.0 collective-permute-done.1
  180.5 0.2 add_convert_fusion.17
  180.8 0.5 collective-permute-start.3
  181.3 2.2 collective-permute-start.4
  183.5 3.3 %collective-permute-done.8 = bf16[18,64,128]{2,1,0:T(8,128)(2,1)S(1)} collective-permute-done((bf16[18,64,128]{2,1,0:T(8,128)(2,1)S(1)}, bf16[18,64,128]{2,1,0:T(8,128)(2,1)S(1)}, u32[]{:S(2)}, u32[]{:S(2)}) %collective-permute-start.8) | collective-permute-done | bytes 294944 | tf_op jit(solution)/shard_map/ppermute | solution.py:396
  186.9 0.2 add_convert_fusion.12
  187.2 2.7 %collective-permute-start.11 = (bf16[18,64,128]{2,1,0:T(8,128)(2,1)S(1)}, bf16[18,64,128]{2,1,0:T(8,128)(2,1)S(1)}, u32[]{:S(2)}, u32[]{:S(2)}) collective-permute-start(bf16[18,64,128]{2,1,0:T(8,128)(2,1)S(1)} %get-tuple-element.102), channel_id=1, source_target_pairs={{32,0},{64,32},{96,64},{128,96},{160,128},{192,160},{224,192},{0,2... | collective-permute-start | bytes 884744 | tf_op jit(solution)/shard_map/ppermute | solution.py:398
  189.8 0.2 add_convert_fusion
  190.2 3.2 %collective-permute-done.3 = bf16[18,64,128]{2,1,0:T(8,128)(2,1)S(1)} collective-permute-done((bf16[18,64,128]{2,1,0:T(8,128)(2,1)S(1)}, bf16[18,64,128]{2,1,0:T(8,128)(2,1)S(1)}, u32[]{:S(2)}, u32[]{:S(2)}) %collective-permute-start.3) | collective-permute-done | bytes 294944 | tf_op jit(solution)/shard_map/ppermute | solution.py:396
  193.3 1.2 collective-permute-start.20
  194.5 0.3 collective-permute-start.26
  194.8 0.2 add_convert_fusion.15
  195.0 4.6 %collective-permute-done.10 = bf16[18,64,128]{2,1,0:T(8,128)(2,1)S(1)} collective-permute-done((bf16[18,64,128]{2,1,0:T(8,128)(2,1)S(1)}, bf16[18,64,128]{2,1,0:T(8,128)(2,1)S(1)}, u32[]{:S(2)}, u32[]{:S(2)}) %collective-permute-start.10) | collective-permute-done | bytes 294944 | tf_op jit(solution)/shard_map/ppermute | solution.py:396
  199.7 1.2 collective-permute-start.27
  200.9 0.2 add_convert_fusion.10
  201.1 4.9 %collective-permute-done.19.refs_1_ = bf16[18,64,128]{2,1,0:T(8,128)(2,1)S(1)} collective-permute-done((bf16[18,64,128]{2,1,0:T(8,128)(2,1)S(1)}, bf16[18,64,128]{2,1,0:T(8,128)(2,1)S(1)}, u32[]{:S(2)}, u32[]{:S(2)}) %collective-permute-start.19) | collective-permute-done | bytes 294944 | tf_op jit(solution)/shard_map/ppermute | solution.py:396
  206.0 2.7 %collective-permute-start.6 = (bf16[18,64,128]{2,1,0:T(8,128)(2,1)S(1)}, bf16[18,64,128]{2,1,0:T(8,128)(2,1)S(1)}, u32[]{:S(2)}, u32[]{:S(2)}) collective-permute-start(bf16[18,64,128]{2,1,0:T(8,128)(2,1)S(1)} %get-tuple-element.91), channel_id=1, source_target_pairs={{32,0},{64,32},{96,64},{128,96},{160,128},{192,160},{224,192},{0,2... | collective-permute-start | bytes 884744 | tf_op jit(solution)/shard_map/ppermute | solution.py:398
  208.7 3.6 %collective-permute-done.26.refs_4_ = bf16[18,64,128]{2,1,0:T(8,128)(2,1)S(1)} collective-permute-done((bf16[18,64,128]{2,1,0:T(8,128)(2,1)S(1)}, bf16[18,64,128]{2,1,0:T(8,128)(2,1)S(1)}, u32[]{:S(2)}, u32[]{:S(2)}) %collective-permute-start.26) | collective-permute-done | bytes 294944 | tf_op jit(solution)/shard_map/ppermute | solution.py:396
  212.3 2.7 %collective-permute-start.13 = (bf16[18,64,128]{2,1,0:T(8,128)(2,1)S(1)}, bf16[18,64,128]{2,1,0:T(8,128)(2,1)S(1)}, u32[]{:S(2)}, u32[]{:S(2)}) collective-permute-start(bf16[18,64,128]{2,1,0:T(8,128)(2,1)S(1)} %get-tuple-element.106), channel_id=1, source_target_pairs={{32,0},{64,32},{96,64},{128,96},{160,128},{192,160},{224,192},{0,2... | collective-permute-start | bytes 884744 | tf_op jit(solution)/shard_map/ppermute | solution.py:398
  215.1 0.6 copy-done.9
  215.7 4.0 %shard_map.99.refs_6_ = f32[12,128,384]{2,1,0:T(8,128)} custom-call(f32[12,128,384]{2,1,0:T(8,128)} %bitcast.15, bf16[144,64,128]{2,1,0:T(8,128)(2,1)} %copy-done.2, bf16[18,64,128]{2,1,0:T(8,128)(2,1)} %copy-done.6, bf16[18,64,128]{2,1,0:T(8,128)(2,1)} %copy-done.7, bf16[144,64,128]{2,1,0:T(8,128)(2,1)} %copy-done.3, bf16[18,64,128]{2,1,0:T(8,128)(2,1)} %copy-done.8, ...), custom_call_target="tpu_custom_call" | custom-call | tf_op jit(solution)/shard_map/pallas_call | solution.py:365
  219.7 2.4 %collective-permute-done.30 = f32[8,128]{1,0:T(8,128)S(1)} collective-permute-done((f32[8,128]{1,0:T(8,128)S(1)}, f32[8,128]{1,0:T(8,128)S(1)}, u32[]{:S(2)}, u32[]{:S(2)}) %collective-permute-start.30) | collective-permute-done | bytes 4128 | tf_op jit(solution)/shard_map/ppermute | solution.py:403
  222.1 0.6 slice_bitcast_fusion
  222.7 2.3 collective-permute-done.12.refs_4_
  224.9 3.6 %shard_map.100 = f32[12,128,384]{2,1,0:T(8,128)} custom-call(f32[12,128,384]{2,1,0:T(8,128)} %bitcast.16, bf16[144,64,128]{2,1,0:T(8,128)(2,1)} %copy-done, bf16[18,64,128]{2,1,0:T(8,128)(2,1)S(1)} %collective-permute-done.5.refs_1_, bf16[18,64,128]{2,1,0:T(8,128)(2,1)S(1)} %collective-permute-done.6.refs_2_, ...), custom_call_target="tpu_custom_call", output_to_operand_aliasing={{}: (7, {})} | custom-call | tf_op jit(solution)/shard_map/pallas_call | solution.py:365
  (61 shorter events, 1.1 us)
Async XLA Ops:
  1.5 17.9 %copy-start.10 = (s32[32]{0:T(128)}, s32[32]{0:T(128)S(1)}, u32[]{:S(2)}) copy-start(s32[32]{0:T(128)S(1)} %reshape.41.refs_0_) | copy-start | bytes 388
  2.8 15.9 %all-to-all-start = ((f32[32,4,128]{2,1,0:T(4,128)}), f32[32,4,128]{2,1,0:T(4,128)S(1)}, u32[]{:S(2)}, u32[]{:S(2)}) async-start(f32[32,4,128]{2,1,0:T(4,128)} %broadcast_in_dim.8), calls=%async_computation | async-start | bytes 131072 | tf_op jit(solution)/shard_map/all_to_all | solution.py:421
  18.8 6.7 %copy-start.5 = (f32[32,4,128]{2,1,0:T(4,128)}, f32[32,4,128]{2,1,0:T(4,128)S(1)}, u32[]{:S(2)}) copy-start(f32[32,4,128]{2,1,0:T(4,128)S(1)} %all-to-all-done.all_ref) | copy-start | bytes 196612
  25.5 69.4 %all-to-all-start.1 = ((bf16[32,2,320,128]{3,2,1,0:T(8,128)(2,1)}), bf16[32,2,320,128]{3,2,1,0:T(8,128)(2,1)}, u32[]{:S(2)}, u32[]{:S(2)}) async-start(bf16[32,2,320,128]{3,2,1,0:T(8,128)(2,1)} %bitcast.18), calls=%async_computation.1 | async-start | bytes 10485760 | tf_op jit(solution)/shard_map/all_to_all | solution.py:431
  94.9 52.1 %all-to-all-start.2 = ((bf16[32,2,208,128]{3,2,1,0:T(8,128)(2,1)}), bf16[32,2,208,128]{3,2,1,0:T(8,128)(2,1)S(1)}, u32[]{:S(2)}, u32[]{:S(2)}) async-start(bf16[32,2,208,128]{3,2,1,0:T(8,128)(2,1)} %bitcast.14), calls=%async_computation.2 | async-start | bytes 6815744 | tf_op jit(solution)/shard_map/all_to_all | solution.py:431
  112.9 23.0 %copy-start.2 = (bf16[144,64,128]{2,1,0:T(8,128)(2,1)}, bf16[144,64,128]{2,1,0:T(8,128)(2,1)S(1)}, u32[]{:S(2)}) copy-start(bf16[144,64,128]{2,1,0:T(8,128)(2,1)S(1)} %get-tuple-element.109.refs_0_) | copy-start | bytes 7077892
  112.9 23.0 %copy-start.3 = (bf16[144,64,128]{2,1,0:T(8,128)(2,1)}, bf16[144,64,128]{2,1,0:T(8,128)(2,1)S(1)}, u32[]{:S(2)}) copy-start(bf16[144,64,128]{2,1,0:T(8,128)(2,1)S(1)} %get-tuple-element.124.refs_3_) | copy-start | bytes 7077892
  112.9 12.8 %collective-permute-start.14 = (bf16[18,64,128]{2,1,0:T(8,128)(2,1)S(1)}, bf16[18,64,128]{2,1,0:T(8,128)(2,1)S(1)}, u32[]{:S(2)}, u32[]{:S(2)}) collective-permute-start(bf16[18,64,128]{2,1,0:T(8,128)(2,1)S(1)} %get-tuple-element.110), channel_id=1, source_target_pairs={{0,32},{32,64},{64,96},{96,128},{128,160},{160,192},{192,224},{224... | collective-permute-start | bytes 884744 | tf_op jit(solution)/shard_map/ppermute | solution.py:396
  114.6 13.9 %collective-permute-start.21 = (bf16[18,64,128]{2,1,0:T(8,128)(2,1)S(1)}, bf16[18,64,128]{2,1,0:T(8,128)(2,1)S(1)}, u32[]{:S(2)}, u32[]{:S(2)}) collective-permute-start(bf16[18,64,128]{2,1,0:T(8,128)(2,1)S(1)} %get-tuple-element.126), channel_id=1, source_target_pairs={{32,0},{64,32},{96,64},{128,96},{160,128},{192,160},{224,192},{0,2... | collective-permute-start | bytes 884744 | tf_op jit(solution)/shard_map/ppermute | solution.py:398
  125.8 9.0 %collective-permute-start.15 = (bf16[18,64,128]{2,1,0:T(8,128)(2,1)S(1)}, bf16[18,64,128]{2,1,0:T(8,128)(2,1)S(1)}, u32[]{:S(2)}, u32[]{:S(2)}) collective-permute-start(bf16[18,64,128]{2,1,0:T(8,128)(2,1)S(1)} %add_convert_fusion.9), channel_id=1, source_target_pairs={{0,32},{32,64},{64,96},{96,128},{128,160},{160,192},{192,224},{224... | collective-permute-start | bytes 884744 | tf_op jit(solution)/shard_map/ppermute | solution.py:396
  125.9 9.0 %collective-permute-start.16 = (bf16[18,64,128]{2,1,0:T(8,128)(2,1)S(1)}, bf16[18,64,128]{2,1,0:T(8,128)(2,1)S(1)}, u32[]{:S(2)}, u32[]{:S(2)}) collective-permute-start(bf16[18,64,128]{2,1,0:T(8,128)(2,1)S(1)} %get-tuple-element.113), channel_id=1, source_target_pairs={{32,0},{64,32},{96,64},{128,96},{160,128},{192,160},{224,192},{0,2... | collective-permute-start | bytes 884744 | tf_op jit(solution)/shard_map/ppermute | solution.py:398
  129.3 28.2 %collective-permute-start.22 = (bf16[18,64,128]{2,1,0:T(8,128)(2,1)}, bf16[18,64,128]{2,1,0:T(8,128)(2,1)}, u32[]{:S(2)}, u32[]{:S(2)}) collective-permute-start(bf16[18,64,128]{2,1,0:T(8,128)(2,1)} %get-tuple-element.127), channel_id=1, source_target_pairs={{0,32},{32,64},{64,96},{96,128},{128,160},{160,192},{192,224},{224... | collective-permute-start | bytes 884744 | tf_op jit(solution)/shard_map/ppermute | solution.py:396
  129.3 28.2 %collective-permute-start.23 = (bf16[18,64,128]{2,1,0:T(8,128)(2,1)}, bf16[18,64,128]{2,1,0:T(8,128)(2,1)}, u32[]{:S(2)}, u32[]{:S(2)}) collective-permute-start(bf16[18,64,128]{2,1,0:T(8,128)(2,1)} %add_convert_fusion.4), channel_id=1, source_target_pairs={{32,0},{64,32},{96,64},{128,96},{160,128},{192,160},{224,192},{0,2... | collective-permute-start | bytes 884744 | tf_op jit(solution)/shard_map/ppermute | solution.py:398
  135.9 27.0 %collective-permute-start.17 = (bf16[18,64,128]{2,1,0:T(8,128)(2,1)}, bf16[18,64,128]{2,1,0:T(8,128)(2,1)}, u32[]{:S(2)}, u32[]{:S(2)}) collective-permute-start(bf16[18,64,128]{2,1,0:T(8,128)(2,1)} %get-tuple-element.116), channel_id=1, source_target_pairs={{0,32},{32,64},{64,96},{96,128},{128,160},{160,192},{192,224},{224... | collective-permute-start | bytes 884744 | tf_op jit(solution)/shard_map/ppermute | solution.py:396
  135.9 29.7 %collective-permute-start.18 = (bf16[18,64,128]{2,1,0:T(8,128)(2,1)}, bf16[18,64,128]{2,1,0:T(8,128)(2,1)}, u32[]{:S(2)}, u32[]{:S(2)}) collective-permute-start(bf16[18,64,128]{2,1,0:T(8,128)(2,1)} %get-tuple-element.117), channel_id=1, source_target_pairs={{32,0},{64,32},{96,64},{128,96},{160,128},{192,160},{224,192},{0,2... | collective-permute-start | bytes 884744 | tf_op jit(solution)/shard_map/ppermute | solution.py:398
  147.0 14.6 %copy-start.4 = (bf16[144,64,128]{2,1,0:T(8,128)(2,1)S(1)}, bf16[144,64,128]{2,1,0:T(8,128)(2,1)}, u32[]{:S(2)}) copy-start(bf16[144,64,128]{2,1,0:T(8,128)(2,1)} %copy-done.3) | copy-start | bytes 7077892
  155.6 39.2 %copy-start = (bf16[144,64,128]{2,1,0:T(8,128)(2,1)}, bf16[144,64,128]{2,1,0:T(8,128)(2,1)S(1)}, u32[]{:S(2)}) copy-start(bf16[144,64,128]{2,1,0:T(8,128)(2,1)S(1)} %get-tuple-element.79.refs_0_) | copy-start | bytes 7077892
  155.6 45.3 %copy-start.1 = (bf16[144,64,128]{2,1,0:T(8,128)(2,1)}, bf16[144,64,128]{2,1,0:T(8,128)(2,1)S(1)}, u32[]{:S(2)}) copy-start(bf16[144,64,128]{2,1,0:T(8,128)(2,1)S(1)} %get-tuple-element.94.refs_3_) | copy-start | bytes 7077892
  155.6 12.3 %collective-permute-start = (bf16[18,64,128]{2,1,0:T(8,128)(2,1)S(1)}, bf16[18,64,128]{2,1,0:T(8,128)(2,1)S(1)}, u32[]{:S(2)}, u32[]{:S(2)}) collective-permute-start(bf16[18,64,128]{2,1,0:T(8,128)(2,1)S(1)} %get-tuple-element.80), channel_id=1, source_target_pairs={{0,32},{32,64},{64,96},{96,128},{128,160},{160,192},{192,224},{224... | collective-permute-start | bytes 884744 | tf_op jit(solution)/shard_map/ppermute | solution.py:396
  157.5 13.2 %collective-permute-start.7 = (bf16[18,64,128]{2,1,0:T(8,128)(2,1)S(1)}, bf16[18,64,128]{2,1,0:T(8,128)(2,1)S(1)}, u32[]{:S(2)}, u32[]{:S(2)}) collective-permute-start(bf16[18,64,128]{2,1,0:T(8,128)(2,1)S(1)} %get-tuple-element.96), channel_id=1, source_target_pairs={{32,0},{64,32},{96,64},{128,96},{160,128},{192,160},{224,192},{0,2... | collective-permute-start | bytes 884744 | tf_op jit(solution)/shard_map/ppermute | solution.py:398
  162.8 11.4 %collective-permute-start.24 = (bf16[18,64,128]{2,1,0:T(8,128)(2,1)S(1)}, bf16[18,64,128]{2,1,0:T(8,128)(2,1)S(1)}, u32[]{:S(2)}, u32[]{:S(2)}) collective-permute-start(bf16[18,64,128]{2,1,0:T(8,128)(2,1)S(1)} %get-tuple-element.131), channel_id=1, source_target_pairs={{0,32},{32,64},{64,96},{96,128},{128,160},{160,192},{192,224},{224... | collective-permute-start | bytes 884744 | tf_op jit(solution)/shard_map/ppermute | solution.py:396
  162.9 13.9 %collective-permute-start.25 = (bf16[18,64,128]{2,1,0:T(8,128)(2,1)S(1)}, bf16[18,64,128]{2,1,0:T(8,128)(2,1)S(1)}, u32[]{:S(2)}, u32[]{:S(2)}) collective-permute-start(bf16[18,64,128]{2,1,0:T(8,128)(2,1)S(1)} %get-tuple-element.132), channel_id=1, source_target_pairs={{32,0},{64,32},{96,64},{128,96},{160,128},{192,160},{224,192},{0,2... | collective-permute-start | bytes 884744 | tf_op jit(solution)/shard_map/ppermute | solution.py:398
  168.0 12.5 %collective-permute-start.1 = (bf16[18,64,128]{2,1,0:T(8,128)(2,1)S(1)}, bf16[18,64,128]{2,1,0:T(8,128)(2,1)S(1)}, u32[]{:S(2)}, u32[]{:S(2)}) collective-permute-start(bf16[18,64,128]{2,1,0:T(8,128)(2,1)S(1)} %add_convert_fusion.19), channel_id=1, source_target_pairs={{0,32},{32,64},{64,96},{96,128},{128,160},{160,192},{192,224},{224... | collective-permute-start | bytes 884744 | tf_op jit(solution)/shard_map/ppermute | solution.py:396
  168.1 12.5 %collective-permute-start.2 = (bf16[18,64,128]{2,1,0:T(8,128)(2,1)S(1)}, bf16[18,64,128]{2,1,0:T(8,128)(2,1)S(1)}, u32[]{:S(2)}, u32[]{:S(2)}) collective-permute-start(bf16[18,64,128]{2,1,0:T(8,128)(2,1)S(1)} %get-tuple-element.83), channel_id=1, source_target_pairs={{32,0},{64,32},{96,64},{128,96},{160,128},{192,160},{224,192},{0,2... | collective-permute-start | bytes 884744 | tf_op jit(solution)/shard_map/ppermute | solution.py:398
  170.8 16.0 %collective-permute-start.8 = (bf16[18,64,128]{2,1,0:T(8,128)(2,1)S(1)}, bf16[18,64,128]{2,1,0:T(8,128)(2,1)S(1)}, u32[]{:S(2)}, u32[]{:S(2)}) collective-permute-start(bf16[18,64,128]{2,1,0:T(8,128)(2,1)S(1)} %get-tuple-element.97), channel_id=1, source_target_pairs={{0,32},{32,64},{64,96},{96,128},{128,160},{160,192},{192,224},{224... | collective-permute-start | bytes 884744 | tf_op jit(solution)/shard_map/ppermute | solution.py:396
  174.2 12.6 %collective-permute-start.9 = (bf16[18,64,128]{2,1,0:T(8,128)(2,1)S(1)}, bf16[18,64,128]{2,1,0:T(8,128)(2,1)S(1)}, u32[]{:S(2)}, u32[]{:S(2)}) collective-permute-start(bf16[18,64,128]{2,1,0:T(8,128)(2,1)S(1)} %add_convert_fusion.14), channel_id=1, source_target_pairs={{32,0},{64,32},{96,64},{128,96},{160,128},{192,160},{224,192},{0,2... | collective-permute-start | bytes 884744 | tf_op jit(solution)/shard_map/ppermute | solution.py:398
  176.8 13.2 %collective-permute-start.28 = (f32[8,128]{1,0:T(8,128)S(1)}, f32[8,128]{1,0:T(8,128)S(1)}, u32[]{:S(2)}, u32[]{:S(2)}) collective-permute-start(f32[8,128]{1,0:T(8,128)S(1)} %get-tuple-element.139), channel_id=1, source_target_pairs={{0,128},{32,160},{64,192},{96,224},{128,0},{160,32},{192,64},{224,... | collective-permute-start | bytes 12296 | tf_op jit(solution)/shard_map/ppermute | solution.py:403
  180.8 12.6 %collective-permute-start.3 = (bf16[18,64,128]{2,1,0:T(8,128)(2,1)S(1)}, bf16[18,64,128]{2,1,0:T(8,128)(2,1)S(1)}, u32[]{:S(2)}, u32[]{:S(2)}) collective-permute-start(bf16[18,64,128]{2,1,0:T(8,128)(2,1)S(1)} %get-tuple-element.86), channel_id=1, source_target_pairs={{0,32},{32,64},{64,96},{96,128},{128,160},{160,192},{192,224},{224... | collective-permute-start | bytes 884744 | tf_op jit(solution)/shard_map/ppermute | solution.py:396
  181.3 13.3 %collective-permute-start.4 = (bf16[18,64,128]{2,1,0:T(8,128)(2,1)S(1)}, bf16[18,64,128]{2,1,0:T(8,128)(2,1)S(1)}, u32[]{:S(2)}, u32[]{:S(2)}) collective-permute-start(bf16[18,64,128]{2,1,0:T(8,128)(2,1)S(1)} %get-tuple-element.87), channel_id=1, source_target_pairs={{32,0},{64,32},{96,64},{128,96},{160,128},{192,160},{224,192},{0,2... | collective-permute-start | bytes 884744 | tf_op jit(solution)/shard_map/ppermute | solution.py:398
  187.1 12.6 %collective-permute-start.10 = (bf16[18,64,128]{2,1,0:T(8,128)(2,1)S(1)}, bf16[18,64,128]{2,1,0:T(8,128)(2,1)S(1)}, u32[]{:S(2)}, u32[]{:S(2)}) collective-permute-start(bf16[18,64,128]{2,1,0:T(8,128)(2,1)S(1)} %get-tuple-element.101), channel_id=1, source_target_pairs={{0,32},{32,64},{64,96},{96,128},{128,160},{160,192},{192,224},{224... | collective-permute-start | bytes 884744 | tf_op jit(solution)/shard_map/ppermute | solution.py:396
  187.2 13.7 %collective-permute-start.11 = (bf16[18,64,128]{2,1,0:T(8,128)(2,1)S(1)}, bf16[18,64,128]{2,1,0:T(8,128)(2,1)S(1)}, u32[]{:S(2)}, u32[]{:S(2)}) collective-permute-start(bf16[18,64,128]{2,1,0:T(8,128)(2,1)S(1)} %get-tuple-element.102), channel_id=1, source_target_pairs={{32,0},{64,32},{96,64},{128,96},{160,128},{192,160},{224,192},{0,2... | collective-permute-start | bytes 884744 | tf_op jit(solution)/shard_map/ppermute | solution.py:398
  190.0 15.9 %collective-permute-start.19 = (bf16[18,64,128]{2,1,0:T(8,128)(2,1)S(1)}, bf16[18,64,128]{2,1,0:T(8,128)(2,1)S(1)}, u32[]{:S(2)}, u32[]{:S(2)}) collective-permute-start(bf16[18,64,128]{2,1,0:T(8,128)(2,1)S(1)} %get-tuple-element.120), channel_id=1, source_target_pairs={{0,32},{32,64},{64,96},{96,128},{128,160},{160,192},{192,224},{224... | collective-permute-start | bytes 884744 | tf_op jit(solution)/shard_map/ppermute | solution.py:396
  193.3 12.6 %collective-permute-start.20 = (bf16[18,64,128]{2,1,0:T(8,128)(2,1)S(1)}, bf16[18,64,128]{2,1,0:T(8,128)(2,1)S(1)}, u32[]{:S(2)}, u32[]{:S(2)}) collective-permute-start(bf16[18,64,128]{2,1,0:T(8,128)(2,1)S(1)} %get-tuple-element.121), channel_id=1, source_target_pairs={{32,0},{64,32},{96,64},{128,96},{160,128},{192,160},{224,192},{0,2... | collective-permute-start | bytes 884744 | tf_op jit(solution)/shard_map/ppermute | solution.py:398
  194.5 17.8 %collective-permute-start.26 = (bf16[18,64,128]{2,1,0:T(8,128)(2,1)S(1)}, bf16[18,64,128]{2,1,0:T(8,128)(2,1)S(1)}, u32[]{:S(2)}, u32[]{:S(2)}) collective-permute-start(bf16[18,64,128]{2,1,0:T(8,128)(2,1)S(1)} %get-tuple-element.135), channel_id=1, source_target_pairs={{0,32},{32,64},{64,96},{96,128},{128,160},{160,192},{192,224},{224... | collective-permute-start | bytes 884744 | tf_op jit(solution)/shard_map/ppermute | solution.py:396
  199.7 15.3 %collective-permute-start.27 = (bf16[18,64,128]{2,1,0:T(8,128)(2,1)S(1)}, bf16[18,64,128]{2,1,0:T(8,128)(2,1)S(1)}, u32[]{:S(2)}, u32[]{:S(2)}) collective-permute-start(bf16[18,64,128]{2,1,0:T(8,128)(2,1)S(1)} %get-tuple-element.136), channel_id=1, source_target_pairs={{32,0},{64,32},{96,64},{128,96},{160,128},{192,160},{224,192},{0,2... | collective-permute-start | bytes 884744 | tf_op jit(solution)/shard_map/ppermute | solution.py:398
  200.9 11.5 %collective-permute-start.29 = (f32[8,128]{1,0:T(8,128)S(1)}, f32[8,128]{1,0:T(8,128)S(1)}, u32[]{:S(2)}, u32[]{:S(2)}) collective-permute-start(f32[8,128]{1,0:T(8,128)S(1)} %add.95), channel_id=1, source_target_pairs={{0,64},{32,96},{64,0},{96,32},{128,192},{160,224},{192,128},{224,1... | collective-permute-start | bytes 12296 | tf_op jit(solution)/shard_map/ppermute | solution.py:403
  206.0 9.1 %copy-start.6 = (bf16[18,64,128]{2,1,0:T(8,128)(2,1)}, bf16[18,64,128]{2,1,0:T(8,128)(2,1)S(1)}, u32[]{:S(2)}) copy-start(bf16[18,64,128]{2,1,0:T(8,128)(2,1)S(1)} %collective-permute-done.19.refs_1_) | copy-start | bytes 884740
  206.0 16.7 %collective-permute-start.5 = (bf16[18,64,128]{2,1,0:T(8,128)(2,1)S(1)}, bf16[18,64,128]{2,1,0:T(8,128)(2,1)S(1)}, u32[]{:S(2)}, u32[]{:S(2)}) collective-permute-start(bf16[18,64,128]{2,1,0:T(8,128)(2,1)S(1)} %get-tuple-element.90), channel_id=1, source_target_pairs={{0,32},{32,64},{64,96},{96,128},{128,160},{160,192},{192,224},{224... | collective-permute-start | bytes 884744 | tf_op jit(solution)/shard_map/ppermute | solution.py:396
  206.0 9.1 %copy-start.7 = (bf16[18,64,128]{2,1,0:T(8,128)(2,1)}, bf16[18,64,128]{2,1,0:T(8,128)(2,1)S(1)}, u32[]{:S(2)}) copy-start(bf16[18,64,128]{2,1,0:T(8,128)(2,1)S(1)} %collective-permute-done.20.refs_2_) | copy-start | bytes 884740
  206.0 16.7 %collective-permute-start.6 = (bf16[18,64,128]{2,1,0:T(8,128)(2,1)S(1)}, bf16[18,64,128]{2,1,0:T(8,128)(2,1)S(1)}, u32[]{:S(2)}, u32[]{:S(2)}) collective-permute-start(bf16[18,64,128]{2,1,0:T(8,128)(2,1)S(1)} %get-tuple-element.91), channel_id=1, source_target_pairs={{32,0},{64,32},{96,64},{128,96},{160,128},{192,160},{224,192},{0,2... | collective-permute-start | bytes 884744 | tf_op jit(solution)/shard_map/ppermute | solution.py:398
  212.3 2.8 %copy-start.8 = (bf16[18,64,128]{2,1,0:T(8,128)(2,1)}, bf16[18,64,128]{2,1,0:T(8,128)(2,1)S(1)}, u32[]{:S(2)}) copy-start(bf16[18,64,128]{2,1,0:T(8,128)(2,1)S(1)} %collective-permute-done.26.refs_4_) | copy-start | bytes 884740
  212.3 12.6 %collective-permute-start.12 = (bf16[18,64,128]{2,1,0:T(8,128)(2,1)S(1)}, bf16[18,64,128]{2,1,0:T(8,128)(2,1)S(1)}, u32[]{:S(2)}, u32[]{:S(2)}) collective-permute-start(bf16[18,64,128]{2,1,0:T(8,128)(2,1)S(1)} %get-tuple-element.105), channel_id=1, source_target_pairs={{0,32},{32,64},{64,96},{96,128},{128,160},{160,192},{192,224},{224... | collective-permute-start | bytes 884744 | tf_op jit(solution)/shard_map/ppermute | solution.py:396
  212.3 12.6 %collective-permute-start.13 = (bf16[18,64,128]{2,1,0:T(8,128)(2,1)S(1)}, bf16[18,64,128]{2,1,0:T(8,128)(2,1)S(1)}, u32[]{:S(2)}, u32[]{:S(2)}) collective-permute-start(bf16[18,64,128]{2,1,0:T(8,128)(2,1)S(1)} %get-tuple-element.106), channel_id=1, source_target_pairs={{32,0},{64,32},{96,64},{128,96},{160,128},{192,160},{224,192},{0,2... | collective-permute-start | bytes 884744 | tf_op jit(solution)/shard_map/ppermute | solution.py:398
  215.0 0.7 copy-start.9
  215.0 7.1 %collective-permute-start.30 = (f32[8,128]{1,0:T(8,128)S(1)}, f32[8,128]{1,0:T(8,128)S(1)}, u32[]{:S(2)}, u32[]{:S(2)}) collective-permute-start(f32[8,128]{1,0:T(8,128)S(1)} %add.96), channel_id=1, source_target_pairs={{0,32},{32,0},{64,96},{96,64},{128,160},{160,128},{192,224},{224,1... | collective-permute-start | bytes 12296 | tf_op jit(solution)/shard_map/ppermute | solution.py:403

commit v8 on v7

--- a/solution.py
+++ b/solution.py
@@ -54,7 +54,9 @@
     )(owner, design)
 
 
-def weigh(ids_ref, sigma_ref, dt_ref, observed_ref, type_ref, sol_ref, wt_ref, head_ref):
+def weigh(
+    owner_ref, sub_ref, sigma_ref, dt_ref, observed_ref, type_ref, all_ref, wt_ref, head_ref
+):
     blocks = observed_ref.shape[0]
     head_ref[...] = jnp.zeros_like(head_ref)
     spread = jnp.zeros(observed_ref.shape, F32)
@@ -66,7 +68,8 @@
     for b in range(blocks):
         parts = []
         for l in range(4):
-            s = jnp.broadcast_to(sol_ref[pl.ds(ids_ref[b * 4 + l], 1), :], (8, TW))
+            s = all_ref[owner_ref[b * 4 + l], pl.ds(sub_ref[b * 4 + l], 1), :]
+            s = jnp.broadcast_to(s, (8, TW))
             hi = s.astype(BF16).astype(F32)
             mid = (s - hi).astype(BF16).astype(F32)
             low = s - hi - mid
@@ -134,13 +137,13 @@
     out_specs = [pl.BlockSpec((group, rows, TW), lambda i, *_: (i, 0, 0))]
     out_shape = [jax.ShapeDtypeStruct((n_slot, rows, TW), BF16)]
     if chunk == 0:
-        dt, observed = args[2], args[3]
+        dt, observed = args[3], args[4]
         kept = [
             jax.ShapeDtypeStruct(dt.shape, BF16),
             jax.ShapeDtypeStruct((observed.shape[0], HEAD, TW), BF16),
         ]
         smem = pl.BlockSpec(memory_space=pltpu.SMEM)
-        in_specs = [smem, smem] + [whole(x) for x in args[2:]]
+        in_specs = [smem] * 3 + [whole(x) for x in args[3:]]
         out_specs = [whole(x) for x in kept] + out_specs
         out_shape = kept + out_shape
     else:
@@ -419,11 +422,11 @@
     small = jnp.pad(small, (0, 4 * TW - small.shape[0])).reshape(1, 4, TW)
     small = jnp.broadcast_to(small, (n_owner, 4, TW))
     everyone = lax.all_to_all(small, "tile", split_axis=0, concat_axis=0, tiled=True)
-    sol = everyone[:, :per_owner].reshape(tile_count, TW)
-
-    dt, slots = prepare(owner_of.reshape(-1), design, n_owner)
+
+    owner, sub = owner_of.reshape(-1), sub_of.reshape(-1)
+    dt, slots = prepare(owner, design, n_owner)
     wt, head, payload = pack(
-        0, slots, tile_ids, sigma_table, dt, observed, obs_type, sol
+        0, slots, owner, sub, sigma_table, dt, observed, obs_type, everyone
     )
 
     def send(p):

time: 229 us -> 230 us (level)
  transfers between devices with their start and end apart: 34 -> 34, of which waited for: 15 -> 15; matrix products, arithmetic and copies ran while one was open for 4% -> 5% of each run, Pallas kernels for 13% -> 13%
where the time goes in v8:
time: 230 us; the launch traced here: 229 us
  waiting for transfers between devices  107 us (47%)
  starting transfers between devices  66.8 us (29%)
  Pallas kernels  40.4 us (18%)
  other arithmetic  7.85 us (3%)
  local copies, waits for them, and re-layouts  6.1 us (3%)
    all_to_all x2, waiting for transfers between devices, send(): g = lax.all_to_all(p, 'tile', split_axis=0, concat_axis=0, tiled=True)  65 us
    ppermute x14, waiting for transfers between devices, ring(): up = lax.ppermute(up, 'arc', rising)  38.5 us
    ppermute x14, starting transfers between devices, ring(): down = lax.ppermute(down, 'arc', falling)  35.2 us
    pallas_call x2, Pallas kernels, gather(): pl.pallas_call(functools.partial(gather_kernel, chunk), grid_spec=pltpu.P...  17 us
    all_to_all x2, starting transfers between devices, send(): g = lax.all_to_all(p, 'tile', split_axis=0, concat_axis=0, tiled=True)  15.4 us
    pallas_call x2, Pallas kernels, pack(): pl.pallas_call(functools.partial(pack_kernel, chunk), grid_spec=pltpu.Pre...  10.5 us
    all_to_all x1, starting transfers between devices, on_device(): lax.all_to_all(small, 'tile', split_axis=0, concat_axis=0, tiled=True)  8.58 us
    pallas_call x2, Pallas kernels, final(): pl.pallas_call(final_kernel, grid=(part // step,), in_specs=in_specs, out...  7.6 us
  transfers between devices with their start and end apart: 34, of which 15 were waited for; matrix products, arithmetic and copies ran while one was open for 5% of the time, Pallas kernels for 13%

profile of v8, /device:TPU:1, one launch (start us, length us, event | category | flops | bytes accessed | tf_op | source)
XLA Modules:
  0.0 229.3 jit_solution(12748053390534369805)
XLA Ops:
  0.6 0.7 add_convert_fusion.20
  1.5 0.7 fusion
  2.2 0.6 broadcast_in_dim.8
  2.8 8.6 %all-to-all-start = ((f32[32,4,128]{2,1,0:T(4,128)}), f32[32,4,128]{2,1,0:T(4,128)S(1)}, u32[]{:S(2)}, u32[]{:S(2)}) async-start(f32[32,4,128]{2,1,0:T(4,128)} %broadcast_in_dim.8), calls=%async_computation | async-start | bytes 131072 | tf_op jit(solution)/shard_map/all_to_all | solution.py:424
  11.4 0.8 copy.14
  12.2 0.8 copy.15
  12.9 0.6 reshape.39.owner_ref.refs_0_
  13.5 0.6 reshape.40.refs_1_
  14.1 3.4 %prepare.1 = (bf16[32,128,128]{2,1,0:T(8,128)(2,1)}, s32[64]{0:T(128)}) custom-call(s32[32]{0:T(128)} %reshape.39.owner_ref.refs_0_, bf16[8,128,512]{2,1,0:T(8,128)(2,1)} %design_ref.1), custom_call_target="tpu_custom_call" | custom-call | tf_op jit(solution)/shard_map/prepare/pallas_call | solution.py:45
  17.5 1.3 all-to-all-done.refs_6_.all_ref
  18.8 0.6 copy-done.5
  19.4 6.1 %shard_map.95 = (bf16[32,128,128]{2,1,0:T(8,128)(2,1)}, bf16[8,16,128]{2,1,0:T(8,128)(2,1)}, bf16[64,320,128]{2,1,0:T(8,128)(2,1)}) custom-call(s32[64]{0:T(128)} %get-tuple-element.71.table_ref, s32[32]{0:T(128)} %reshape.39.owner_ref.refs_0_, s32[32]{0:T(128)} %reshape.40.refs_1_, f32[8]{0:T(128)} %refs_2_.1, ...), custom_call_target="tpu_custom_call" | custom-call | tf_op jit(solution)/shard_map/pallas_call | solution.py:151
  25.5 6.1 %all-to-all-start.1 = ((bf16[32,2,320,128]{3,2,1,0:T(8,128)(2,1)}), bf16[32,2,320,128]{3,2,1,0:T(8,128)(2,1)}, u32[]{:S(2)}, u32[]{:S(2)}) async-start(bf16[32,2,320,128]{3,2,1,0:T(8,128)(2,1)} %bitcast.17), calls=%async_computation.1 | async-start | bytes 10485760 | tf_op jit(solution)/shard_map/all_to_all | solution.py:434
  31.6 0.6 pad_add_fusion.where_ref
  32.2 1.9 route.1
  34.1 0.8 reshape.43.table_ref
  34.9 4.5 %shard_map.96 = bf16[64,208,128]{2,1,0:T(8,128)(2,1)} custom-call(s32[64]{0:T(128)} %get-tuple-element.71.table_ref, bf16[32,128,128]{2,1,0:T(8,128)(2,1)} %get-tuple-element.74.refs_0_, bf16[8,16,128]{2,1,0:T(8,128)(2,1)} %get-tuple-element.75.refs_1_), custom_call_target="tpu_custom_call" | custom-call | tf_op jit(solution)/shard_map/pallas_call | solution.py:151
  39.3 56.7 %all-to-all-done.1 = bf16[32,2,320,128]{3,2,1,0:T(8,128)(2,1)} async-done(((bf16[32,2,320,128]{3,2,1,0:T(8,128)(2,1)}), bf16[32,2,320,128]{3,2,1,0:T(8,128)(2,1)}, u32[]{:S(2)}, u32[]{:S(2)}) %all-to-all-start.1) | async-done | bytes 5242912 | tf_op jit(solution)/shard_map/all_to_all | solution.py:434
  96.0 9.2 %all-to-all-start.2 = ((bf16[32,2,208,128]{3,2,1,0:T(8,128)(2,1)}), bf16[32,2,208,128]{3,2,1,0:T(8,128)(2,1)S(1)}, u32[]{:S(2)}, u32[]{:S(2)}) async-start(bf16[32,2,208,128]{3,2,1,0:T(8,128)(2,1)} %bitcast.13), calls=%async_computation.2 | async-start | bytes 6815744 | tf_op jit(solution)/shard_map/all_to_all | solution.py:434
  105.2 8.4 %shard_map.98 = (bf16[144,64,128]{2,1,0:T(8,128)(2,1)S(1)}, bf16[144,64,128]{2,1,0:T(8,128)(2,1)S(1)}, bf16[18,64,128]{2,1,0:T(8,128)(2,1)S(1)}, bf16[18,64,128]...) custom-call(s32[512]{0:T(512)S(1)} %reshape.43.table_ref, ...), custom_call_target="tpu_custom_call" | custom-call | tf_op jit(solution)/shard_map/pallas_call | solution.py:309
  113.6 1.7 collective-permute-start.14
  115.4 4.0 %collective-permute-start.21 = (bf16[18,64,128]{2,1,0:T(8,128)(2,1)S(1)}, bf16[18,64,128]{2,1,0:T(8,128)(2,1)S(1)}, u32[]{:S(2)}, u32[]{:S(2)}) collective-permute-start(bf16[18,64,128]{2,1,0:T(8,128)(2,1)S(1)} %get-tuple-element.126), channel_id=1, source_target_pairs={{32,0},{64,32},{96,64},{128,96},{160,128},{192,160},{224,192},{0,2... | collective-permute-start | bytes 884744 | tf_op jit(solution)/shard_map/ppermute | solution.py:401
  119.4 7.1 %collective-permute-done.14 = bf16[18,64,128]{2,1,0:T(8,128)(2,1)S(1)} collective-permute-done((bf16[18,64,128]{2,1,0:T(8,128)(2,1)S(1)}, bf16[18,64,128]{2,1,0:T(8,128)(2,1)S(1)}, u32[]{:S(2)}, u32[]{:S(2)}) %collective-permute-start.14) | collective-permute-done | bytes 294944 | tf_op jit(solution)/shard_map/ppermute | solution.py:399
  126.6 2.7 %collective-permute-start.16 = (bf16[18,64,128]{2,1,0:T(8,128)(2,1)S(1)}, bf16[18,64,128]{2,1,0:T(8,128)(2,1)S(1)}, u32[]{:S(2)}, u32[]{:S(2)}) collective-permute-start(bf16[18,64,128]{2,1,0:T(8,128)(2,1)S(1)} %get-tuple-element.113), channel_id=1, source_target_pairs={{32,0},{64,32},{96,64},{128,96},{160,128},{192,160},{224,192},{0,2... | collective-permute-start | bytes 884744 | tf_op jit(solution)/shard_map/ppermute | solution.py:401
  129.3 0.8 add_convert_fusion.4
  130.1 2.7 %collective-permute-start.23 = (bf16[18,64,128]{2,1,0:T(8,128)(2,1)}, bf16[18,64,128]{2,1,0:T(8,128)(2,1)}, u32[]{:S(2)}, u32[]{:S(2)}) collective-permute-start(bf16[18,64,128]{2,1,0:T(8,128)(2,1)} %add_convert_fusion.4), channel_id=1, source_target_pairs={{32,0},{64,32},{96,64},{128,96},{160,128},{192,160},{224,192},{0,2... | collective-permute-start | bytes 884744 | tf_op jit(solution)/shard_map/ppermute | solution.py:401
  132.8 2.8 %collective-permute-done.15 = bf16[18,64,128]{2,1,0:T(8,128)(2,1)S(1)} collective-permute-done((bf16[18,64,128]{2,1,0:T(8,128)(2,1)S(1)}, bf16[18,64,128]{2,1,0:T(8,128)(2,1)S(1)}, u32[]{:S(2)}, u32[]{:S(2)}) %collective-permute-start.15) | collective-permute-done | bytes 294944 | tf_op jit(solution)/shard_map/ppermute | solution.py:399
  135.6 1.1 add_convert_fusion.7
  136.7 2.7 %collective-permute-start.18 = (bf16[18,64,128]{2,1,0:T(8,128)(2,1)}, bf16[18,64,128]{2,1,0:T(8,128)(2,1)}, u32[]{:S(2)}, u32[]{:S(2)}) collective-permute-start(bf16[18,64,128]{2,1,0:T(8,128)(2,1)} %get-tuple-element.117), channel_id=1, source_target_pairs={{32,0},{64,32},{96,64},{128,96},{160,128},{192,160},{224,192},{0,2... | collective-permute-start | bytes 884744 | tf_op jit(solution)/shard_map/ppermute | solution.py:401
  139.3 8.4 %all-to-all-done.2 = bf16[32,2,208,128]{3,2,1,0:T(8,128)(2,1)S(1)} async-done(((bf16[32,2,208,128]{3,2,1,0:T(8,128)(2,1)}), bf16[32,2,208,128]{3,2,1,0:T(8,128)(2,1)S(1)}, u32[]{:S(2)}, u32[]{:S(2)}) %all-to-all-start.2) | async-done | bytes 3407904 | tf_op jit(solution)/shard_map/all_to_all | solution.py:434
  147.7 8.6 %shard_map.97 = (bf16[144,64,128]{2,1,0:T(8,128)(2,1)S(1)}, bf16[144,64,128]{2,1,0:T(8,128)(2,1)S(1)}, bf16[18,64,128]{2,1,0:T(8,128)(2,1)S(1)}, bf16[18,64,128]...) custom-call(s32[512]{0:T(512)S(1)} %reshape.43.table_ref, ...), custom_call_target="tpu_custom_call" | custom-call | tf_op jit(solution)/shard_map/pallas_call | solution.py:309
  156.3 1.9 collective-permute-start
  158.2 4.0 %collective-permute-start.7 = (bf16[18,64,128]{2,1,0:T(8,128)(2,1)S(1)}, bf16[18,64,128]{2,1,0:T(8,128)(2,1)S(1)}, u32[]{:S(2)}, u32[]{:S(2)}) collective-permute-start(bf16[18,64,128]{2,1,0:T(8,128)(2,1)S(1)} %get-tuple-element.96), channel_id=1, source_target_pairs={{32,0},{64,32},{96,64},{128,96},{160,128},{192,160},{224,192},{0,2... | collective-permute-start | bytes 884744 | tf_op jit(solution)/shard_map/ppermute | solution.py:401
  162.3 1.3 add_convert_fusion.2
  163.6 2.7 %collective-permute-start.25 = (bf16[18,64,128]{2,1,0:T(8,128)(2,1)S(1)}, bf16[18,64,128]{2,1,0:T(8,128)(2,1)S(1)}, u32[]{:S(2)}, u32[]{:S(2)}) collective-permute-start(bf16[18,64,128]{2,1,0:T(8,128)(2,1)S(1)} %get-tuple-element.132), channel_id=1, source_target_pairs={{32,0},{64,32},{96,64},{128,96},{160,128},{192,160},{224,192},{0,2... | collective-permute-start | bytes 884744 | tf_op jit(solution)/shard_map/ppermute | solution.py:401
  166.3 2.3 %collective-permute-done = bf16[18,64,128]{2,1,0:T(8,128)(2,1)S(1)} collective-permute-done((bf16[18,64,128]{2,1,0:T(8,128)(2,1)S(1)}, bf16[18,64,128]{2,1,0:T(8,128)(2,1)S(1)}, u32[]{:S(2)}, u32[]{:S(2)}) %collective-permute-start) | collective-permute-done | bytes 294944 | tf_op jit(solution)/shard_map/ppermute | solution.py:399
  168.8 2.7 %collective-permute-start.2 = (bf16[18,64,128]{2,1,0:T(8,128)(2,1)S(1)}, bf16[18,64,128]{2,1,0:T(8,128)(2,1)S(1)}, u32[]{:S(2)}, u32[]{:S(2)}) collective-permute-start(bf16[18,64,128]{2,1,0:T(8,128)(2,1)S(1)} %get-tuple-element.83), channel_id=1, source_target_pairs={{32,0},{64,32},{96,64},{128,96},{160,128},{192,160},{224,192},{0,2... | collective-permute-start | bytes 884744 | tf_op jit(solution)/shard_map/ppermute | solution.py:401
  171.7 3.3 %collective-permute-done.24 = bf16[18,64,128]{2,1,0:T(8,128)(2,1)S(1)} collective-permute-done((bf16[18,64,128]{2,1,0:T(8,128)(2,1)S(1)}, bf16[18,64,128]{2,1,0:T(8,128)(2,1)S(1)}, u32[]{:S(2)}, u32[]{:S(2)}) %collective-permute-start.24) | collective-permute-done | bytes 294944 | tf_op jit(solution)/shard_map/ppermute | solution.py:399
  175.0 1.2 collective-permute-start.9
  176.2 1.4 add_convert_fusion.5
  177.6 2.6 %collective-permute-start.28 = (f32[8,128]{1,0:T(8,128)S(1)}, f32[8,128]{1,0:T(8,128)S(1)}, u32[]{:S(2)}, u32[]{:S(2)}) collective-permute-start(f32[8,128]{1,0:T(8,128)S(1)} %get-tuple-element.139), channel_id=1, source_target_pairs={{0,128},{32,160},{64,192},{96,224},{128,0},{160,32},{192,64},{224,... | collective-permute-start | bytes 12296 | tf_op jit(solution)/shard_map/ppermute | solution.py:406
  180.2 1.1 collective-permute-done.1
  181.3 0.2 add_convert_fusion.17
  181.5 0.5 collective-permute-start.3
  182.0 2.3 collective-permute-start.4
  184.3 3.3 %collective-permute-done.8 = bf16[18,64,128]{2,1,0:T(8,128)(2,1)S(1)} collective-permute-done((bf16[18,64,128]{2,1,0:T(8,128)(2,1)S(1)}, bf16[18,64,128]{2,1,0:T(8,128)(2,1)S(1)}, u32[]{:S(2)}, u32[]{:S(2)}) %collective-permute-start.8) | collective-permute-done | bytes 294944 | tf_op jit(solution)/shard_map/ppermute | solution.py:399
  187.6 0.2 add_convert_fusion.12
  187.9 2.7 %collective-permute-start.11 = (bf16[18,64,128]{2,1,0:T(8,128)(2,1)S(1)}, bf16[18,64,128]{2,1,0:T(8,128)(2,1)S(1)}, u32[]{:S(2)}, u32[]{:S(2)}) collective-permute-start(bf16[18,64,128]{2,1,0:T(8,128)(2,1)S(1)} %get-tuple-element.102), channel_id=1, source_target_pairs={{32,0},{64,32},{96,64},{128,96},{160,128},{192,160},{224,192},{0,2... | collective-permute-start | bytes 884744 | tf_op jit(solution)/shard_map/ppermute | solution.py:401
  190.9 3.2 %collective-permute-done.3 = bf16[18,64,128]{2,1,0:T(8,128)(2,1)S(1)} collective-permute-done((bf16[18,64,128]{2,1,0:T(8,128)(2,1)S(1)}, bf16[18,64,128]{2,1,0:T(8,128)(2,1)S(1)}, u32[]{:S(2)}, u32[]{:S(2)}) %collective-permute-start.3) | collective-permute-done | bytes 294944 | tf_op jit(solution)/shard_map/ppermute | solution.py:399
  194.1 1.2 collective-permute-start.20
  195.3 0.3 collective-permute-start.26
  195.8 4.6 %collective-permute-done.10 = bf16[18,64,128]{2,1,0:T(8,128)(2,1)S(1)} collective-permute-done((bf16[18,64,128]{2,1,0:T(8,128)(2,1)S(1)}, bf16[18,64,128]{2,1,0:T(8,128)(2,1)S(1)}, u32[]{:S(2)}, u32[]{:S(2)}) %collective-permute-start.10) | collective-permute-done | bytes 294944 | tf_op jit(solution)/shard_map/ppermute | solution.py:399
  200.4 1.2 collective-permute-start.27
  201.6 0.2 add_convert_fusion.10
  201.8 4.9 %collective-permute-done.19.refs_1_ = bf16[18,64,128]{2,1,0:T(8,128)(2,1)S(1)} collective-permute-done((bf16[18,64,128]{2,1,0:T(8,128)(2,1)S(1)}, bf16[18,64,128]{2,1,0:T(8,128)(2,1)S(1)}, u32[]{:S(2)}, u32[]{:S(2)}) %collective-permute-start.19) | collective-permute-done | bytes 294944 | tf_op jit(solution)/shard_map/ppermute | solution.py:399
  206.8 2.7 %collective-permute-start.6 = (bf16[18,64,128]{2,1,0:T(8,128)(2,1)S(1)}, bf16[18,64,128]{2,1,0:T(8,128)(2,1)S(1)}, u32[]{:S(2)}, u32[]{:S(2)}) collective-permute-start(bf16[18,64,128]{2,1,0:T(8,128)(2,1)S(1)} %get-tuple-element.91), channel_id=1, source_target_pairs={{32,0},{64,32},{96,64},{128,96},{160,128},{192,160},{224,192},{0,2... | collective-permute-start | bytes 884744 | tf_op jit(solution)/shard_map/ppermute | solution.py:401
  209.4 3.6 %collective-permute-done.26.refs_4_ = bf16[18,64,128]{2,1,0:T(8,128)(2,1)S(1)} collective-permute-done((bf16[18,64,128]{2,1,0:T(8,128)(2,1)S(1)}, bf16[18,64,128]{2,1,0:T(8,128)(2,1)S(1)}, u32[]{:S(2)}, u32[]{:S(2)}) %collective-permute-start.26) | collective-permute-done | bytes 294944 | tf_op jit(solution)/shard_map/ppermute | solution.py:399
  213.1 2.7 %collective-permute-start.13 = (bf16[18,64,128]{2,1,0:T(8,128)(2,1)S(1)}, bf16[18,64,128]{2,1,0:T(8,128)(2,1)S(1)}, u32[]{:S(2)}, u32[]{:S(2)}) collective-permute-start(bf16[18,64,128]{2,1,0:T(8,128)(2,1)S(1)} %get-tuple-element.106), channel_id=1, source_target_pairs={{32,0},{64,32},{96,64},{128,96},{160,128},{192,160},{224,192},{0,2... | collective-permute-start | bytes 884744 | tf_op jit(solution)/shard_map/ppermute | solution.py:401
  215.9 0.6 copy-done.9
  216.5 4.0 %shard_map.99.refs_6_ = f32[12,128,384]{2,1,0:T(8,128)} custom-call(f32[12,128,384]{2,1,0:T(8,128)} %bitcast.14, bf16[144,64,128]{2,1,0:T(8,128)(2,1)} %copy-done.2, bf16[18,64,128]{2,1,0:T(8,128)(2,1)} %copy-done.6, bf16[18,64,128]{2,1,0:T(8,128)(2,1)} %copy-done.7, bf16[144,64,128]{2,1,0:T(8,128)(2,1)} %copy-done.3, bf16[18,64,128]{2,1,0:T(8,128)(2,1)} %copy-done.8, ...), custom_call_target="tpu_custom_call" | custom-call | tf_op jit(solution)/shard_map/pallas_call | solution.py:368
  220.5 2.4 %collective-permute-done.30 = f32[8,128]{1,0:T(8,128)S(1)} collective-permute-done((f32[8,128]{1,0:T(8,128)S(1)}, f32[8,128]{1,0:T(8,128)S(1)}, u32[]{:S(2)}, u32[]{:S(2)}) %collective-permute-start.30) | collective-permute-done | bytes 4128 | tf_op jit(solution)/shard_map/ppermute | solution.py:406
  222.9 0.6 slice_bitcast_fusion
  223.4 2.3 collective-permute-done.12.refs_4_
  225.7 3.6 %shard_map.100 = f32[12,128,384]{2,1,0:T(8,128)} custom-call(f32[12,128,384]{2,1,0:T(8,128)} %bitcast.15, bf16[144,64,128]{2,1,0:T(8,128)(2,1)} %copy-done, bf16[18,64,128]{2,1,0:T(8,128)(2,1)S(1)} %collective-permute-done.5.refs_1_, bf16[18,64,128]{2,1,0:T(8,128)(2,1)S(1)} %collective-permute-done.6.refs_2_, ...), custom_call_target="tpu_custom_call", output_to_operand_aliasing={{}: (7, {})} | custom-call | tf_op jit(solution)/shard_map/pallas_call | solution.py:368
  (59 shorter events, 1.5 us)
Async XLA Ops:
  2.8 15.9 %all-to-all-start = ((f32[32,4,128]{2,1,0:T(4,128)}), f32[32,4,128]{2,1,0:T(4,128)S(1)}, u32[]{:S(2)}, u32[]{:S(2)}) async-start(f32[32,4,128]{2,1,0:T(4,128)} %broadcast_in_dim.8), calls=%async_computation | async-start | bytes 131072 | tf_op jit(solution)/shard_map/all_to_all | solution.py:424
  18.8 0.6 copy-start.5
  25.5 70.5 %all-to-all-start.1 = ((bf16[32,2,320,128]{3,2,1,0:T(8,128)(2,1)}), bf16[32,2,320,128]{3,2,1,0:T(8,128)(2,1)}, u32[]{:S(2)}, u32[]{:S(2)}) async-start(bf16[32,2,320,128]{3,2,1,0:T(8,128)(2,1)} %bitcast.17), calls=%async_computation.1 | async-start | bytes 10485760 | tf_op jit(solution)/shard_map/all_to_all | solution.py:434
  96.0 51.7 %all-to-all-start.2 = ((bf16[32,2,208,128]{3,2,1,0:T(8,128)(2,1)}), bf16[32,2,208,128]{3,2,1,0:T(8,128)(2,1)S(1)}, u32[]{:S(2)}, u32[]{:S(2)}) async-start(bf16[32,2,208,128]{3,2,1,0:T(8,128)(2,1)} %bitcast.13), calls=%async_computation.2 | async-start | bytes 6815744 | tf_op jit(solution)/shard_map/all_to_all | solution.py:434
  113.6 23.0 %copy-start.2 = (bf16[144,64,128]{2,1,0:T(8,128)(2,1)}, bf16[144,64,128]{2,1,0:T(8,128)(2,1)S(1)}, u32[]{:S(2)}) copy-start(bf16[144,64,128]{2,1,0:T(8,128)(2,1)S(1)} %get-tuple-element.109.refs_0_) | copy-start | bytes 7077892
  113.6 23.0 %copy-start.3 = (bf16[144,64,128]{2,1,0:T(8,128)(2,1)}, bf16[144,64,128]{2,1,0:T(8,128)(2,1)S(1)}, u32[]{:S(2)}) copy-start(bf16[144,64,128]{2,1,0:T(8,128)(2,1)S(1)} %get-tuple-element.124.refs_3_) | copy-start | bytes 7077892
  113.6 12.8 %collective-permute-start.14 = (bf16[18,64,128]{2,1,0:T(8,128)(2,1)S(1)}, bf16[18,64,128]{2,1,0:T(8,128)(2,1)S(1)}, u32[]{:S(2)}, u32[]{:S(2)}) collective-permute-start(bf16[18,64,128]{2,1,0:T(8,128)(2,1)S(1)} %get-tuple-element.110), channel_id=1, source_target_pairs={{0,32},{32,64},{64,96},{96,128},{128,160},{160,192},{192,224},{224... | collective-permute-start | bytes 884744 | tf_op jit(solution)/shard_map/ppermute | solution.py:399
  115.4 13.9 %collective-permute-start.21 = (bf16[18,64,128]{2,1,0:T(8,128)(2,1)S(1)}, bf16[18,64,128]{2,1,0:T(8,128)(2,1)S(1)}, u32[]{:S(2)}, u32[]{:S(2)}) collective-permute-start(bf16[18,64,128]{2,1,0:T(8,128)(2,1)S(1)} %get-tuple-element.126), channel_id=1, source_target_pairs={{32,0},{64,32},{96,64},{128,96},{160,128},{192,160},{224,192},{0,2... | collective-permute-start | bytes 884744 | tf_op jit(solution)/shard_map/ppermute | solution.py:401
  126.5 9.0 %collective-permute-start.15 = (bf16[18,64,128]{2,1,0:T(8,128)(2,1)S(1)}, bf16[18,64,128]{2,1,0:T(8,128)(2,1)S(1)}, u32[]{:S(2)}, u32[]{:S(2)}) collective-permute-start(bf16[18,64,128]{2,1,0:T(8,128)(2,1)S(1)} %add_convert_fusion.9), channel_id=1, source_target_pairs={{0,32},{32,64},{64,96},{96,128},{128,160},{160,192},{192,224},{224... | collective-permute-start | bytes 884744 | tf_op jit(solution)/shard_map/ppermute | solution.py:399
  126.6 9.0 %collective-permute-start.16 = (bf16[18,64,128]{2,1,0:T(8,128)(2,1)S(1)}, bf16[18,64,128]{2,1,0:T(8,128)(2,1)S(1)}, u32[]{:S(2)}, u32[]{:S(2)}) collective-permute-start(bf16[18,64,128]{2,1,0:T(8,128)(2,1)S(1)} %get-tuple-element.113), channel_id=1, source_target_pairs={{32,0},{64,32},{96,64},{128,96},{160,128},{192,160},{224,192},{0,2... | collective-permute-start | bytes 884744 | tf_op jit(solution)/shard_map/ppermute | solution.py:401
  130.1 28.1 %collective-permute-start.22 = (bf16[18,64,128]{2,1,0:T(8,128)(2,1)}, bf16[18,64,128]{2,1,0:T(8,128)(2,1)}, u32[]{:S(2)}, u32[]{:S(2)}) collective-permute-start(bf16[18,64,128]{2,1,0:T(8,128)(2,1)} %get-tuple-element.127), channel_id=1, source_target_pairs={{0,32},{32,64},{64,96},{96,128},{128,160},{160,192},{192,224},{224... | collective-permute-start | bytes 884744 | tf_op jit(solution)/shard_map/ppermute | solution.py:399
  130.1 28.1 %collective-permute-start.23 = (bf16[18,64,128]{2,1,0:T(8,128)(2,1)}, bf16[18,64,128]{2,1,0:T(8,128)(2,1)}, u32[]{:S(2)}, u32[]{:S(2)}) collective-permute-start(bf16[18,64,128]{2,1,0:T(8,128)(2,1)} %add_convert_fusion.4), channel_id=1, source_target_pairs={{32,0},{64,32},{96,64},{128,96},{160,128},{192,160},{224,192},{0,2... | collective-permute-start | bytes 884744 | tf_op jit(solution)/shard_map/ppermute | solution.py:401
  136.7 27.0 %collective-permute-start.17 = (bf16[18,64,128]{2,1,0:T(8,128)(2,1)}, bf16[18,64,128]{2,1,0:T(8,128)(2,1)}, u32[]{:S(2)}, u32[]{:S(2)}) collective-permute-start(bf16[18,64,128]{2,1,0:T(8,128)(2,1)} %get-tuple-element.116), channel_id=1, source_target_pairs={{0,32},{32,64},{64,96},{96,128},{128,160},{160,192},{192,224},{224... | collective-permute-start | bytes 884744 | tf_op jit(solution)/shard_map/ppermute | solution.py:399
  136.7 29.6 %collective-permute-start.18 = (bf16[18,64,128]{2,1,0:T(8,128)(2,1)}, bf16[18,64,128]{2,1,0:T(8,128)(2,1)}, u32[]{:S(2)}, u32[]{:S(2)}) collective-permute-start(bf16[18,64,128]{2,1,0:T(8,128)(2,1)} %get-tuple-element.117), channel_id=1, source_target_pairs={{32,0},{64,32},{96,64},{128,96},{160,128},{192,160},{224,192},{0,2... | collective-permute-start | bytes 884744 | tf_op jit(solution)/shard_map/ppermute | solution.py:401
  147.7 14.6 %copy-start.4 = (bf16[144,64,128]{2,1,0:T(8,128)(2,1)S(1)}, bf16[144,64,128]{2,1,0:T(8,128)(2,1)}, u32[]{:S(2)}) copy-start(bf16[144,64,128]{2,1,0:T(8,128)(2,1)} %copy-done.3) | copy-start | bytes 7077892
  156.3 39.3 %copy-start = (bf16[144,64,128]{2,1,0:T(8,128)(2,1)}, bf16[144,64,128]{2,1,0:T(8,128)(2,1)S(1)}, u32[]{:S(2)}) copy-start(bf16[144,64,128]{2,1,0:T(8,128)(2,1)S(1)} %get-tuple-element.79.refs_0_) | copy-start | bytes 7077892
  156.3 45.3 %copy-start.1 = (bf16[144,64,128]{2,1,0:T(8,128)(2,1)}, bf16[144,64,128]{2,1,0:T(8,128)(2,1)S(1)}, u32[]{:S(2)}) copy-start(bf16[144,64,128]{2,1,0:T(8,128)(2,1)S(1)} %get-tuple-element.94.refs_3_) | copy-start | bytes 7077892
  156.3 12.3 %collective-permute-start = (bf16[18,64,128]{2,1,0:T(8,128)(2,1)S(1)}, bf16[18,64,128]{2,1,0:T(8,128)(2,1)S(1)}, u32[]{:S(2)}, u32[]{:S(2)}) collective-permute-start(bf16[18,64,128]{2,1,0:T(8,128)(2,1)S(1)} %get-tuple-element.80), channel_id=1, source_target_pairs={{0,32},{32,64},{64,96},{96,128},{128,160},{160,192},{192,224},{224... | collective-permute-start | bytes 884744 | tf_op jit(solution)/shard_map/ppermute | solution.py:399
  158.2 13.3 %collective-permute-start.7 = (bf16[18,64,128]{2,1,0:T(8,128)(2,1)S(1)}, bf16[18,64,128]{2,1,0:T(8,128)(2,1)S(1)}, u32[]{:S(2)}, u32[]{:S(2)}) collective-permute-start(bf16[18,64,128]{2,1,0:T(8,128)(2,1)S(1)} %get-tuple-element.96), channel_id=1, source_target_pairs={{32,0},{64,32},{96,64},{128,96},{160,128},{192,160},{224,192},{0,2... | collective-permute-start | bytes 884744 | tf_op jit(solution)/shard_map/ppermute | solution.py:401
  163.5 11.4 %collective-permute-start.24 = (bf16[18,64,128]{2,1,0:T(8,128)(2,1)S(1)}, bf16[18,64,128]{2,1,0:T(8,128)(2,1)S(1)}, u32[]{:S(2)}, u32[]{:S(2)}) collective-permute-start(bf16[18,64,128]{2,1,0:T(8,128)(2,1)S(1)} %get-tuple-element.131), channel_id=1, source_target_pairs={{0,32},{32,64},{64,96},{96,128},{128,160},{160,192},{192,224},{224... | collective-permute-start | bytes 884744 | tf_op jit(solution)/shard_map/ppermute | solution.py:399
  163.6 13.9 %collective-permute-start.25 = (bf16[18,64,128]{2,1,0:T(8,128)(2,1)S(1)}, bf16[18,64,128]{2,1,0:T(8,128)(2,1)S(1)}, u32[]{:S(2)}, u32[]{:S(2)}) collective-permute-start(bf16[18,64,128]{2,1,0:T(8,128)(2,1)S(1)} %get-tuple-element.132), channel_id=1, source_target_pairs={{32,0},{64,32},{96,64},{128,96},{160,128},{192,160},{224,192},{0,2... | collective-permute-start | bytes 884744 | tf_op jit(solution)/shard_map/ppermute | solution.py:401
  168.7 12.5 %collective-permute-start.1 = (bf16[18,64,128]{2,1,0:T(8,128)(2,1)S(1)}, bf16[18,64,128]{2,1,0:T(8,128)(2,1)S(1)}, u32[]{:S(2)}, u32[]{:S(2)}) collective-permute-start(bf16[18,64,128]{2,1,0:T(8,128)(2,1)S(1)} %add_convert_fusion.19), channel_id=1, source_target_pairs={{0,32},{32,64},{64,96},{96,128},{128,160},{160,192},{192,224},{224... | collective-permute-start | bytes 884744 | tf_op jit(solution)/shard_map/ppermute | solution.py:399
  168.8 12.5 %collective-permute-start.2 = (bf16[18,64,128]{2,1,0:T(8,128)(2,1)S(1)}, bf16[18,64,128]{2,1,0:T(8,128)(2,1)S(1)}, u32[]{:S(2)}, u32[]{:S(2)}) collective-permute-start(bf16[18,64,128]{2,1,0:T(8,128)(2,1)S(1)} %get-tuple-element.83), channel_id=1, source_target_pairs={{32,0},{64,32},{96,64},{128,96},{160,128},{192,160},{224,192},{0,2... | collective-permute-start | bytes 884744 | tf_op jit(solution)/shard_map/ppermute | solution.py:401
  171.6 16.0 %collective-permute-start.8 = (bf16[18,64,128]{2,1,0:T(8,128)(2,1)S(1)}, bf16[18,64,128]{2,1,0:T(8,128)(2,1)S(1)}, u32[]{:S(2)}, u32[]{:S(2)}) collective-permute-start(bf16[18,64,128]{2,1,0:T(8,128)(2,1)S(1)} %get-tuple-element.97), channel_id=1, source_target_pairs={{0,32},{32,64},{64,96},{96,128},{128,160},{160,192},{192,224},{224... | collective-permute-start | bytes 884744 | tf_op jit(solution)/shard_map/ppermute | solution.py:399
  175.0 12.6 %collective-permute-start.9 = (bf16[18,64,128]{2,1,0:T(8,128)(2,1)S(1)}, bf16[18,64,128]{2,1,0:T(8,128)(2,1)S(1)}, u32[]{:S(2)}, u32[]{:S(2)}) collective-permute-start(bf16[18,64,128]{2,1,0:T(8,128)(2,1)S(1)} %add_convert_fusion.14), channel_id=1, source_target_pairs={{32,0},{64,32},{96,64},{128,96},{160,128},{192,160},{224,192},{0,2... | collective-permute-start | bytes 884744 | tf_op jit(solution)/shard_map/ppermute | solution.py:401
  177.6 13.2 %collective-permute-start.28 = (f32[8,128]{1,0:T(8,128)S(1)}, f32[8,128]{1,0:T(8,128)S(1)}, u32[]{:S(2)}, u32[]{:S(2)}) collective-permute-start(f32[8,128]{1,0:T(8,128)S(1)} %get-tuple-element.139), channel_id=1, source_target_pairs={{0,128},{32,160},{64,192},{96,224},{128,0},{160,32},{192,64},{224,... | collective-permute-start | bytes 12296 | tf_op jit(solution)/shard_map/ppermute | solution.py:406
  181.5 12.6 %collective-permute-start.3 = (bf16[18,64,128]{2,1,0:T(8,128)(2,1)S(1)}, bf16[18,64,128]{2,1,0:T(8,128)(2,1)S(1)}, u32[]{:S(2)}, u32[]{:S(2)}) collective-permute-start(bf16[18,64,128]{2,1,0:T(8,128)(2,1)S(1)} %get-tuple-element.86), channel_id=1, source_target_pairs={{0,32},{32,64},{64,96},{96,128},{128,160},{160,192},{192,224},{224... | collective-permute-start | bytes 884744 | tf_op jit(solution)/shard_map/ppermute | solution.py:399
  182.0 13.3 %collective-permute-start.4 = (bf16[18,64,128]{2,1,0:T(8,128)(2,1)S(1)}, bf16[18,64,128]{2,1,0:T(8,128)(2,1)S(1)}, u32[]{:S(2)}, u32[]{:S(2)}) collective-permute-start(bf16[18,64,128]{2,1,0:T(8,128)(2,1)S(1)} %get-tuple-element.87), channel_id=1, source_target_pairs={{32,0},{64,32},{96,64},{128,96},{160,128},{192,160},{224,192},{0,2... | collective-permute-start | bytes 884744 | tf_op jit(solution)/shard_map/ppermute | solution.py:401
  187.8 12.6 %collective-permute-start.10 = (bf16[18,64,128]{2,1,0:T(8,128)(2,1)S(1)}, bf16[18,64,128]{2,1,0:T(8,128)(2,1)S(1)}, u32[]{:S(2)}, u32[]{:S(2)}) collective-permute-start(bf16[18,64,128]{2,1,0:T(8,128)(2,1)S(1)} %get-tuple-element.101), channel_id=1, source_target_pairs={{0,32},{32,64},{64,96},{96,128},{128,160},{160,192},{192,224},{224... | collective-permute-start | bytes 884744 | tf_op jit(solution)/shard_map/ppermute | solution.py:399
  187.9 13.7 %collective-permute-start.11 = (bf16[18,64,128]{2,1,0:T(8,128)(2,1)S(1)}, bf16[18,64,128]{2,1,0:T(8,128)(2,1)S(1)}, u32[]{:S(2)}, u32[]{:S(2)}) collective-permute-start(bf16[18,64,128]{2,1,0:T(8,128)(2,1)S(1)} %get-tuple-element.102), channel_id=1, source_target_pairs={{32,0},{64,32},{96,64},{128,96},{160,128},{192,160},{224,192},{0,2... | collective-permute-start | bytes 884744 | tf_op jit(solution)/shard_map/ppermute | solution.py:401
  190.8 15.9 %collective-permute-start.19 = (bf16[18,64,128]{2,1,0:T(8,128)(2,1)S(1)}, bf16[18,64,128]{2,1,0:T(8,128)(2,1)S(1)}, u32[]{:S(2)}, u32[]{:S(2)}) collective-permute-start(bf16[18,64,128]{2,1,0:T(8,128)(2,1)S(1)} %get-tuple-element.120), channel_id=1, source_target_pairs={{0,32},{32,64},{64,96},{96,128},{128,160},{160,192},{192,224},{224... | collective-permute-start | bytes 884744 | tf_op jit(solution)/shard_map/ppermute | solution.py:399
  194.1 12.6 %collective-permute-start.20 = (bf16[18,64,128]{2,1,0:T(8,128)(2,1)S(1)}, bf16[18,64,128]{2,1,0:T(8,128)(2,1)S(1)}, u32[]{:S(2)}, u32[]{:S(2)}) collective-permute-start(bf16[18,64,128]{2,1,0:T(8,128)(2,1)S(1)} %get-tuple-element.121), channel_id=1, source_target_pairs={{32,0},{64,32},{96,64},{128,96},{160,128},{192,160},{224,192},{0,2... | collective-permute-start | bytes 884744 | tf_op jit(solution)/shard_map/ppermute | solution.py:401
  195.3 17.8 %collective-permute-start.26 = (bf16[18,64,128]{2,1,0:T(8,128)(2,1)S(1)}, bf16[18,64,128]{2,1,0:T(8,128)(2,1)S(1)}, u32[]{:S(2)}, u32[]{:S(2)}) collective-permute-start(bf16[18,64,128]{2,1,0:T(8,128)(2,1)S(1)} %get-tuple-element.135), channel_id=1, source_target_pairs={{0,32},{32,64},{64,96},{96,128},{128,160},{160,192},{192,224},{224... | collective-permute-start | bytes 884744 | tf_op jit(solution)/shard_map/ppermute | solution.py:399
  200.4 15.3 %collective-permute-start.27 = (bf16[18,64,128]{2,1,0:T(8,128)(2,1)S(1)}, bf16[18,64,128]{2,1,0:T(8,128)(2,1)S(1)}, u32[]{:S(2)}, u32[]{:S(2)}) collective-permute-start(bf16[18,64,128]{2,1,0:T(8,128)(2,1)S(1)} %get-tuple-element.136), channel_id=1, source_target_pairs={{32,0},{64,32},{96,64},{128,96},{160,128},{192,160},{224,192},{0,2... | collective-permute-start | bytes 884744 | tf_op jit(solution)/shard_map/ppermute | solution.py:401
  201.6 11.5 %collective-permute-start.29 = (f32[8,128]{1,0:T(8,128)S(1)}, f32[8,128]{1,0:T(8,128)S(1)}, u32[]{:S(2)}, u32[]{:S(2)}) collective-permute-start(f32[8,128]{1,0:T(8,128)S(1)} %add.95), channel_id=1, source_target_pairs={{0,64},{32,96},{64,0},{96,32},{128,192},{160,224},{192,128},{224,1... | collective-permute-start | bytes 12296 | tf_op jit(solution)/shard_map/ppermute | solution.py:406
  206.7 9.1 %copy-start.6 = (bf16[18,64,128]{2,1,0:T(8,128)(2,1)}, bf16[18,64,128]{2,1,0:T(8,128)(2,1)S(1)}, u32[]{:S(2)}) copy-start(bf16[18,64,128]{2,1,0:T(8,128)(2,1)S(1)} %collective-permute-done.19.refs_1_) | copy-start | bytes 884740
  206.7 16.7 %collective-permute-start.5 = (bf16[18,64,128]{2,1,0:T(8,128)(2,1)S(1)}, bf16[18,64,128]{2,1,0:T(8,128)(2,1)S(1)}, u32[]{:S(2)}, u32[]{:S(2)}) collective-permute-start(bf16[18,64,128]{2,1,0:T(8,128)(2,1)S(1)} %get-tuple-element.90), channel_id=1, source_target_pairs={{0,32},{32,64},{64,96},{96,128},{128,160},{160,192},{192,224},{224... | collective-permute-start | bytes 884744 | tf_op jit(solution)/shard_map/ppermute | solution.py:399
  206.8 9.1 %copy-start.7 = (bf16[18,64,128]{2,1,0:T(8,128)(2,1)}, bf16[18,64,128]{2,1,0:T(8,128)(2,1)S(1)}, u32[]{:S(2)}) copy-start(bf16[18,64,128]{2,1,0:T(8,128)(2,1)S(1)} %collective-permute-done.20.refs_2_) | copy-start | bytes 884740
  206.8 16.7 %collective-permute-start.6 = (bf16[18,64,128]{2,1,0:T(8,128)(2,1)S(1)}, bf16[18,64,128]{2,1,0:T(8,128)(2,1)S(1)}, u32[]{:S(2)}, u32[]{:S(2)}) collective-permute-start(bf16[18,64,128]{2,1,0:T(8,128)(2,1)S(1)} %get-tuple-element.91), channel_id=1, source_target_pairs={{32,0},{64,32},{96,64},{128,96},{160,128},{192,160},{224,192},{0,2... | collective-permute-start | bytes 884744 | tf_op jit(solution)/shard_map/ppermute | solution.py:401
  213.1 2.8 %copy-start.8 = (bf16[18,64,128]{2,1,0:T(8,128)(2,1)}, bf16[18,64,128]{2,1,0:T(8,128)(2,1)S(1)}, u32[]{:S(2)}) copy-start(bf16[18,64,128]{2,1,0:T(8,128)(2,1)S(1)} %collective-permute-done.26.refs_4_) | copy-start | bytes 884740
  213.1 12.6 %collective-permute-start.12 = (bf16[18,64,128]{2,1,0:T(8,128)(2,1)S(1)}, bf16[18,64,128]{2,1,0:T(8,128)(2,1)S(1)}, u32[]{:S(2)}, u32[]{:S(2)}) collective-permute-start(bf16[18,64,128]{2,1,0:T(8,128)(2,1)S(1)} %get-tuple-element.105), channel_id=1, source_target_pairs={{0,32},{32,64},{64,96},{96,128},{128,160},{160,192},{192,224},{224... | collective-permute-start | bytes 884744 | tf_op jit(solution)/shard_map/ppermute | solution.py:399
  213.1 12.6 %collective-permute-start.13 = (bf16[18,64,128]{2,1,0:T(8,128)(2,1)S(1)}, bf16[18,64,128]{2,1,0:T(8,128)(2,1)S(1)}, u32[]{:S(2)}, u32[]{:S(2)}) collective-permute-start(bf16[18,64,128]{2,1,0:T(8,128)(2,1)S(1)} %get-tuple-element.106), channel_id=1, source_target_pairs={{32,0},{64,32},{96,64},{128,96},{160,128},{192,160},{224,192},{0,2... | collective-permute-start | bytes 884744 | tf_op jit(solution)/shard_map/ppermute | solution.py:401
  215.8 0.7 copy-start.9
  215.8 7.1 %collective-permute-start.30 = (f32[8,128]{1,0:T(8,128)S(1)}, f32[8,128]{1,0:T(8,128)S(1)}, u32[]{:S(2)}, u32[]{:S(2)}) collective-permute-start(f32[8,128]{1,0:T(8,128)S(1)} %add.96), channel_id=1, source_target_pairs={{0,32},{32,0},{64,96},{96,64},{128,160},{160,128},{192,224},{224,1... | collective-permute-start | bytes 12296 | tf_op jit(solution)/shard_map/ppermute | solution.py:406
